TPU v7x, 32 devices: a whole 2x2x4 slice. The times are simulated.
32 devices in a mesh: seq: 8 (over z, x), row: 4 (over y, core).
Axes of the slice: x: 2, y: 2, z: 4, core: 2. Of those that a mesh axis runs over, the one named last changes fastest.
Arguments:
- tokens: bfloat16 [4, 2048, 1024], P('row', 'seq'), may hold values from -6 to 6
- cotangent: bfloat16 [4, 2048, 1024], P('row', 'seq'), may hold values from -6 to 6
- segment_ids: int32 [4, 2048], P('row'), may hold values from 0 to 15, never falling along the last dimension, each value on 1 to 1536 neighbouring positions
- routes: int32 [4, 2048, 8], P('row', 'seq'), may hold values from 0 to 15, all different within a row; in each aligned block of 256 rows (0 to 255, 256 to 511, ..., all dimensions but the last counted through in order) at most 192 rows name the same one
- norm_attn: float32 [1024], P(('seq', 'row')), may hold values from 0.1 to 1.9
- w_query: float32 [1024, 1024], P(('seq', 'row')), may hold values from -0.75 to 0.75
- key_weight_matrix: float32 [1024, 512], P(('seq', 'row')), may hold values from -0.75 to 0.75
- value_weight_matrix: float32 [1024, 512], P(('seq', 'row')), may hold values from -0.1875 to 0.1875
- w_output: float32 [1024, 1024], P(('seq', 'row')), may hold values from -1.5 to 1.5
- norm_moe: float32 [1024], P(('seq', 'row')), may hold values from 0.1 to 1.9
- w_router: float32 [1024, 16], P(('seq', 'row')), may hold values from -0.09375 to 0.09375
- expert_in: float32 [16384, 1024], P(('seq', 'row')), may hold values from -0.1875 to 0.1875
- expert_out: float32 [16384, 512], P(('seq', 'row')), may hold values from -4 to 4
Outputs:
- layer_out: bfloat16 [4, 2048, 1024], P('row', 'seq')
- grad_tokens: float32 [4, 2048, 1024], P('row', 'seq')
- grad_norm_attn: float32 [1024], P(('seq', 'row'))
- grad_w_query: float32 [1024, 1024], P(('seq', 'row'))
- grad_w_key: float32 [1024, 512], P(('seq', 'row'))
- grad_w_value: float32 [1024, 512], P(('seq', 'row'))
- grad_w_output: float32 [1024, 1024], P(('seq', 'row'))
- grad_norm_moe: float32 [1024], P(('seq', 'row'))
- grad_w_router: float32 [1024, 16], P(('seq', 'row'))
- grad_expert_in: float32 [16384, 1024], P(('seq', 'row'))
- grad_expert_out: float32 [16384, 512], P(('seq', 'row'))
Inputs may be any that keep to these rules, and one draw needn't show every extreme that they name: `segment_ids`: along each row the ids never fall; each document (run of equal ids) holds 1 to 1536 tokens, and some document holds exactly 1536. `routes`: each token names 8 different experts; within the 256 tokens of one device (aligned blocks along a row) no expert is named more than 192 times, and in some blocks an expert is named exactly 192 times.
All inputs are finite; a program needn't handle non-finite values.
Results may differ from a plain program's by a relative error of at most 0.019.
The roundings to bfloat16 on the way count: a program that leaves them out, or rounds other values in their place, can miss the bound.
Values may be sent and summed in bfloat16 or wider, within the bound.
No kernel may reach another device: no remote copies, remote signals or barrier semaphores. Data moves between devices by JAX's collectives and lax.ppermute only.
A program may use at most 320 MiB of HBM per device.

v0:
```python
import math

import jax
import jax.numpy as jnp
from jax import lax
from jax.sharding import PartitionSpec as P

QUERY_HEADS = 16
KEY_VALUE_HEADS = 8
HEAD_SIZE = 64
F = 512
E = 16
TOPK = 8
CAP = 192


NORM_EPS = 1e-06
RESIDUAL_SCALE = 0.22
SCALE_OF_SCORES = 0.015625
ROPE_BASE = 10000.0
NEGATIVE_HUGE = -1e30
HIGHEST_DOT = lax.Precision.HIGHEST


def doc_positions(seg_row):
    count_all = seg_row.shape[0]
    index_all = jnp.arange(count_all, dtype=jnp.int32)
    changed = jnp.concatenate([jnp.ones((1,), jnp.bool_), seg_row[1:] != seg_row[:-1]])
    starts = jnp.where(changed, index_all, jnp.zeros_like(index_all))
    return index_all - lax.cummax(starts, axis=0)


def rope_tables(positions, head_size):
    half_size = head_size // 2
    freq_scale = jnp.power(ROPE_BASE, -2.0 * jnp.arange(half_size, dtype=jnp.float32) / head_size)
    angle_table = positions.astype(jnp.float32)[:, None] * freq_scale[None, :]
    return (jnp.cos(angle_table), jnp.sin(angle_table))


def apply_rotation_heads(values, cosine_table, sine_table, head_count):
    token_count = values.shape[0]
    shaped = values.reshape(token_count, head_count, -1)
    half_size = shaped.shape[-1] // 2
    first_half = shaped[..., :half_size]
    second_half = shaped[..., half_size:]
    cos_b = cosine_table[:, None, :]
    sin_b = sine_table[:, None, :]
    turned = jnp.concatenate(
        [first_half * cos_b - second_half * sin_b, second_half * cos_b + first_half * sin_b],
        axis=-1,
    )
    return turned.reshape(token_count, -1)


def reverse_rotation_heads(grads_in, cosine_table, sine_table, head_count):
    token_count = grads_in.shape[0]
    shaped = grads_in.reshape(token_count, head_count, -1)
    half_size = shaped.shape[-1] // 2
    first_half = shaped[..., :half_size]
    second_half = shaped[..., half_size:]
    cos_b = cosine_table[:, None, :]
    sin_b = sine_table[:, None, :]
    turned = jnp.concatenate(
        [first_half * cos_b + second_half * sin_b, second_half * cos_b - first_half * sin_b],
        axis=-1,
    )
    return turned.reshape(token_count, -1)


def rms_scale(values, gain):
    mean_square = jnp.mean(values * values, axis=-1, keepdims=True)
    return values * lax.rsqrt(mean_square + NORM_EPS) * gain


def rms_back(values, gain, grad_norm):
    mean_square = jnp.mean(values * values, axis=-1, keepdims=True)
    inverse = lax.rsqrt(mean_square + NORM_EPS)
    scaled_grad = grad_norm * gain
    grad_values = inverse * scaled_grad - values * inverse**3 * jnp.mean(
        values * scaled_grad, axis=-1, keepdims=True
    )
    grad_gain = jnp.sum(grad_norm * values * inverse, axis=0)
    return (grad_values, grad_gain)


def contract_rows(left_side, right_side):
    return lax.dot_general(
        left_side, right_side, (((0,), (0,)), ((), ())), preferred_element_type=jnp.float32
    )


def contract_cols(left_side, right_side):
    return lax.dot_general(
        left_side, right_side, (((1,), (1,)), ((), ())), preferred_element_type=jnp.float32
    )


def body(
    tokens,
    cotangent,
    segment_ids,
    routes,
    norm_attn,
    w_query,
    key_weight_matrix,
    value_weight_matrix,
    w_output,
    norm_moe,
    w_router,
    expert_in,
    expert_out,
):
    x_local = tokens[0].astype(jnp.float32)
    token_count, width = x_local.shape
    seg_row = segment_ids[0]
    row_length_local = seg_row.shape[0]
    query_group_width = QUERY_HEADS // KEY_VALUE_HEADS
    seq_index = lax.axis_index("seq")
    tok_start = seq_index * token_count
    positions = tok_start + jnp.arange(token_count, dtype=jnp.int32)
    seg_local = lax.dynamic_slice_in_dim(seg_row, tok_start, token_count)
    rope_local = lax.dynamic_slice_in_dim(doc_positions(seg_row), tok_start, token_count)
    gain_one, query_w, key_w, value_w, output_w, gain_two, router_w = (
        lax.all_gather(norm_attn.astype(jnp.bfloat16), ("seq", "row"), axis=0, tiled=True),
        lax.all_gather(w_query.astype(jnp.bfloat16), ("seq", "row"), axis=0, tiled=True),
        lax.all_gather(key_weight_matrix.astype(jnp.bfloat16), ("seq", "row"), axis=0, tiled=True),
        lax.all_gather(
            value_weight_matrix.astype(jnp.bfloat16), ("seq", "row"), axis=0, tiled=True
        ),
        lax.all_gather(w_output.astype(jnp.bfloat16), ("seq", "row"), axis=0, tiled=True),
        lax.all_gather(norm_moe.astype(jnp.bfloat16), ("seq", "row"), axis=0, tiled=True),
        lax.all_gather(w_router.astype(jnp.bfloat16), ("seq", "row"), axis=0, tiled=True),
    )
    gain_one_f = gain_one.astype(jnp.float32)
    gain_two_f = gain_two.astype(jnp.float32)
    normed_one = rms_scale(x_local, gain_one_f).astype(jnp.bfloat16)
    query_pre = jnp.dot(normed_one, query_w, preferred_element_type=jnp.float32)
    key_before_rotation = jnp.dot(normed_one, key_w, preferred_element_type=jnp.float32)
    value_pre = jnp.dot(normed_one, value_w, preferred_element_type=jnp.float32)
    cosine_table, sine_table = rope_tables(rope_local, HEAD_SIZE)
    rotated_query = apply_rotation_heads(query_pre, cosine_table, sine_table, QUERY_HEADS).astype(
        jnp.bfloat16
    )
    rotated_key = apply_rotation_heads(
        key_before_rotation, cosine_table, sine_table, KEY_VALUE_HEADS
    ).astype(jnp.bfloat16)
    value_reduced_precision = value_pre.astype(jnp.bfloat16)
    key_all, value_all = (
        lax.all_gather(rotated_key, "seq", axis=0, tiled=True),
        lax.all_gather(value_reduced_precision, "seq", axis=0, tiled=True),
    )
    heads_of_queries = rotated_query.reshape(
        token_count, KEY_VALUE_HEADS, query_group_width, HEAD_SIZE
    )
    block_of_keys = math.gcd(row_length_local, 512)
    first_key = jnp.sum((seg_row < seg_local[0]).astype(jnp.int32))
    lower_triangle_block = first_key // block_of_keys
    upper_triangle_block = (tok_start + token_count - 1) // block_of_keys + 1

    def block_scores(block_index):
        key_start = block_index * block_of_keys
        key_blk = lax.dynamic_slice_in_dim(key_all, key_start, block_of_keys).reshape(
            block_of_keys, KEY_VALUE_HEADS, HEAD_SIZE
        )
        value_blk = lax.dynamic_slice_in_dim(value_all, key_start, block_of_keys).reshape(
            block_of_keys, KEY_VALUE_HEADS, HEAD_SIZE
        )
        seg_keys = lax.dynamic_slice_in_dim(seg_row, key_start, block_of_keys)
        key_pos = key_start + jnp.arange(block_of_keys, dtype=jnp.int32)
        scores = (
            jnp.einsum(
                "tkgd,skd->kgts", heads_of_queries, key_blk, preferred_element_type=jnp.float32
            )
            * SCALE_OF_SCORES
        )
        allowed = (seg_local[:, None] == seg_keys[None, :]) & (
            positions[:, None] >= key_pos[None, :]
        )
        return (scores, allowed, key_blk, value_blk)

    def max_step(block_index, carried):
        running_max, running_sum = carried
        scores, allowed, _, _ = block_scores(block_index)
        masked = jnp.where(allowed, scores, NEGATIVE_HUGE)
        new_max = jnp.maximum(running_max, jnp.max(masked, axis=-1))
        fresh = jnp.sum(jnp.where(allowed, jnp.exp(masked - new_max[..., None]), 0.0), axis=-1)
        return (new_max, running_sum * jnp.exp(running_max - new_max) + fresh)

    initial_maximum = jnp.full(
        (KEY_VALUE_HEADS, query_group_width, token_count), NEGATIVE_HUGE, jnp.float32
    )
    initial_running_sum = jnp.zeros((KEY_VALUE_HEADS, query_group_width, token_count), jnp.float32)
    final_max, final_total = lax.fori_loop(
        lower_triangle_block, upper_triangle_block, max_step, (initial_maximum, initial_running_sum)
    )
    log_total = final_max + jnp.log(final_total)

    def mixing_update(block_index, mixed_sum):
        scores, allowed, _, value_blk = block_scores(block_index)
        probs_low = jnp.where(allowed, jnp.exp(scores - log_total[..., None]), 0.0).astype(
            jnp.bfloat16
        )
        return mixed_sum + jnp.einsum(
            "kgts,skd->tkgd", probs_low, value_blk, preferred_element_type=jnp.float32
        )

    attention_result = lax.fori_loop(
        lower_triangle_block,
        upper_triangle_block,
        mixing_update,
        jnp.zeros((token_count, KEY_VALUE_HEADS, query_group_width, HEAD_SIZE), jnp.float32),
    ).reshape(token_count, QUERY_HEADS * HEAD_SIZE)
    attended_low = attention_result.astype(jnp.bfloat16)
    attn_out = jnp.dot(attended_low, output_w, preferred_element_type=jnp.float32)
    resid = x_local + RESIDUAL_SCALE * attn_out
    normed_two = rms_scale(resid, gain_two_f).astype(jnp.bfloat16)
    logits = jnp.dot(normed_two, router_w, preferred_element_type=jnp.float32)
    route_local = routes[0]
    expert_ids = jnp.arange(E, dtype=jnp.int32)
    route_hot = (route_local[:, :, None] == expert_ids[None, None, :]).astype(jnp.float32)
    chosen = jnp.sum(route_hot * logits[:, None, :], axis=-1)
    gates = jax.nn.softmax(chosen, axis=-1)
    pair_count = token_count * TOPK
    flat_ids = route_local.reshape(pair_count)
    flat_hot = (flat_ids[:, None] == expert_ids[None, :]).astype(jnp.int32)
    earlier = jnp.cumsum(flat_hot, axis=0) - flat_hot
    slot_rank = jnp.sum(earlier * flat_hot, axis=1)
    pair_slot = flat_ids * CAP + slot_rank
    slot_pair = (
        jnp.full((E * CAP,), -1, jnp.int32)
        .at[pair_slot]
        .set(jnp.arange(pair_count, dtype=jnp.int32))
    )
    slot_used = slot_pair >= 0
    pair_safe = jnp.where(slot_used, slot_pair, 0)
    slot_token = pair_safe // TOPK
    slot_inputs = jnp.where(
        slot_used[:, None], normed_two[slot_token], jnp.zeros((), jnp.bfloat16)
    ).reshape(E, CAP, width)
    in_all, out_all = (
        lax.all_gather(expert_in.astype(jnp.bfloat16), ("seq", "row"), axis=0, tiled=True),
        lax.all_gather(expert_out.astype(jnp.bfloat16), ("seq", "row"), axis=0, tiled=True),
    )
    in_stack = in_all.reshape(E, width, 2 * F)
    out_stack = out_all.reshape(E, width, F)
    pre_act = jnp.einsum("ecd,edf->ecf", slot_inputs, in_stack, preferred_element_type=jnp.float32)
    gate_pre = pre_act[..., :F]
    up_pre = pre_act[..., F:]
    hidden_low = (jax.nn.silu(gate_pre) * up_pre).astype(jnp.bfloat16)
    expert_res = jnp.einsum(
        "ecf,edf->ecd", hidden_low, out_stack, preferred_element_type=jnp.float32
    )
    pair_res = expert_res.reshape(E * CAP, width)[pair_slot].reshape(token_count, TOPK, width)
    moe_sum = jnp.sum(gates[:, :, None] * pair_res, axis=1)
    layer_sum = resid + RESIDUAL_SCALE * moe_sum
    grad_out = cotangent[0].astype(jnp.float32)
    grad_moe = RESIDUAL_SCALE * grad_out
    grad_gates = jnp.sum(pair_res * grad_moe[:, None, :], axis=-1)
    gates_flat = gates.reshape(pair_count)
    slot_grad = (
        jnp.where(slot_used[:, None], gates_flat[pair_safe][:, None] * grad_moe[slot_token], 0.0)
        .astype(jnp.bfloat16)
        .reshape(E, CAP, width)
    )
    in_back, out_back = (
        lax.all_gather(expert_in.astype(jnp.bfloat16), ("seq", "row"), axis=0, tiled=True),
        lax.all_gather(expert_out.astype(jnp.bfloat16), ("seq", "row"), axis=0, tiled=True),
    )
    in_stack_back = in_back.reshape(E, width, 2 * F)
    out_stack_back = out_back.reshape(E, width, F)
    grad_hidden = jnp.einsum(
        "ecd,edf->ecf", slot_grad, out_stack_back, preferred_element_type=jnp.float32
    )
    gate_sig = jax.nn.sigmoid(gate_pre)
    gate_act = gate_pre * gate_sig
    grad_gate = grad_hidden * up_pre * (gate_sig + gate_pre * gate_sig * (1.0 - gate_sig))
    grad_up = grad_hidden * gate_act
    grad_pre = jnp.concatenate([grad_gate, grad_up], axis=-1).astype(jnp.bfloat16)
    slot_back = jnp.einsum(
        "ecf,edf->ecd", grad_pre, in_stack_back, preferred_element_type=jnp.float32
    )
    pair_back = slot_back.reshape(E * CAP, width)[pair_slot].reshape(token_count, TOPK, width)
    grad_chosen = gates * (grad_gates - jnp.sum(gates * grad_gates, axis=-1, keepdims=True))
    grad_logits = jnp.sum(route_hot * grad_chosen[:, :, None], axis=1)
    grad_normed_two = jnp.sum(pair_back, axis=1) + jnp.dot(
        grad_logits, router_w.astype(jnp.float32).T, precision=HIGHEST_DOT
    )
    grad_router = jnp.dot(normed_two.astype(jnp.float32).T, grad_logits, precision=HIGHEST_DOT)
    grad_resid_norm, grad_gain_two = rms_back(resid, gain_two_f, grad_normed_two)
    grad_resid = grad_out + grad_resid_norm
    shard_rows = expert_in.shape[0]

    def one_piece(piece_index):
        first_row = piece_index * shard_rows
        expert_index = first_row // width
        feature_start = first_row % width
        inputs_part = lax.dynamic_slice(
            slot_inputs, (expert_index, 0, feature_start), (1, CAP, shard_rows)
        )[0]
        grads_part = lax.dynamic_slice(
            slot_grad, (expert_index, 0, feature_start), (1, CAP, shard_rows)
        )[0]
        pre_grads = lax.dynamic_index_in_dim(grad_pre, expert_index, 0, keepdims=False)
        hidden_one = lax.dynamic_index_in_dim(hidden_low, expert_index, 0, keepdims=False)
        in_term = contract_rows(inputs_part, pre_grads)
        out_term = contract_rows(grads_part, hidden_one)
        return jnp.concatenate([in_term, out_term], axis=1)

    pieces = lax.map(
        one_piece,
        jnp.arange(lax.axis_size(("seq", "row")) * shard_rows // shard_rows, dtype=jnp.int32),
    )
    expert_grads = lax.psum_scatter(
        pieces.reshape(lax.axis_size(("seq", "row")) * shard_rows, 3 * F),
        ("seq", "row"),
        scatter_dimension=0,
        tiled=True,
    )
    grad_attn_low = (RESIDUAL_SCALE * grad_resid).astype(jnp.bfloat16)
    grad_output_w = contract_rows(attended_low, grad_attn_low)
    gradient_attention_lowered = contract_cols(grad_attn_low, output_w).astype(jnp.bfloat16)
    gradient_of_heads = gradient_attention_lowered.reshape(
        token_count, KEY_VALUE_HEADS, query_group_width, HEAD_SIZE
    )
    row_delta = jnp.sum(
        gradient_of_heads.astype(jnp.float32)
        * attention_result.reshape(token_count, KEY_VALUE_HEADS, query_group_width, HEAD_SIZE),
        axis=-1,
    )
    delta_heads = jnp.transpose(row_delta, (1, 2, 0))

    def back_step(block_index, carried):
        grad_query, grad_keys, grad_values = carried
        scores, allowed, key_blk, value_blk = block_scores(block_index)
        probs = jnp.where(allowed, jnp.exp(scores - log_total[..., None]), 0.0)
        probs_low = probs.astype(jnp.bfloat16)
        grad_probs = jnp.einsum(
            "tkgd,skd->kgts", gradient_of_heads, value_blk, preferred_element_type=jnp.float32
        )
        grad_scores = (probs * (grad_probs - delta_heads[..., None])).astype(jnp.bfloat16)
        grad_query = grad_query + jnp.einsum(
            "kgts,skd->tkgd", grad_scores, key_blk, preferred_element_type=jnp.float32
        )
        key_part = jnp.einsum(
            "kgts,tkgd->skd", grad_scores, heads_of_queries, preferred_element_type=jnp.float32
        ).reshape(block_of_keys, KEY_VALUE_HEADS * HEAD_SIZE)
        value_part = jnp.einsum(
            "kgts,tkgd->skd", probs_low, gradient_of_heads, preferred_element_type=jnp.float32
        ).reshape(block_of_keys, KEY_VALUE_HEADS * HEAD_SIZE)
        key_start = block_index * block_of_keys
        grad_keys = lax.dynamic_update_slice_in_dim(
            grad_keys,
            lax.dynamic_slice_in_dim(grad_keys, key_start, block_of_keys) + key_part,
            key_start,
            0,
        )
        grad_values = lax.dynamic_update_slice_in_dim(
            grad_values,
            lax.dynamic_slice_in_dim(grad_values, key_start, block_of_keys) + value_part,
            key_start,
            0,
        )
        return (grad_query, grad_keys, grad_values)

    start_grads = (
        jnp.zeros((token_count, KEY_VALUE_HEADS, query_group_width, HEAD_SIZE), jnp.float32),
        jnp.zeros((row_length_local, KEY_VALUE_HEADS * HEAD_SIZE), jnp.float32),
        jnp.zeros((row_length_local, KEY_VALUE_HEADS * HEAD_SIZE), jnp.float32),
    )
    grad_query, grad_keys, grad_values = lax.fori_loop(
        lower_triangle_block, upper_triangle_block, back_step, start_grads
    )
    local_key_rows, value_own = (
        lax.psum_scatter(
            grad_keys.astype(jnp.bfloat16), "seq", scatter_dimension=0, tiled=True
        ).astype(jnp.float32),
        lax.psum_scatter(
            grad_values.astype(jnp.bfloat16), "seq", scatter_dimension=0, tiled=True
        ).astype(jnp.float32),
    )
    grad_query_pre = reverse_rotation_heads(
        grad_query.reshape(token_count, QUERY_HEADS * HEAD_SIZE) * SCALE_OF_SCORES,
        cosine_table,
        sine_table,
        QUERY_HEADS,
    ).astype(jnp.bfloat16)
    gradient_key_unrotated = reverse_rotation_heads(
        local_key_rows * SCALE_OF_SCORES, cosine_table, sine_table, KEY_VALUE_HEADS
    ).astype(jnp.bfloat16)
    grad_value_pre = value_own.astype(jnp.bfloat16)
    grad_query_w = contract_rows(normed_one, grad_query_pre)
    grad_key_w = contract_rows(normed_one, gradient_key_unrotated)
    grad_value_w = contract_rows(normed_one, grad_value_pre)
    grad_normed_one = (
        contract_cols(grad_query_pre, query_w)
        + contract_cols(gradient_key_unrotated, key_w)
        + contract_cols(grad_value_pre, value_w)
    )
    grad_x_norm, grad_gain_one = rms_back(x_local, gain_one_f, grad_normed_one)
    grad_input = grad_resid + grad_x_norm
    dense_sums = (
        lax.psum_scatter(grad_gain_one, ("seq", "row"), scatter_dimension=0, tiled=True),
        lax.psum_scatter(grad_query_w, ("seq", "row"), scatter_dimension=0, tiled=True),
        lax.psum_scatter(grad_key_w, ("seq", "row"), scatter_dimension=0, tiled=True),
        lax.psum_scatter(grad_value_w, ("seq", "row"), scatter_dimension=0, tiled=True),
        lax.psum_scatter(grad_output_w, ("seq", "row"), scatter_dimension=0, tiled=True),
        lax.psum_scatter(grad_gain_two, ("seq", "row"), scatter_dimension=0, tiled=True),
        lax.psum_scatter(grad_router, ("seq", "row"), scatter_dimension=0, tiled=True),
    )
    return (
        layer_sum.astype(jnp.bfloat16)[None],
        grad_input[None],
        dense_sums[0],
        dense_sums[1],
        dense_sums[2],
        dense_sums[3],
        dense_sums[4],
        dense_sums[5],
        dense_sums[6],
        expert_grads[:, : 2 * F],
        expert_grads[:, 2 * F :],
    )


def solution(mesh):
    in_specs = (
        P("row", "seq", None),
        P("row", "seq", None),
        P("row", None),
        P("row", "seq", None),
        P(("seq", "row")),
        P(("seq", "row"), None),
        P(("seq", "row"), None),
        P(("seq", "row"), None),
        P(("seq", "row"), None),
        P(("seq", "row")),
        P(("seq", "row"), None),
        P(("seq", "row"), None),
        P(("seq", "row"), None),
    )
    out_specs = (
        P("row", "seq", None),
        P("row", "seq", None),
        P(("seq", "row")),
        P(("seq", "row"), None),
        P(("seq", "row"), None),
        P(("seq", "row"), None),
        P(("seq", "row"), None),
        P(("seq", "row")),
        P(("seq", "row"), None),
        P(("seq", "row"), None),
        P(("seq", "row"), None),
    )
    return jax.shard_map(body, mesh=mesh, in_specs=in_specs, out_specs=out_specs, check_vma=False)
```

profile of v0, /device:TPU:0, one launch (start us, length us, event | category | flops | bytes accessed | tf_op | source)
XLA Modules:
  0.0 2503.9 jit_solution(4478467016662320655)
XLA Ops:
  13.7 42.1 %all-reduce.5 = (bf16[1024]{0:T(1024)(128)(2,1)S(1)}, bf16[1024]{0:T(1024)(128)(2,1)S(1)}) all-reduce(bf16[1024]{0:T(1024)(128)(2,1)S(1)} %dynamic-update-slice, bf16[1024]{0:T(1024)(128)(2,1)S(1)} %dynamic-update-slice.1), channel_id=1, replica_groups=mesh['seq'=8,'row'=4] {'seq','row'}, use_global_device_ids=true, to_apply=%add | all-reduce | flops 2048 | bytes 8192
  57.6 10.5 all-gather.10.cloned.1.call-done
  72.7 51.5 %all-gather.14.cloned.1.call-done = bf16[1024,512]{1,0:T(8,128)(2,1)} async-done(((bf16[32,512]{1,0:T(8,128)(2,1)}), bf16[1024,512]{1,0:T(8,128)(2,1)}) %all-gather.14.cloned.1.call-update) | async-done | bytes 1048592 | tf_op jit(solution)/shard_map/all_gather | solution.py:126
  137.9 40.0 %all-gather = bf16[32,32,16]{1,2,0:T(8,128)(2,1)S(1)} all-gather(bf16[1,32,16]{1,2,0:T(8,128)(2,1)S(1)} %convert_bitcast_fusion.1), channel_id=1, replica_groups=mesh['seq'=8,'row'=4] {'seq','row'}, dimensions={0}, use_global_device_ids=true | all-gather | bytes 33792 | tf_op jit(solution)/shard_map/all_gather | solution.py:132
  178.1 4.5 reduce-window.19
  183.4 8.1 scatter_custom_fusion
  191.8 14.1 gather_fusion.3
  210.5 23.2 all-gather.12.cloned.1.call-done
  233.7 2.9 copy.93
  236.6 49.1 %all-gather.16.cloned.1.call-done = bf16[2048,512]{0,1:T(8,128)(2,1)} async-done(((bf16[256,512]{0,1:T(8,128)(2,1)}), bf16[2048,512]{0,1:T(8,128)(2,1)}) %all-gather.16.cloned.1.call-update) | async-done | bytes 2097168 | tf_op jit(solution)/shard_map/all_gather | solution.py:149
  285.8 4.9 while.52
  291.8 7.5 while.53
  294.2 4.9 fusion.194
  299.3 2.9 convert_element_type.187
  302.2 41.4 %all-gather.20.cloned.1.call-done = bf16[1024,1024]{1,0:T(8,128)(2,1)} async-done(((bf16[32,1024]{1,0:T(8,128)(2,1)}), bf16[1024,1024]{1,0:T(8,128)(2,1)}) %all-gather.20.cloned.1.call-update) | async-done | bytes 2097168 | tf_op jit(solution)/shard_map/all_gather | solution.py:130
  347.4 14.0 gather_fusion
  362.1 17.4 gather_fusion.2
  379.6 6.6 broadcast_select_fusion
  386.2 8.7 select_convert_fusion
  394.8 145.4 %all-gather.22.cloned.1.call-done = bf16[16384,1024]{1,0:T(8,128)(2,1)} async-done(((bf16[512,1024]{1,0:T(8,128)(2,1)}), bf16[16384,1024]{1,0:T(8,128)(2,1)}) %all-gather.22.cloned.1.call-update) | async-done | bytes 33554448 | tf_op jit(solution)/shard_map/all_gather | solution.py:241
  540.2 25.4 %fusion.103 = f32[16,192,1024]{2,1,0:T(8,128)} fusion(bf16[16,192,1024]{2,1,0:T(8,128)(2,1)} %broadcast_select_fusion, bf16[16,1024,1024]{2,1,0:T(8,128)(2,1)} %bitcast.351), kind=kOutput, calls=%fused_computation.203 | convolution fusion | flops 6442450944 | bytes 52428800 | tf_op jit(solution)/shard_map/ecd,edf->ecf/dot_general | solution.py:246
  565.6 91.1 %all-gather.24.cloned.1.call-done = bf16[16384,512]{1,0:T(8,128)(2,1)} async-done(((bf16[512,512]{1,0:T(8,128)(2,1)}), bf16[16384,512]{1,0:T(8,128)(2,1)}) %all-gather.24.cloned.1.call-update) | async-done | bytes 16777232 | tf_op jit(solution)/shard_map/all_gather | solution.py:242
  656.7 16.6 multiply_convert_fusion.1
  673.3 13.8 fusion.104
  687.2 31.7 %fusion.99 = f32[16,192,1024]{2,1,0:T(8,128)} fusion(bf16[16,1024,1024]{2,1,0:T(8,128)(2,1)} %bitcast.352, bf16[16,192,512]{2,1,0:T(8,128)(2,1)} %get-tuple-element.582, bf16[16,192,512]{2,1,0:T(8,128)(2,1)S(1)} %get-tuple-element.581), kind=kOutput, calls=%fused_computation.199 | convolution fusion | flops 6455033856 | bytes 52428800 | tf_op jit(solution)/shard_map/ecf,edf->ecd/dot_general | solution.py:279
  718.9 16.3 gather_fusion.4
  735.1 5.4 bitcast_reduce_fusion
  740.5 16.4 gather_fusion.1
  756.9 6.5 fusion.48
  765.1 2.9 convert_add_fusion
  768.0 3.1 convolution_convert_fusion
  777.7 14.8 while.54
  789.0 3.3 constant_dynamic-update-slice_fusion.3
  792.5 3.8 convert_element_type.212
  796.4 3.9 convert_element_type.208
  801.8 6.3 pad_maximum_fusion
  808.3 205.7 %while.51 = (s32[]{:T(128)}, f32[32,512,1536]{2,1,0:T(8,128)}, s32[32]{0:T(128)S(1)}, bf16[16,192,1024]{2,1,0:T(8,128)(2,1)}, bf16[16,192,1024]{2,1,0:T(8,128)(2...) while((s32[]{:T(128)}, f32[32,512,1536]{2,1,0:T(8,128)}, ...), condition=%wide.region_40.41_spmd, body=%wide.region_39.40_spmd.sunk | while | flops 302776352 | bytes 10423728 | solution.py:309
  1018.1 2.9 fusion.74
  1021.1 2.9 fusion.77
  1027.1 3.3 fusion.105
  1030.4 82.6 %reduce-scatter.25.cloned.1.call-done = f32[32,16]{1,0:T(8,128)} async-done(((f32[1024,16]{1,0:T(8,128)}), f32[32,16]{1,0:T(8,128)}) %reduce-scatter.25.cloned.1.call-update) | async-done | bytes 2064
  1118.4 37.0 %all-reduce.4 = (f32[1024]{0:T(1024)S(1)}, f32[1024]{0:T(1024)S(1)}) all-reduce(f32[1024]{0:T(1024)S(1)} %get-tuple-element.489, f32[1024]{0:T(1024)S(1)} %copy-done.34), channel_id=4, replica_groups=mesh['seq'=8,'row'=4] {'seq','row'}, use_global_device_ids=true, to_apply=%region_31.32.clone | all-reduce | flops 2048 | bytes 16384
  1157.9 785.2 %reduce-scatter.23.cloned.1.call-done = f32[512,1536]{1,0:T(8,128)} async-done(((f32[16384,1536]{1,0:T(8,128)}), f32[512,1536]{1,0:T(8,128)}) %reduce-scatter.23.cloned.1.call-update) | async-done | bytes 3145744 | tf_op jit(solution)/shard_map/reduce_scatter | solution.py:313
  1945.3 3.2 slice.104
  1948.5 137.9 %reduce-scatter.21.cloned.1.call-done = f32[32,1024]{1,0:T(8,128)} async-done(((f32[1024,1024]{1,0:T(8,128)}), f32[32,1024]{1,0:T(8,128)}) %reduce-scatter.21.cloned.1.call-update) | async-done | bytes 131088 | tf_op jit(solution)/shard_map/reduce_scatter | solution.py:406
  2086.4 139.9 %reduce-scatter.15.cloned.1.call-done = f32[32,1024]{1,0:T(8,128)} async-done(((f32[1024,1024]{1,0:T(8,128)}), f32[32,1024]{1,0:T(8,128)}) %reduce-scatter.15.cloned.1.call-update) | async-done | bytes 131088 | tf_op jit(solution)/shard_map/reduce_scatter | solution.py:403
  2226.3 135.4 %reduce-scatter.19.cloned.1.call-done = f32[32,512]{1,0:T(8,128)} async-done(((f32[1024,512]{1,0:T(8,128)}), f32[32,512]{1,0:T(8,128)}) %reduce-scatter.19.cloned.1.call-update) | async-done | bytes 65552 | tf_op jit(solution)/shard_map/reduce_scatter | solution.py:405
  2361.8 135.3 %reduce-scatter.17.cloned.1.call-done = f32[32,512]{1,0:T(8,128)} async-done(((f32[1024,512]{1,0:T(8,128)}), f32[32,512]{1,0:T(8,128)}) %reduce-scatter.17.cloned.1.call-update) | async-done | bytes 65552 | tf_op jit(solution)/shard_map/reduce_scatter | solution.py:404
  (377 shorter events, 263.7 us)
Async XLA Ops:
  7.2 121.0 %copy-start.27 = (f32[32,1024]{1,0:T(8,128)S(1)}, f32[32,1024]{1,0:T(8,128)}, u32[]{:S(2)}) copy-start(f32[32,1024]{1,0:T(8,128)} %param.29) | copy-start | bytes 393220
  7.2 60.8 %all-gather.10.cloned.1.call-start = ((), (), s32[]{:S(2)}) async-start(), calls=%async_computation.8 | async-start | bytes 1081344 | tf_op jit(solution)/shard_map/all_gather | solution.py:127
  8.7 115.4 %all-gather.14.cloned.1.call-start = ((), (), s32[]{:S(2)}) async-start(), calls=%async_computation.10 | async-start | bytes 1081344 | tf_op jit(solution)/shard_map/all_gather | solution.py:126
  10.3 196.2 %all-gather.18.cloned.1.call-start = ((), (), s32[]{:S(2)}) async-start(), calls=%async_computation.12 | async-start | bytes 2162688 | tf_op jit(solution)/shard_map/all_gather | solution.py:125
  11.9 221.8 %all-gather.12.cloned.1.call-start = ((), (), s32[]{:S(2)}) async-start(), calls=%async_computation.9 | async-start | bytes 2359296 | tf_op jit(solution)/shard_map/all_gather | solution.py:150
  55.7 153.6 %copy-start.25 = (f32[1024]{0:T(1024)}, f32[1024]{0:T(1024)S(1)}, u32[]{:S(2)}) copy-start(f32[1024]{0:T(1024)S(1)} %convert_element_type.175) | copy-start | bytes 12292
  57.6 151.8 %copy-start.32 = (f32[256]{0:T(256)}, f32[256]{0:T(256)S(1)}, u32[]{:S(2)}) copy-start(f32[256]{0:T(256)S(1)} %get-tuple-element.599) | copy-start | bytes 3076
  68.0 63.7 %copy-start.15 = (f32[512,512]{1,0:T(8,128)S(1)}, f32[512,512]{1,0:T(8,128)}, u32[]{:S(2)}) copy-start(f32[512,512]{1,0:T(8,128)} %param.33) | copy-start | bytes 3145732
  70.7 215.0 %all-gather.16.cloned.1.call-start = ((), (), s32[]{:S(2)}) async-start(), calls=%async_computation.11 | async-start | bytes 2359296 | tf_op jit(solution)/shard_map/all_gather | solution.py:149
  72.6 137.6 %copy-start.17 = (f32[256,32]{0,1:T(8,128)}, f32[256,32]{0,1:T(8,128)S(1)}, u32[]{:S(2)}) copy-start(f32[256,32]{0,1:T(8,128)S(1)} %get-tuple-element.596) | copy-start | bytes 98308
  72.6 137.6 %copy-start.19 = (f32[256,32]{0,1:T(8,128)}, f32[256,32]{0,1:T(8,128)S(1)}, u32[]{:S(2)}) copy-start(f32[256,32]{0,1:T(8,128)S(1)} %get-tuple-element.597) | copy-start | bytes 98308
  72.6 60.1 %copy-start.21 = (s32[1,2048]{1,0:T(1,128)S(1)}, s32[1,2048]{1,0:T(1,128)}, u32[]{:S(2)}) copy-start(s32[1,2048]{1,0:T(1,128)} %param.23) | copy-start | bytes 24580
  124.2 13.0 copy-start.28
  124.2 13.7 copy-start.39
  125.7 66.0 %copy-start.14 = (bf16[1,256,1024]{2,1,0:T(8,128)(2,1)S(1)}, bf16[1,256,1024]{2,1,0:T(8,128)(2,1)}, u32[]{:S(2)}) copy-start(bf16[1,256,1024]{2,1,0:T(8,128)(2,1)} %param.22) | copy-start | bytes 1572868
  128.2 215.5 %all-gather.20.cloned.1.call-start = ((), (), s32[]{:S(2)}) async-start(), calls=%async_computation.13 | async-start | bytes 2162688 | tf_op jit(solution)/shard_map/all_gather | solution.py:130
  128.9 411.3 %all-gather.22.cloned.1.call-start = ((), (), s32[]{:S(2)}) async-start(), calls=%async_computation.14 | async-start | bytes 34603008 | tf_op jit(solution)/shard_map/all_gather | solution.py:241
  131.7 525.0 %all-gather.24.cloned.1.call-start = ((), (), s32[]{:S(2)}) async-start(), calls=%async_computation.15 | async-start | bytes 17301504 | tf_op jit(solution)/shard_map/all_gather | solution.py:242
  132.7 888.4 %reduce-scatter.13.cloned.1.call-start = ((), (), s32[]{:S(2)}) async-start(), calls=%async_computation.17 | async-start | bytes 2359296 | tf_op jit(solution)/shard_map/reduce_scatter | solution.py:377
  137.6 209.4 %copy-start.30 = (f32[1024]{0:T(1024)}, f32[1024]{0:T(1024)S(1)}, u32[]{:S(2)}) copy-start(f32[1024]{0:T(1024)S(1)} %convert_element_type.191) | copy-start | bytes 12292
  191.8 14.1 copy-start
  191.8 17.6 copy-start.7
  299.3 47.6 %copy-start.4 = (bf16[256,8,2,64]{0,3,2,1:T(8,128)(2,1)}, bf16[256,8,2,64]{0,3,2,1:T(8,128)(2,1)S(1)}, u32[]{:S(2)}) copy-start(bf16[256,8,2,64]{0,3,2,1:T(8,128)(2,1)S(1)} %get-tuple-element.1063) | copy-start | bytes 1572868
  299.3 62.1 %copy-start.6 = (bf16[2048,512]{0,1:T(8,128)(2,1)}, bf16[2048,512]{0,1:T(8,128)(2,1)S(1)}, u32[]{:S(2)}) copy-start(bf16[2048,512]{0,1:T(8,128)(2,1)S(1)} %get-tuple-element.1068) | copy-start | bytes 6291460
  299.3 62.1 %copy-start.22 = (s32[2048]{0:T(1024)}, s32[2048]{0:T(1024)S(1)}, u32[]{:S(2)}) copy-start(s32[2048]{0:T(1024)S(1)} %get-tuple-element.1097) | copy-start | bytes 24580
  299.3 62.1 %copy-start.23 = (s32[256]{0:T(256)}, s32[256]{0:T(256)S(1)}, u32[]{:S(2)}) copy-start(s32[256]{0:T(256)S(1)} %get-tuple-element.1099) | copy-start | bytes 3076
  299.3 62.1 %copy-start.35 = (f32[8,2,256]{2,1,0:T(2,128)}, f32[8,2,256]{2,1,0:T(2,128)S(1)}, u32[]{:S(2)}) copy-start(f32[8,2,256]{2,1,0:T(2,128)S(1)} %get-tuple-element.1111) | copy-start | bytes 49156
  346.9 14.5 copy-start.37
  347.4 14.0 copy-start.2
  673.3 13.8 copy-start.11
  687.2 31.7 %copy-start.29 = (s32[2048]{0:T(1024)S(1)}, s32[2048]{0:T(1024)}, u32[]{:S(2)}) copy-start(s32[2048]{0:T(1024)} %broadcast_clamp_fusion) | copy-start | bytes 24580
  740.5 16.4 copy-start.1
  756.9 6.7 copy-start.10
  756.9 6.7 copy-start.31
  756.9 6.7 copy-start.38
  756.9 8.2 copy-start.41
  763.6 8.9 copy-start.12
  771.2 6.5 copy-start.36
  796.3 227.7 %reduce-scatter.11.cloned.1.call-start = ((), (), s32[]{:S(2)}) async-start(), calls=%async_computation.16 | async-start | bytes 2359296 | tf_op jit(solution)/shard_map/reduce_scatter | solution.py:374
  800.3 312.8 %reduce-scatter.25.cloned.1.call-start = ((), (), s32[]{:S(2)}) async-start(), calls=%async_computation.23 | async-start | bytes 540672
  808.2 1134.9 %reduce-scatter.23.cloned.1.call-start = ((), (), s32[]{:S(2)}) async-start(), calls=%async_computation.22 | async-start | bytes 103809024 | tf_op jit(solution)/shard_map/reduce_scatter | solution.py:313
  1014.0 1072.4 %reduce-scatter.21.cloned.1.call-start = ((), (), s32[]{:S(2)}) async-start(), calls=%async_computation.21 | async-start | bytes 4325376 | tf_op jit(solution)/shard_map/reduce_scatter | solution.py:406
  1017.6 1208.7 %reduce-scatter.15.cloned.1.call-start = ((), (), s32[]{:S(2)}) async-start(), calls=%async_computation.18 | async-start | bytes 4325376 | tf_op jit(solution)/shard_map/reduce_scatter | solution.py:403
  1021.0 1340.8 %reduce-scatter.19.cloned.1.call-start = ((), (), s32[]{:S(2)}) async-start(), calls=%async_computation.20 | async-start | bytes 2162688 | tf_op jit(solution)/shard_map/reduce_scatter | solution.py:405
  1024.0 1473.0 %reduce-scatter.17.cloned.1.call-start = ((), (), s32[]{:S(2)}) async-start(), calls=%async_computation.19 | async-start | bytes 2162688 | tf_op jit(solution)/shard_map/reduce_scatter | solution.py:404
  1025.1 91.4 %copy-start.16 = (bf16[256,512]{0,1:T(8,128)(2,1)S(1)}, bf16[256,512]{0,1:T(8,128)(2,1)}, u32[]{:S(2)}) copy-start(bf16[256,512]{0,1:T(8,128)(2,1)} %reduce-scatter.13.cloned.1.call-done) | copy-start | bytes 786436
  1027.1 91.3 %copy-start.34 = (f32[1024]{0:T(1024)S(1)}, f32[1024]{0:T(1024)}, u32[]{:S(2)}) copy-start(f32[1024]{0:T(1024)} %get-tuple-element.487) | copy-start | bytes 12292
  1027.1 129.5 %copy-start.40 = (f32[256]{0:T(256)S(1)}, f32[256]{0:T(256)}, u32[]{:S(2)}) copy-start(f32[256]{0:T(256)} %get-tuple-element.598) | copy-start | bytes 3076
  (10 other events, 39.0 us)
Sparse Core Ops, SparseCore 0:
  11.5 56.5 all-gather.9
  71.5 52.6 all-gather.13
  127.6 55.3 all-gather.17
  185.5 48.1 all-gather.11
  236.2 49.5 all-gather.15
  289.1 54.5 all-gather.19
  346.5 193.6 all-gather.21
  543.6 113.0 all-gather.23
  796.4 109.6 reduce-scatter.12
  910.1 66.9 reduce-scatter.10
  979.9 133.1 reduce-scatter.24
  1120.5 822.5 reduce-scatter.22
  1946.0 140.3 reduce-scatter.20
  2089.2 137.0 reduce-scatter.14
  2229.1 132.6 reduce-scatter.18
  2364.4 132.5 reduce-scatter.16
where the time goes:
time: 2520 us; the launch traced here: 2500 us
  waiting for transfers between devices  1830 us (73%)
  matrix products  236 us (9%)
  other arithmetic  140 us (6%)
  local copies, waits for them, and re-layouts  138 us (5%)
  blocking collectives  119 us (5%)
    reduce_scatter x1, waiting for transfers between devices, body(): lax.psum_scatter(pieces.reshape(lax.axis_size(('seq', 'row')) * shard_row...  785 us
    all_gather x1, waiting for transfers between devices, body(): lax.all_gather(expert_in.astype(jnp.bfloat16), ('seq', 'row'), axis=0, ti...  145 us
    reduce_scatter x1, waiting for transfers between devices, body(): lax.psum_scatter(grad_query_w, ('seq', 'row'), scatter_dimension=0, tiled...  140 us
    reduce_scatter x1, waiting for transfers between devices, body(): lax.psum_scatter(grad_output_w, ('seq', 'row'), scatter_dimension=0, tile...  138 us
    reduce_scatter x1, waiting for transfers between devices, body(): lax.psum_scatter(grad_value_w, ('seq', 'row'), scatter_dimension=0, tiled...  135 us
    reduce_scatter x1, waiting for transfers between devices, body(): lax.psum_scatter(grad_key_w, ('seq', 'row'), scatter_dimension=0, tiled=T...  135 us
    dot_general x68, matrix products, contract_rows(): lax.dot_general(left_side, right_side, (((0,), (0,)), ((), ())), preferre...  113 us
    all_gather x1, waiting for transfers between devices, body(): lax.all_gather(expert_out.astype(jnp.bfloat16), ('seq', 'row'), axis=0, t...  91.1 us
  transfers between devices with their start and end apart: 16, of which 13 were waited for; matrix products, arithmetic and copies ran while one was open for 15% of the time, Pallas kernels for 0%

commit v1 on v0

v1 whole, which is shorter than its diff:
```python
import math

import jax
import jax.numpy as jnp
from jax import lax
from jax.sharding import Mesh, PartitionSpec as P

QUERY_HEADS = 16
KEY_VALUE_HEADS = 8
HEAD_SIZE = 64
F = 512
E = 16
GROUPS = 4
EXPERTS_HERE = E // GROUPS

NORM_EPS = 1e-06
RESIDUAL_SCALE = 0.22
SCALE_OF_SCORES = 0.015625
ROPE_BASE = 10000.0
NEGATIVE_HUGE = -1e30
HIGHEST_DOT = lax.Precision.HIGHEST

PLANE = ("b", "row")
SEQ = ("a", "b")
ALL = ("a", "b", "row")


def rope_tables(positions, head_size):
    half_size = head_size // 2
    freq_scale = jnp.power(ROPE_BASE, -2.0 * jnp.arange(half_size, dtype=jnp.float32) / head_size)
    angle_table = positions.astype(jnp.float32)[:, None] * freq_scale[None, :]
    return (jnp.cos(angle_table), jnp.sin(angle_table))


def apply_rotation_heads(values, cosine_table, sine_table, head_count):
    token_count = values.shape[0]
    shaped = values.reshape(token_count, head_count, -1)
    half_size = shaped.shape[-1] // 2
    first_half = shaped[..., :half_size]
    second_half = shaped[..., half_size:]
    cos_b = cosine_table[:, None, :]
    sin_b = sine_table[:, None, :]
    turned = jnp.concatenate(
        [first_half * cos_b - second_half * sin_b, second_half * cos_b + first_half * sin_b],
        axis=-1,
    )
    return turned.reshape(token_count, -1)


def reverse_rotation_heads(grads_in, cosine_table, sine_table, head_count):
    return apply_rotation_heads(grads_in, cosine_table, -sine_table, head_count)


def rms_scale(values, gain):
    mean_square = jnp.mean(values * values, axis=-1, keepdims=True)
    return values * lax.rsqrt(mean_square + NORM_EPS) * gain


def rms_back(values, gain, grad_norm):
    mean_square = jnp.mean(values * values, axis=-1, keepdims=True)
    inverse = lax.rsqrt(mean_square + NORM_EPS)
    scaled_grad = grad_norm * gain
    grad_values = inverse * scaled_grad - values * inverse**3 * jnp.mean(
        values * scaled_grad, axis=-1, keepdims=True
    )
    grad_gain = jnp.sum(grad_norm * values * inverse, axis=0)
    return (grad_values, grad_gain)


def contract_rows(left_side, right_side):
    return lax.dot_general(
        left_side, right_side, (((0,), (0,)), ((), ())), preferred_element_type=jnp.float32
    )


def contract_cols(left_side, right_side):
    return lax.dot_general(
        left_side, right_side, (((1,), (1,)), ((), ())), preferred_element_type=jnp.float32
    )


def gather(x, axes):
    return lax.all_gather(x, axes, axis=0, tiled=True)


def scatter_sum(x, axes):
    return lax.psum_scatter(x, axes, scatter_dimension=0, tiled=True)


def pad_lanes(x, lanes):
    return jnp.pad(x, ((0, 0), (0, lanes - x.shape[1])))


def dense_sum(x):
    rows, cols = x.shape
    groups, plane = lax.axis_size("a"), lax.axis_size(PLANE)
    own = rows // (groups * plane)
    x = x.reshape(groups, plane, own, cols).transpose(1, 0, 2, 3).reshape(rows, cols)
    return scatter_sum(scatter_sum(x, PLANE), "a").astype(jnp.float32)


def body(
    tokens,
    cotangent,
    segment_ids,
    routes,
    norm_attn,
    w_query,
    key_weight_matrix,
    value_weight_matrix,
    w_output,
    norm_moe,
    w_router,
    expert_in,
    expert_out,
):
    bf16 = jnp.bfloat16
    x_local = tokens[0].astype(jnp.float32)
    token_count, width = x_local.shape
    seg_row = segment_ids[0]
    row_length_local = seg_row.shape[0]
    query_group_width = QUERY_HEADS // KEY_VALUE_HEADS
    group = lax.axis_index("a")
    seq_index = lax.axis_index(SEQ)
    tok_start = seq_index * token_count
    positions = tok_start + jnp.arange(token_count, dtype=jnp.int32)
    seg_local = lax.dynamic_slice_in_dim(seg_row, tok_start, token_count)
    doc_start = jnp.sum((seg_row[None, :] < seg_local[:, None]).astype(jnp.int32), axis=1)
    rope_local = positions - doc_start

    qkv_width = 2 * QUERY_HEADS * HEAD_SIZE
    first_pack = jnp.concatenate(
        [
            w_query.astype(bf16),
            key_weight_matrix.astype(bf16),
            value_weight_matrix.astype(bf16),
            pad_lanes(norm_attn.astype(bf16)[:, None], 128),
        ],
        axis=1,
    )
    second_pack = jnp.concatenate(
        [
            w_output.astype(bf16),
            pad_lanes(
                jnp.concatenate([w_router.astype(bf16), norm_moe.astype(bf16)[:, None]], axis=1),
                128,
            ),
        ],
        axis=1,
    )
    first_all = gather(first_pack, ALL)
    second_all = gather(second_pack, ALL)
    qkv_w = first_all[:, :qkv_width]
    gain_one_f = first_all[:, qkv_width].astype(jnp.float32)
    output_w = second_all[:, :width]
    router_w = second_all[:, width : width + E]
    gain_two_f = second_all[:, width + E].astype(jnp.float32)

    normed_one = rms_scale(x_local, gain_one_f).astype(bf16)
    qkv_pre = jnp.dot(normed_one, qkv_w, preferred_element_type=jnp.float32)
    q_width = QUERY_HEADS * HEAD_SIZE
    kv_width = KEY_VALUE_HEADS * HEAD_SIZE
    cosine_table, sine_table = rope_tables(rope_local, HEAD_SIZE)
    rotated_query = apply_rotation_heads(
        qkv_pre[:, :q_width], cosine_table, sine_table, QUERY_HEADS
    ).astype(bf16)
    rotated_key = apply_rotation_heads(
        qkv_pre[:, q_width : q_width + kv_width], cosine_table, sine_table, KEY_VALUE_HEADS
    ).astype(bf16)
    value_reduced_precision = qkv_pre[:, q_width + kv_width :].astype(bf16)
    kv_all = gather(jnp.concatenate([rotated_key, value_reduced_precision], axis=1), SEQ)
    key_all, value_all = kv_all[:, :kv_width], kv_all[:, kv_width:]

    out_w = gather(expert_out.astype(bf16), PLANE).reshape(EXPERTS_HERE, width, F)
    in_w = gather(expert_in.astype(bf16), PLANE).reshape(EXPERTS_HERE, width, 2 * F)
    grad_all = gather(cotangent[0], "a")
    routes_all = gather(routes[0], "a")

    heads_of_queries = rotated_query.reshape(
        token_count, KEY_VALUE_HEADS, query_group_width, HEAD_SIZE
    )
    block_of_keys = math.gcd(row_length_local, 512)
    first_key = doc_start[0]
    lower_triangle_block = first_key // block_of_keys
    upper_triangle_block = (tok_start + token_count - 1) // block_of_keys + 1

    def block_scores(block_index):
        key_start = block_index * block_of_keys
        key_blk = lax.dynamic_slice_in_dim(key_all, key_start, block_of_keys).reshape(
            block_of_keys, KEY_VALUE_HEADS, HEAD_SIZE
        )
        value_blk = lax.dynamic_slice_in_dim(value_all, key_start, block_of_keys).reshape(
            block_of_keys, KEY_VALUE_HEADS, HEAD_SIZE
        )
        key_pos = key_start + jnp.arange(block_of_keys, dtype=jnp.int32)
        scores = (
            jnp.einsum(
                "tkgd,skd->kgts", heads_of_queries, key_blk, preferred_element_type=jnp.float32
            )
            * SCALE_OF_SCORES
        )
        allowed = (doc_start[:, None] <= key_pos[None, :]) & (
            positions[:, None] >= key_pos[None, :]
        )
        return (scores, allowed, key_blk, value_blk)

    def max_step(block_index, carried):
        running_max, running_sum = carried
        scores, allowed, _, _ = block_scores(block_index)
        masked = jnp.where(allowed, scores, NEGATIVE_HUGE)
        new_max = jnp.maximum(running_max, jnp.max(masked, axis=-1))
        fresh = jnp.sum(jnp.where(allowed, jnp.exp(masked - new_max[..., None]), 0.0), axis=-1)
        return (new_max, running_sum * jnp.exp(running_max - new_max) + fresh)

    initial_maximum = jnp.full(
        (KEY_VALUE_HEADS, query_group_width, token_count), NEGATIVE_HUGE, jnp.float32
    )
    initial_running_sum = jnp.zeros((KEY_VALUE_HEADS, query_group_width, token_count), jnp.float32)
    final_max, final_total = lax.fori_loop(
        lower_triangle_block, upper_triangle_block, max_step, (initial_maximum, initial_running_sum)
    )
    log_total = final_max + jnp.log(final_total)

    def mixing_update(block_index, mixed_sum):
        scores, allowed, _, value_blk = block_scores(block_index)
        probs_low = jnp.where(allowed, jnp.exp(scores - log_total[..., None]), 0.0).astype(
            bf16
        )
        return mixed_sum + jnp.einsum(
            "kgts,skd->tkgd", probs_low, value_blk, preferred_element_type=jnp.float32
        )

    attention_result = lax.fori_loop(
        lower_triangle_block,
        upper_triangle_block,
        mixing_update,
        jnp.zeros((token_count, KEY_VALUE_HEADS, query_group_width, HEAD_SIZE), jnp.float32),
    ).reshape(token_count, q_width)
    attended_low = attention_result.astype(bf16)
    attn_out = jnp.dot(attended_low, output_w, preferred_element_type=jnp.float32)
    resid = x_local + RESIDUAL_SCALE * attn_out
    normed_two = rms_scale(resid, gain_two_f).astype(bf16)

    normed_all = gather(normed_two, "a")
    expert_ids = jnp.arange(E, dtype=jnp.int32)
    routed = jnp.any(routes_all[:, :, None] == expert_ids[None, None, :], axis=1)
    logits = jnp.dot(normed_all, router_w, preferred_element_type=jnp.float32)
    top_logit = jnp.max(jnp.where(routed, logits, NEGATIVE_HUGE), axis=-1, keepdims=True)
    weights = jnp.where(routed, jnp.exp(jnp.minimum(logits - top_logit, 0.0)), 0.0)
    gates_all = weights / jnp.sum(weights, axis=-1, keepdims=True)
    gates_group = lax.dynamic_slice_in_dim(gates_all, group * EXPERTS_HERE, EXPERTS_HERE, 1)
    gate_cols = gates_group.T[:, :, None]

    grad_hidden = jnp.einsum(
        "td,edf->etf", grad_all, out_w, preferred_element_type=jnp.float32
    )
    pre_act = jnp.einsum("td,edf->etf", normed_all, in_w, preferred_element_type=jnp.float32)
    gate_pre = pre_act[..., :F]
    up_pre = pre_act[..., F:]
    gate_sig = jax.nn.sigmoid(gate_pre)
    gate_act = gate_pre * gate_sig
    hidden = gate_act * up_pre
    gated_hidden = (gate_cols * hidden).astype(bf16)
    grad_gates = RESIDUAL_SCALE * jnp.sum(
        hidden.astype(bf16).astype(jnp.float32) * grad_hidden, axis=-1
    )
    scaled_grad = (RESIDUAL_SCALE * gate_cols) * grad_hidden
    grad_gate = scaled_grad * up_pre * (gate_sig + gate_pre * gate_sig * (1.0 - gate_sig))
    grad_up = scaled_grad * gate_act
    grad_pre = jnp.concatenate([grad_gate, grad_up], axis=-1).astype(bf16)

    back_part = jnp.einsum("etf,edf->td", grad_pre, in_w, preferred_element_type=jnp.float32)
    gate_grads = jnp.zeros((gates_all.shape[0], E), jnp.float32)
    gate_grads = lax.dynamic_update_slice_in_dim(
        gate_grads, grad_gates.T, group * EXPERTS_HERE, 1
    )
    gate_high = gate_grads.astype(bf16)
    gate_low = (gate_grads - lax.reduce_precision(gate_grads, 8, 7)).astype(bf16)
    back_own = scatter_sum(
        jnp.concatenate(
            [back_part.astype(bf16), pad_lanes(jnp.concatenate([gate_high, gate_low], 1), 128)],
            axis=1,
        ),
        "a",
    ).astype(jnp.float32)
    moe_part = jnp.einsum("etf,edf->td", gated_hidden, out_w, preferred_element_type=jnp.float32)
    moe_sum = scatter_sum(moe_part.astype(bf16), "a").astype(jnp.float32)
    layer_sum = resid + RESIDUAL_SCALE * moe_sum

    grad_in_part = jnp.einsum("td,etf->edf", normed_all, grad_pre, preferred_element_type=jnp.float32)
    grad_out_part = RESIDUAL_SCALE * jnp.einsum(
        "td,etf->edf", grad_all, gated_hidden, preferred_element_type=jnp.float32
    )
    grad_expert_in = scatter_sum(
        grad_in_part.astype(bf16).reshape(EXPERTS_HERE * width, 2 * F), PLANE
    ).astype(jnp.float32)
    grad_expert_out = scatter_sum(
        grad_out_part.astype(bf16).reshape(EXPERTS_HERE * width, F), PLANE
    ).astype(jnp.float32)

    grad_out = cotangent[0].astype(jnp.float32)
    gates = lax.dynamic_slice_in_dim(gates_all, group * token_count, token_count)
    gate_grads_own = back_own[:, width : width + E] + back_own[:, width + E : width + 2 * E]
    grad_logits = gates * (
        gate_grads_own - jnp.sum(gates * gate_grads_own, axis=-1, keepdims=True)
    )
    grad_normed_two = back_own[:, :width] + jnp.dot(
        grad_logits, router_w.astype(jnp.float32).T, precision=HIGHEST_DOT
    )
    grad_router = jnp.dot(normed_two.astype(jnp.float32).T, grad_logits, precision=HIGHEST_DOT)
    grad_resid_norm, grad_gain_two = rms_back(resid, gain_two_f, grad_normed_two)
    grad_resid = grad_out + grad_resid_norm
    grad_attn_low = (RESIDUAL_SCALE * grad_resid).astype(bf16)
    grad_output_w = contract_rows(attended_low, grad_attn_low)
    second_sum = dense_sum(
        jnp.concatenate(
            [
                grad_output_w.astype(bf16),
                pad_lanes(
                    jnp.concatenate([grad_router, grad_gain_two[:, None]], axis=1), 128
                ).astype(bf16),
            ],
            axis=1,
        )
    )
    gradient_attention_lowered = contract_cols(grad_attn_low, output_w).astype(bf16)
    gradient_of_heads = gradient_attention_lowered.reshape(
        token_count, KEY_VALUE_HEADS, query_group_width, HEAD_SIZE
    )
    row_delta = jnp.sum(
        gradient_of_heads.astype(jnp.float32)
        * attention_result.reshape(token_count, KEY_VALUE_HEADS, query_group_width, HEAD_SIZE),
        axis=-1,
    )
    delta_heads = jnp.transpose(row_delta, (1, 2, 0))

    def back_step(block_index, carried):
        grad_query, grad_keys, grad_values = carried
        scores, allowed, key_blk, value_blk = block_scores(block_index)
        probs = jnp.where(allowed, jnp.exp(scores - log_total[..., None]), 0.0)
        probs_low = probs.astype(bf16)
        grad_probs = jnp.einsum(
            "tkgd,skd->kgts", gradient_of_heads, value_blk, preferred_element_type=jnp.float32
        )
        grad_scores = (probs * (grad_probs - delta_heads[..., None])).astype(bf16)
        grad_query = grad_query + jnp.einsum(
            "kgts,skd->tkgd", grad_scores, key_blk, preferred_element_type=jnp.float32
        )
        key_part = jnp.einsum(
            "kgts,tkgd->skd", grad_scores, heads_of_queries, preferred_element_type=jnp.float32
        ).reshape(block_of_keys, kv_width)
        value_part = jnp.einsum(
            "kgts,tkgd->skd", probs_low, gradient_of_heads, preferred_element_type=jnp.float32
        ).reshape(block_of_keys, kv_width)
        key_start = block_index * block_of_keys
        grad_keys = lax.dynamic_update_slice_in_dim(grad_keys, key_part, key_start, 0)
        grad_values = lax.dynamic_update_slice_in_dim(grad_values, value_part, key_start, 0)
        return (grad_query, grad_keys, grad_values)

    start_grads = (
        jnp.zeros((token_count, KEY_VALUE_HEADS, query_group_width, HEAD_SIZE), jnp.float32),
        jnp.zeros((row_length_local, kv_width), jnp.float32),
        jnp.zeros((row_length_local, kv_width), jnp.float32),
    )
    grad_query, grad_keys, grad_values = lax.fori_loop(
        lower_triangle_block, upper_triangle_block, back_step, start_grads
    )
    kv_own = scatter_sum(
        jnp.concatenate([grad_keys.astype(bf16), grad_values.astype(bf16)], axis=1), SEQ
    ).astype(jnp.float32)
    grad_query_pre = reverse_rotation_heads(
        grad_query.reshape(token_count, q_width) * SCALE_OF_SCORES,
        cosine_table,
        sine_table,
        QUERY_HEADS,
    ).astype(bf16)
    gradient_key_unrotated = reverse_rotation_heads(
        kv_own[:, :kv_width] * SCALE_OF_SCORES, cosine_table, sine_table, KEY_VALUE_HEADS
    ).astype(bf16)
    grad_value_pre = kv_own[:, kv_width:].astype(bf16)
    grad_qkv = jnp.concatenate([grad_query_pre, gradient_key_unrotated, grad_value_pre], axis=1)
    grad_qkv_w = contract_rows(normed_one, grad_qkv)
    grad_normed_one = contract_cols(grad_qkv, qkv_w)
    grad_x_norm, grad_gain_one = rms_back(x_local, gain_one_f, grad_normed_one)
    grad_input = grad_resid + grad_x_norm
    first_sum = dense_sum(
        jnp.concatenate(
            [grad_qkv_w.astype(bf16), pad_lanes(grad_gain_one[:, None], 128).astype(bf16)], axis=1
        )
    )
    return (
        layer_sum.astype(bf16)[None],
        grad_input[None],
        first_sum[:, qkv_width],
        first_sum[:, :q_width],
        first_sum[:, q_width : q_width + kv_width],
        first_sum[:, q_width + kv_width : qkv_width],
        second_sum[:, :width],
        second_sum[:, width + E],
        second_sum[:, width : width + E],
        grad_expert_in,
        grad_expert_out,
    )


def solution(mesh):
    seq, row = mesh.shape["seq"], mesh.shape["row"]
    cut = Mesh(mesh.devices.reshape(GROUPS, seq // GROUPS, row), ("a", "b", "row"))
    token_spec = P("row", SEQ, None)
    row_spec = P(ALL, None)
    flat_spec = P(ALL)
    in_specs = (
        token_spec,
        token_spec,
        P("row", None),
        token_spec,
        flat_spec,
        row_spec,
        row_spec,
        row_spec,
        row_spec,
        flat_spec,
        row_spec,
        row_spec,
        row_spec,
    )
    out_specs = (
        token_spec,
        token_spec,
        flat_spec,
        row_spec,
        row_spec,
        row_spec,
        row_spec,
        flat_spec,
        row_spec,
        row_spec,
        row_spec,
    )
    return jax.shard_map(body, mesh=cut, in_specs=in_specs, out_specs=out_specs, check_vma=False)
```

time: 2520 us -> 1040 us (0.41)
  waiting for transfers between devices: 1830 us -> 739 us
  matrix products: 236 us -> 123 us
  other arithmetic: 140 us -> 44.9 us
  local copies, waits for them, and re-layouts: 138 us -> 58.1 us
  blocking collectives: 119 us -> 42.8 us
    reduce_scatter x7 -> x9, waiting for transfers between devices: 1330 us -> 410 us  [scatter_sum(): return lax.psum_scatter(x, axes, scatter_dimension=0, tiled=True)]
    dot_general x68 -> x2, matrix products: 113 us -> 2.06 us  [contract_rows(): lax.dot_general(left_side, right_side, (((0,), (0,)), ((), ())), preferre...]
    all_gather x8 -> x7, waiting for transfers between devices: 412 us -> 328 us  [gather(): return lax.all_gather(x, axes, axis=0, tiled=True)]
    unnamed x17 -> x16, waiting for transfers between devices: 82.9 us -> 0.77 us
    unnamed x2 -> x0, blocking collectives: 79.1 us -> none
    gather x5 -> x0, local copies, waits for them, and re-layouts: 78.1 us -> none  [the longest x1 17.4 us: body(): gates_flat[pair_safe][:, None] * grad_moe[slot_token]]
    dynamic_update_slice x33 -> x1, other arithmetic: 65.1 us -> 0.02 us  [body(): lax.dynamic_update_slice_in_dim(gate_grads, grad_gates.T, group * EXPERTS...]
    dot_general x8 -> x9, matrix products: 92.9 us -> 95.4 us  [the longest x1 23.1 us: body(): jnp.einsum('etf,edf->td', grad_pre, in_w, preferred_element_type=jnp.floa...]
  transfers between devices with their start and end apart: 16 -> 16, of which waited for: 13 -> 16; matrix products, arithmetic and copies ran while one was open for 15% -> 12% of each run, Pallas kernels for 0% -> 0%
where the time goes in v1:
time: 1040 us; the launch traced here: 1030 us
  waiting for transfers between devices  739 us (71%)
  matrix products  123 us (12%)
  local copies, waits for them, and re-layouts  58.1 us (6%)
  other arithmetic  44.9 us (4%)
  blocking collectives  42.8 us (4%)
  between operations  17.6 us (2%)
    reduce_scatter x9, waiting for transfers between devices, scatter_sum(): return lax.psum_scatter(x, axes, scatter_dimension=0, tiled=True)  410 us
    all_gather x7, waiting for transfers between devices, gather(): return lax.all_gather(x, axes, axis=0, tiled=True)  328 us
    all_gather x1, blocking collectives, gather(): return lax.all_gather(x, axes, axis=0, tiled=True)  42.8 us
    dot_general x1, matrix products, body(): jnp.einsum('etf,edf->td', grad_pre, in_w, preferred_element_type=jnp.floa...  23.1 us
  transfers between devices with their start and end apart: 16, of which 16 were waited for; matrix products, arithmetic and copies ran while one was open for 12% of the time, Pallas kernels for 0%

profile of v1, /device:TPU:0, one launch (start us, length us, event | category | flops | bytes accessed | tf_op | source)
XLA Modules:
  0.0 1027.1 jit_solution(14977281171140766003)
XLA Ops:
  19.1 58.1 %all-gather.10.cloned.1.call-done = bf16[1024,2176]{1,0:T(8,128)(2,1)} async-done(((bf16[32,2176]{1,0:T(8,128)(2,1)}), bf16[1024,2176]{1,0:T(8,128)(2,1)}) %all-gather.10.cloned.1.call-update) | async-done | bytes 4456464 | tf_op jit(solution)/shard_map/all_gather | solution.py:83
  78.3 3.6 fusion.41
  87.7 48.6 %all-gather.14.cloned.1.call-done = bf16[1024,1152]{1,0:T(8,128)(2,1)} async-done(((bf16[32,1152]{1,0:T(8,128)(2,1)}), bf16[1024,1152]{1,0:T(8,128)(2,1)}) %all-gather.14.cloned.1.call-update) | async-done | bytes 2359312 | tf_op jit(solution)/shard_map/all_gather | solution.py:83
  139.3 72.0 %all-gather.12.cloned.1.call-done = bf16[2048,1024]{1,0:T(8,128)(2,1)} async-done(((bf16[256,1024]{1,0:T(8,128)(2,1)}), bf16[2048,1024]{1,0:T(8,128)(2,1)}) %all-gather.12.cloned.1.call-update) | async-done | bytes 4194320 | tf_op jit(solution)/shard_map/all_gather | solution.py:83
  211.3 4.5 fusion.97
  215.8 2.9 copy.206
  218.8 3.7 while.39
  220.4 2.0 select_reduce_fusion.3
  222.5 3.9 copy.205
  227.5 6.8 while.40
  227.5 1.9 constant_dynamic-slice_fusion.11
  229.6 4.7 fusion.156
  234.3 2.0 convert_element_type.210
  237.2 2.6 multiply_reduce_fusion.3
  241.9 2.9 convert_element_type.218
  246.4 42.8 %all-gather = s32[1,1024,8]{1,2,0:T(8,128)S(1)} all-gather(s32[1,256,8]{1,2,0:T(8,128)S(1)} %copy-done.20), channel_id=2, replica_groups=mesh['a'=4,'b'=2,'row'=4] {'a'}, dimensions={1}, use_global_device_ids=true | all-gather | bytes 40960 | tf_op jit(solution)/shard_map/all_gather | solution.py:83
  289.3 29.2 %all-gather.16.cloned.1.call-done = bf16[1024,1024]{0,1:T(8,128)(2,1)} async-done(((bf16[256,1024]{0,1:T(8,128)(2,1)}), bf16[1024,1024]{0,1:T(8,128)(2,1)}) %all-gather.16.cloned.1.call-update) | async-done | bytes 2097168 | tf_op jit(solution)/shard_map/all_gather | solution.py:83
  318.5 2.0 select_reduce_fusion.1
  320.6 51.9 %all-gather.18.cloned.1.call-done = bf16[4096,1024]{1,0:T(8,128)(2,1)} async-done(((bf16[512,1024]{1,0:T(8,128)(2,1)}), bf16[4096,1024]{1,0:T(8,128)(2,1)}) %all-gather.18.cloned.1.call-update) | async-done | bytes 8388624 | tf_op jit(solution)/shard_map/all_gather | solution.py:83
  372.6 16.1 %convolution_bitcast_fusion.1 = f32[4,1024,1024]{1,2,0:T(8,128)} fusion(bf16[4,1024,1024]{2,1,0:T(8,128)(2,1)} %bitcast.307, bf16[1024,1024]{0,1:T(8,128)(2,1)} %all-gather.16.cloned.1.call-done), kind=kOutput, calls=%fused_computation.49 | convolution fusion | flops 8589934592 | bytes 27262976 | tf_op jit(solution)/shard_map/td,edf->etf/dot_general | solution.py:257
  388.7 31.3 %all-gather.22.cloned.1.call-done = bf16[1,1024,1024]{2,1,0:T(8,128)(2,1)} async-done(((bf16[1,256,1024]{2,1,0:T(8,128)(2,1)}), bf16[1,1024,1024]{2,1,0:T(8,128)(2,1)}) %all-gather.22.cloned.1.call-update) | async-done | bytes 2097168 | tf_op jit(solution)/shard_map/all_gather | solution.py:83
  419.9 37.4 %all-gather.20.cloned.1.call-done = bf16[4096,512]{1,0:T(8,128)(2,1)} async-done(((bf16[512,512]{1,0:T(8,128)(2,1)}), bf16[4096,512]{1,0:T(8,128)(2,1)}) %all-gather.20.cloned.1.call-update) | async-done | bytes 4194320 | tf_op jit(solution)/shard_map/all_gather | solution.py:83
  457.3 15.5 %multiply_convert_fusion.2 = (bf16[4,1024,512]{1,2,0:T(8,128)(2,1)S(1)}, bf16[4,1024,512]{1,2,0:T(8,128)(2,1)}, f32[4,1024]{1,0:T(4,128)S(1)}, bf16[4,1024,512]{1,2,0:T(8,128)(2,1)}) fusion(f32[4,1024,1024]{1,2,0:T(8,128)} %convolution_bitcast_fusion.1, f32[4,1024]{1,0:T(4,128)S(1)} %get-tuple-element.561, f32[4,1024]{1,0:T(4,128)S(1)} %get-tuple-element.562, ...), kind=kOutput, calls=%fused_computation.56 | convolution fusion | flops 4336906240 | bytes 35700736 | tf_op jit(solution)/shard_map/td,edf->etf/dot_general | solution.py:254
  472.9 23.1 %bitcast_convert_fusion = bf16[1024,1024]{0,1:T(8,128)(2,1)S(1)} fusion(bf16[4,1024,1024]{2,1,0:T(8,128)(2,1)} %bitcast.308, bf16[4,1024,512]{1,2,0:T(8,128)(2,1)} %get-tuple-element.570, bf16[4,1024,512]{1,2,0:T(8,128)(2,1)S(1)} %get-tuple-element.569), kind=kOutput, calls=%fused_computation.66 | convolution fusion | flops 8607760384 | bytes 18874368 | tf_op jit(solution)/shard_map/etf,edf->td/dot_general | solution.py:272
  497.7 9.3 bitcast_convert_fusion.1
  507.3 38.5 %reduce-scatter.12.cloned.1.call-done = bf16[256,1152]{0,1:T(8,128)(2,1)} async-done(((bf16[1024,1152]{0,1:T(8,128)(2,1)}), bf16[256,1152]{0,1:T(8,128)(2,1)}) %reduce-scatter.12.cloned.1.call-update) | async-done | bytes 589840 | tf_op jit(solution)/shard_map/reduce_scatter | solution.py:87
  547.0 2.8 multiply_reduce_fusion
  549.9 41.7 %reduce-scatter.10.cloned.1.call-done = bf16[256,1024]{0,1:T(8,128)(2,1)} async-done(((bf16[1024,1024]{0,1:T(8,128)(2,1)}), bf16[256,1024]{0,1:T(8,128)(2,1)}) %reduce-scatter.10.cloned.1.call-update) | async-done | bytes 524304 | tf_op jit(solution)/shard_map/reduce_scatter | solution.py:87
  591.5 3.0 convert_add_fusion.1
  600.8 11.9 %while.41 = (s32[]{:T(128)}, f32[256,8,2,64]{0,3,2,1:T(8,128)S(1)}, bf16[2048,512]{0,1:T(8,128)(2,1)}, bf16[2048,512]{0,1:T(8,128)(2,1)}, s32[]{:T(128)}, /*inde...) while((s32[]{:T(128)}, f32[256,8,2,64]{0,3,2,1:T(8,128)S(1)}, ...), condition=%wide.region_19.20_spmd.clone, body=%wide.region_18.19_spmd.clone.sunk | while | flops 1363804928 | bytes 49208540 | solution.py:365
  604.5 2.9 fusion.168
  612.7 4.8 pad_maximum_fusion.3
  622.2 4.3 copy.224
  626.5 3.4 copy.225
  630.3 109.2 %reduce-scatter.14.cloned.1.call-done = bf16[256,1024]{0,1:T(8,128)(2,1)} async-done(((bf16[2048,1024]{0,1:T(8,128)(2,1)}), bf16[256,1024]{0,1:T(8,128)(2,1)}) %reduce-scatter.14.cloned.1.call-update) | async-done | bytes 524304 | tf_op jit(solution)/shard_map/reduce_scatter | solution.py:87
  741.6 4.5 fusion.69
  748.0 2.5 copy.223
  750.6 9.7 fusion.38
  760.3 6.2 copy.227
  766.6 18.6 %reduce-scatter.20.cloned.1.call-done = bf16[128,1152]{1,0:T(8,128)(2,1)} async-done(((bf16[1024,1152]{1,0:T(8,128)(2,1)}), bf16[128,1152]{1,0:T(8,128)(2,1)}) %reduce-scatter.20.cloned.1.call-update) | async-done | bytes 294928 | tf_op jit(solution)/shard_map/reduce_scatter | solution.py:87
  785.5 14.9 %convolution_convert_fusion = bf16[4,1024,1024]{1,2,0:T(8,128)(2,1)} fusion(bf16[4,1024,512]{1,2,0:T(8,128)(2,1)} %get-tuple-element.570, bf16[4,1024,512]{1,2,0:T(8,128)(2,1)} %copy-done.24, bf16[1024,1024]{0,1:T(8,128)(2,1)} %all-gather.16.cloned.1.call-done), kind=kOutput, calls=%fused_computation.61 | convolution fusion | flops 8610906112 | bytes 18874368 | tf_op jit(solution)/shard_map/td,etf->edf/dot_general | solution.py:290
  800.5 41.1 %reduce-scatter.16.cloned.1.call-done = bf16[128,2176]{1,0:T(8,128)(2,1)} async-done(((bf16[1024,2176]{1,0:T(8,128)(2,1)}), bf16[128,2176]{1,0:T(8,128)(2,1)}) %reduce-scatter.16.cloned.1.call-update) | async-done | bytes 557072 | tf_op jit(solution)/shard_map/reduce_scatter | solution.py:87
  842.6 53.6 %reduce-scatter.26.cloned.1.call-done = bf16[512,512]{1,0:T(8,128)(2,1)} async-done(((bf16[4096,512]{1,0:T(8,128)(2,1)}), bf16[512,512]{1,0:T(8,128)(2,1)}) %reduce-scatter.26.cloned.1.call-update) | async-done | bytes 524304 | tf_op jit(solution)/shard_map/reduce_scatter | solution.py:87
  896.2 2.1 convert_element_type.247
  898.4 20.0 %reduce-scatter.22.cloned.1.call-done = bf16[32,1152]{1,0:T(8,128)(2,1)} async-done(((bf16[128,1152]{1,0:T(8,128)(2,1)}), bf16[32,1152]{1,0:T(8,128)(2,1)}) %reduce-scatter.22.cloned.1.call-update) | async-done | bytes 73744 | tf_op jit(solution)/shard_map/reduce_scatter | solution.py:87
  922.8 68.8 %reduce-scatter.24.cloned.1.call-done = bf16[512,1024]{1,0:T(8,128)(2,1)} async-done(((bf16[4096,1024]{1,0:T(8,128)(2,1)}), bf16[512,1024]{1,0:T(8,128)(2,1)}) %reduce-scatter.24.cloned.1.call-update) | async-done | bytes 1048592 | tf_op jit(solution)/shard_map/reduce_scatter | solution.py:87
  991.7 2.8 convert_element_type.244
  997.3 18.4 %reduce-scatter.18.cloned.1.call-done = bf16[32,2176]{1,0:T(8,128)(2,1)} async-done(((bf16[128,2176]{1,0:T(8,128)(2,1)}), bf16[32,2176]{1,0:T(8,128)(2,1)}) %reduce-scatter.18.cloned.1.call-update) | async-done | bytes 139280 | tf_op jit(solution)/shard_map/reduce_scatter | solution.py:87
  (191 shorter events, 67.0 us)
Async XLA Ops:
  7.2 70.0 %all-gather.10.cloned.1.call-start = ((), (), s32[]{:S(2)}) async-start(), calls=%async_computation.9 | async-start | bytes 4595712 | tf_op jit(solution)/shard_map/all_gather | solution.py:83
  11.3 125.0 %all-gather.14.cloned.1.call-start = ((), (), s32[]{:S(2)}) async-start(), calls=%async_computation.11 | async-start | bytes 2433024 | tf_op jit(solution)/shard_map/all_gather | solution.py:83
  14.4 196.9 %all-gather.12.cloned.1.call-start = ((), (), s32[]{:S(2)}) async-start(), calls=%async_computation.10 | async-start | bytes 4718592 | tf_op jit(solution)/shard_map/all_gather | solution.py:83
  15.7 66.1 %copy-start.4 = (bf16[1,256,1024]{1,2,0:T(8,128)(2,1)}, bf16[1,256,1024]{1,2,0:T(8,128)(2,1)S(1)}, u32[]{:S(2)}) copy-start(bf16[1,256,1024]{1,2,0:T(8,128)(2,1)S(1)} %copy.199) | copy-start | bytes 1572868
  18.2 63.6 %copy-start.22 = (f32[256]{0:T(256)}, f32[256]{0:T(256)S(1)}, u32[]{:S(2)}) copy-start(f32[256]{0:T(256)S(1)} %get-tuple-element.593) | copy-start | bytes 3076
  19.1 120.1 %copy-start.14 = (f32[256,32]{0,1:T(8,128)}, f32[256,32]{0,1:T(8,128)S(1)}, u32[]{:S(2)}) copy-start(f32[256,32]{0,1:T(8,128)S(1)} %get-tuple-element.591) | copy-start | bytes 98308
  78.2 3.6 copy-start.18
  81.8 1.3 copy-start.11
  84.5 234.0 %all-gather.16.cloned.1.call-start = ((), (), s32[]{:S(2)}) async-start(), calls=%async_computation.12 | async-start | bytes 2621440 | tf_op jit(solution)/shard_map/all_gather | solution.py:83
  234.3 7.5 copy-start
  236.4 0.8 copy-start.7
  239.8 1.0 copy-start.2
  240.8 5.5 copy-start.20
  241.8 3.6 copy-start.13
  241.8 130.7 %all-gather.18.cloned.1.call-start = ((), (), s32[]{:S(2)}) async-start(), calls=%async_computation.13 | async-start | bytes 9437184 | tf_op jit(solution)/shard_map/all_gather | solution.py:83
  244.8 175.2 %all-gather.22.cloned.1.call-start = ((), (), s32[]{:S(2)}) async-start(), calls=%async_computation.24 | async-start | bytes 2621440 | tf_op jit(solution)/shard_map/all_gather | solution.py:83
  245.3 212.0 %all-gather.20.cloned.1.call-start = ((), (), s32[]{:S(2)}) async-start(), calls=%async_computation.14 | async-start | bytes 4718592 | tf_op jit(solution)/shard_map/all_gather | solution.py:83
  246.3 299.5 %reduce-scatter.12.cloned.1.call-start = ((), (), s32[]{:S(2)}) async-start(), calls=%async_computation.16 | async-start | bytes 2949120 | tf_op jit(solution)/shard_map/reduce_scatter | solution.py:87
  472.8 23.2 %copy-start.24 = (bf16[4,1024,512]{1,2,0:T(8,128)(2,1)}, bf16[4,1024,512]{1,2,0:T(8,128)(2,1)S(1)}, u32[]{:S(2)}) copy-start(bf16[4,1024,512]{1,2,0:T(8,128)(2,1)S(1)} %get-tuple-element.569) | copy-start | bytes 12582916
  497.6 93.9 %reduce-scatter.10.cloned.1.call-start = ((), (), s32[]{:S(2)}) async-start(), calls=%async_computation.15 | async-start | bytes 2621440 | tf_op jit(solution)/shard_map/reduce_scatter | solution.py:87
  497.7 9.4 copy-start.9
  507.0 40.0 %copy-start.3 = (f32[256,1024]{0,1:T(8,128)S(1)}, f32[256,1024]{0,1:T(8,128)}, u32[]{:S(2)}) copy-start(f32[256,1024]{0,1:T(8,128)} %copy-done.2) | copy-start | bytes 3145732
  507.0 232.5 %reduce-scatter.14.cloned.1.call-start = ((), (), s32[]{:S(2)}) async-start(), calls=%async_computation.17 | async-start | bytes 4718592 | tf_op jit(solution)/shard_map/reduce_scatter | solution.py:87
  547.0 2.9 copy-start.12
  591.5 3.0 copy-start.17
  591.5 5.8 copy-start.1
  617.5 1.0 copy-start.6
  617.5 2.3 copy-start.8
  617.5 167.6 %reduce-scatter.20.cloned.1.call-start = ((), (), s32[]{:S(2)}) async-start(), calls=%async_computation.20 | async-start | bytes 2654208 | tf_op jit(solution)/shard_map/reduce_scatter | solution.py:87
  626.5 3.6 copy-start.15
  626.5 3.6 copy-start.16
  629.9 111.7 %copy-start.5 = (bf16[1,256,1024]{1,2,0:T(8,128)(2,1)S(1)}, bf16[1,256,1024]{1,2,0:T(8,128)(2,1)}, u32[]{:S(2)}) copy-start(bf16[1,256,1024]{1,2,0:T(8,128)(2,1)} %copy-done.4) | copy-start | bytes 1572868
  629.9 111.7 %copy-start.19 = (f32[1024]{0:T(1024)S(1)}, f32[1024]{0:T(1024)}, u32[]{:S(2)}) copy-start(f32[1024]{0:T(1024)} %copy-done.18) | copy-start | bytes 12292
  629.9 111.7 %copy-start.23 = (f32[256]{0:T(256)S(1)}, f32[256]{0:T(256)}, u32[]{:S(2)}) copy-start(f32[256]{0:T(256)} %copy-done.22) | copy-start | bytes 3076
  629.9 211.6 %reduce-scatter.16.cloned.1.call-start = ((), (), s32[]{:S(2)}) async-start(), calls=%async_computation.18 | async-start | bytes 5013504 | tf_op jit(solution)/shard_map/reduce_scatter | solution.py:87
  750.5 145.7 %reduce-scatter.26.cloned.1.call-start = ((), (), s32[]{:S(2)}) async-start(), calls=%async_computation.23 | async-start | bytes 4718592 | tf_op jit(solution)/shard_map/reduce_scatter | solution.py:87
  766.5 151.8 %reduce-scatter.22.cloned.1.call-start = ((), (), s32[]{:S(2)}) async-start(), calls=%async_computation.21 | async-start | bytes 368640 | tf_op jit(solution)/shard_map/reduce_scatter | solution.py:87
  785.2 206.5 %reduce-scatter.24.cloned.1.call-start = ((), (), s32[]{:S(2)}) async-start(), calls=%async_computation.22 | async-start | bytes 9437184 | tf_op jit(solution)/shard_map/reduce_scatter | solution.py:87
  800.4 41.2 %copy-start.10 = (bf16[1,256,1024]{1,2,0:T(8,128)(2,1)S(1)}, bf16[1,256,1024]{1,2,0:T(8,128)(2,1)}, u32[]{:S(2)}) copy-start(bf16[1,256,1024]{1,2,0:T(8,128)(2,1)} %get-tuple-element.580) | copy-start | bytes 1572868
  800.4 194.1 %copy-start.21 = (f32[256]{0:T(256)S(1)}, f32[256]{0:T(256)}, u32[]{:S(2)}) copy-start(f32[256]{0:T(256)} %get-tuple-element.592) | copy-start | bytes 3076
  800.4 215.3 %reduce-scatter.18.cloned.1.call-start = ((), (), s32[]{:S(2)}) async-start(), calls=%async_computation.19 | async-start | bytes 696320 | tf_op jit(solution)/shard_map/reduce_scatter | solution.py:87
Sparse Core Ops, SparseCore 0:
  11.4 65.6 all-gather.9
  80.6 55.6 all-gather.13
  139.0 72.2 all-gather.11
  242.0 76.5 all-gather.15
  320.2 52.2 all-gather.17
  374.0 45.9 all-gather.21
  421.8 35.4 all-gather.19
  497.8 48.0 reduce-scatter.11
  548.1 43.3 reduce-scatter.9
  617.6 121.8 reduce-scatter.13
  742.9 42.2 reduce-scatter.19
  788.8 52.6 reduce-scatter.15
  844.9 51.2 reduce-scatter.25
  898.4 19.8 reduce-scatter.21
  922.1 69.5 reduce-scatter.23
  993.8 21.8 reduce-scatter.17

commit v2 on v1

v2 whole, which is shorter than its diff:
```python
import functools

import jax
import jax.numpy as jnp
from jax import lax
from jax.experimental import pallas as pl
from jax.experimental.pallas import tpu as pltpu
from jax.sharding import Mesh, PartitionSpec as P

QUERY_HEADS = 16
KEY_VALUE_HEADS = 8
HEAD_SIZE = 64
F = 512
E = 16
GROUPS = 4
EXPERTS_HERE = E // GROUPS
LANES = 128
PAIR = 2 * HEAD_SIZE
HEAD_PACK = 4 * HEAD_SIZE
BLOCK = 256

NORM_EPS = 1e-06
RESIDUAL_SCALE = 0.22
SCALE_OF_SCORES = 0.015625
ROPE_BASE = 10000.0
NEGATIVE_HUGE = -1e30
HIGHEST_DOT = lax.Precision.HIGHEST
VMEM_LIMIT = 60 * 1024 * 1024

PLANE = ("b", "y", "c")
SEQ = ("a", "b")
ALL = ("a", "b", "y", "c")

f32 = jnp.float32
bf16 = jnp.bfloat16


def rotation_tables(positions, with_values):
    half = HEAD_SIZE // 2
    freq = jnp.power(ROPE_BASE, -2.0 * jnp.arange(half, dtype=f32) / HEAD_SIZE)
    angle = positions.astype(f32)[:, None] * freq[None, :]
    cos, sin = jnp.cos(angle), jnp.sin(angle)
    cos, sin = jnp.concatenate([cos, cos], 1), jnp.concatenate([-sin, sin], 1)
    return (
        jnp.concatenate([cos, cos, cos, jnp.ones_like(cos)], 1),
        jnp.concatenate([sin, sin, sin, jnp.zeros_like(sin)], 1),
    )


def rms_back(values, gain, grad_norm):
    mean_square = jnp.mean(values * values, axis=-1, keepdims=True)
    inverse = lax.rsqrt(mean_square + NORM_EPS)
    scaled_grad = grad_norm * gain
    grad_values = inverse * scaled_grad - values * inverse**3 * jnp.mean(
        values * scaled_grad, axis=-1, keepdims=True
    )
    grad_gain = jnp.sum(grad_norm * values * inverse, axis=0)
    return (grad_values, grad_gain)


def rms_scale(values, gain):
    mean_square = jnp.mean(values * values, axis=-1, keepdims=True)
    return values * lax.rsqrt(mean_square + NORM_EPS) * gain


def contract_rows(left_side, right_side):
    return lax.dot_general(
        left_side, right_side, (((0,), (0,)), ((), ())), preferred_element_type=f32
    )


def contract_cols(left_side, right_side):
    return lax.dot_general(
        left_side, right_side, (((1,), (1,)), ((), ())), preferred_element_type=f32
    )


def gather(x, axes):
    return lax.all_gather(x, axes, axis=0, tiled=True)


def scatter_sum(x, axes):
    return lax.psum_scatter(x, axes, scatter_dimension=0, tiled=True)


def pad_lanes(x, lanes):
    return jnp.pad(x, ((0, 0), (0, lanes - x.shape[1])))


def chain_gather(x, axis):
    n, me = lax.axis_size(axis), lax.axis_index(axis)
    up = down = x
    ups, downs = [None], [None]
    for _ in range(n - 1):
        up = lax.ppermute(up, axis, [(i, i + 1) for i in range(n - 1)])
        down = lax.ppermute(down, axis, [(i + 1, i) for i in range(n - 1)])
        ups.append(up)
        downs.append(down)
    out = jnp.zeros((n,) + x.shape, x.dtype)
    out = lax.dynamic_update_index_in_dim(out, x, me, 0)
    for k in range(1, n):
        piece = jnp.where(me >= k, ups[k], downs[n - k])
        out = lax.dynamic_update_index_in_dim(out, piece, (me - k) % n, 0)
    return out.reshape((n * x.shape[0],) + x.shape[1:])


def halve(v, axis):
    if lax.axis_size(axis) != 2:
        return scatter_sum(v, axis)
    me = lax.axis_index(axis)
    v = v.reshape((2, v.shape[0] // 2) + v.shape[1:])
    other = lax.ppermute(lax.dynamic_index_in_dim(v, 1 - me, 0, False), axis, [(0, 1), (1, 0)])
    own = lax.dynamic_index_in_dim(v, me, 0, False)
    return (own.astype(f32) + other.astype(f32)).astype(v.dtype)


def line_sum(v, axis):
    n, me = lax.axis_size(axis), lax.axis_index(axis)
    v = v.reshape((n, v.shape[0] // n) + v.shape[1:])
    total = lax.dynamic_index_in_dim(v, me, 0, False).astype(f32)
    for k in range(n - 1, 0, -1):
        for step in (k, -k):
            pairs = [(i, i + step) for i in range(n) if 0 <= i + step < n]
            block = lax.dynamic_index_in_dim(v, jnp.clip(me + step, 0, n - 1), 0, False)
            total = total + lax.ppermute(block, axis, pairs).astype(f32)
    return total


def rows_for(x, order):
    sizes = tuple(lax.axis_size(axis) for axis in ALL)
    shape = sizes + (x.shape[0] // lax.axis_size(ALL),) + x.shape[1:]
    moved = [ALL.index(axis) for axis in order] + list(range(4, len(shape)))
    return x.reshape(shape).transpose(moved).reshape(x.shape)


def rotate_lanes(x, cos, sin):
    width = x.shape[-1]
    lane = lax.broadcasted_iota(jnp.int32, x.shape, x.ndim - 1)
    swapped = jnp.where(
        lane % HEAD_SIZE < HEAD_SIZE // 2,
        pltpu.roll(x, width - HEAD_SIZE // 2, x.ndim - 1),
        pltpu.roll(x, HEAD_SIZE // 2, x.ndim - 1),
    )
    return x * cos + swapped * sin


def project_kernel(x_ref, gain_ref, w_ref, cos_ref, sin_ref, qkv_ref, normed_ref):
    @pl.when(pl.program_id(0) == 0)
    def _():
        x = x_ref[...].astype(f32)
        gain = jnp.transpose(gain_ref[...].astype(f32))[0:1, :]
        normed_ref[...] = rms_scale(x, gain).astype(bf16)

    pre = jnp.dot(normed_ref[...], w_ref[...], preferred_element_type=f32)
    qkv_ref[0] = rotate_lanes(pre, cos_ref[...], sin_ref[...]).astype(bf16)


def project(x, packed, cos, sin):
    tokens, width = x.shape
    whole = pl.BlockSpec((tokens, width), lambda h: (0, 0))
    table = pl.BlockSpec((tokens, HEAD_PACK), lambda h: (0, 0))
    gain_at = KEY_VALUE_HEADS * HEAD_PACK // LANES
    return pl.pallas_call(
        project_kernel,
        grid=(KEY_VALUE_HEADS,),
        in_specs=[
            whole,
            pl.BlockSpec((width, LANES), lambda h: (0, gain_at)),
            pl.BlockSpec((width, HEAD_PACK), lambda h: (0, h)),
            table,
            table,
        ],
        out_specs=[pl.BlockSpec((1, tokens, HEAD_PACK), lambda h: (h, 0, 0)), whole],
        out_shape=[
            jax.ShapeDtypeStruct((KEY_VALUE_HEADS, tokens, HEAD_PACK), bf16),
            jax.ShapeDtypeStruct((tokens, width), bf16),
        ],
        compiler_params=pltpu.CompilerParams(vmem_limit_bytes=VMEM_LIMIT),
        cost_estimate=pl.CostEstimate(
            flops=2 * tokens * width * KEY_VALUE_HEADS * HEAD_PACK,
            bytes_accessed=6 * 2**20,
            transcendentals=0,
        ),
        name="project",
    )(x, packed, packed, cos, sin)


def lower_lanes(shape):
    return lax.broadcasted_iota(jnp.int32, shape, len(shape) - 1) < HEAD_SIZE


def both_heads_low(pair):
    low = lower_lanes(pair.shape)
    return jnp.concatenate(
        [jnp.where(low, pair, 0.0), jnp.where(low, pltpu.roll(pair, HEAD_SIZE, 1), 0.0)], axis=0
    )


def both_heads_high(pair):
    low = lower_lanes(pair.shape)
    return jnp.concatenate(
        [jnp.where(low, 0.0, pltpu.roll(pair, HEAD_SIZE, 1)), jnp.where(low, 0.0, pair)], axis=0
    )


def allowed_pairs(shape, query_start, key_start, doc):
    rows = lax.broadcasted_iota(jnp.int32, (shape[0] // 2, 1), 0) + query_start
    rows = jnp.concatenate([rows, rows], axis=0)
    keys = lax.broadcasted_iota(jnp.int32, shape, 1) + key_start
    return (keys >= jnp.concatenate([doc, doc], axis=0)) & (keys <= rows)


def attend_kernel(bounds_ref, q_ref, kv_ref, doc_ref, o_ref, low_ref, lse_ref, top, total, acc):
    i = pl.program_id(0)
    steps = pl.num_programs(0)
    offset = bounds_ref[steps]
    q = both_heads_low(q_ref[...].astype(f32) * SCALE_OF_SCORES).astype(bf16)
    doc = doc_ref[...]
    top[...] = jnp.full_like(top, NEGATIVE_HUGE)
    total[...] = jnp.zeros_like(total)
    acc[...] = jnp.zeros_like(acc)

    def step(j, carried):
        start = pl.multiple_of(j * BLOCK, BLOCK)
        kv = kv_ref[pl.ds(start, BLOCK), :]
        scores = contract_cols(q, kv)
        allowed = allowed_pairs(scores.shape, (i + offset) * BLOCK, j * BLOCK, doc)
        scores = jnp.where(allowed, scores, NEGATIVE_HUGE)
        old = top[...]
        new = jnp.maximum(old, jnp.max(scores, axis=1, keepdims=True))
        probs = jnp.exp(scores - new)
        keep = jnp.exp(old - new)
        top[...] = new
        total[...] = total[...] * keep + jnp.sum(probs, axis=1, keepdims=True)
        acc[...] = acc[...] * keep + jnp.dot(probs.astype(bf16), kv, preferred_element_type=f32)
        return carried

    lax.fori_loop(bounds_ref[i], i + offset + 1, step, 0)
    mixed = acc[...] / total[...]
    first, second = mixed[:BLOCK], mixed[BLOCK:]
    out = jnp.where(lower_lanes(first.shape), pltpu.roll(first, HEAD_SIZE, 1), second)
    o_ref[...] = out
    low_ref[...] = out.astype(bf16)
    lse_ref[0] = top[...] + jnp.log(total[...])


def attend(bounds, qkv, kv, kv_at, doc):
    queries, keys = qkv.shape[0], kv.shape[0]
    steps = queries // BLOCK
    pair = pl.BlockSpec((BLOCK, PAIR), lambda i, s: (i, 0))
    return pl.pallas_call(
        attend_kernel,
        grid_spec=pltpu.PrefetchScalarGridSpec(
            num_scalar_prefetch=1,
            grid=(steps,),
            in_specs=[
                pair,
                pl.BlockSpec((keys, PAIR), lambda i, s: (0, kv_at)),
                pl.BlockSpec((BLOCK, 1), lambda i, s: (i, 0)),
            ],
            out_specs=[pair, pair, pl.BlockSpec((1, 2 * BLOCK, 1), lambda i, s: (i, 0, 0))],
            scratch_shapes=[
                pltpu.VMEM((2 * BLOCK, 1), f32),
                pltpu.VMEM((2 * BLOCK, 1), f32),
                pltpu.VMEM((2 * BLOCK, PAIR), f32),
            ],
        ),
        out_shape=[
            jax.ShapeDtypeStruct((queries, PAIR), f32),
            jax.ShapeDtypeStruct((queries, PAIR), bf16),
            jax.ShapeDtypeStruct((steps, 2 * BLOCK, 1), f32),
        ],
        compiler_params=pltpu.CompilerParams(vmem_limit_bytes=VMEM_LIMIT),
        cost_estimate=pl.CostEstimate(
            flops=4 * queries * keys * PAIR, bytes_accessed=6 * 2**20, transcendentals=queries * keys
        ),
        name="attend",
    )(bounds, qkv, kv, doc)


def attend_back_kernel(
    bounds_ref, q_ref, kv_ref, doc_ref, do_ref, o_ref, lse_ref, dq_ref, dkv_ref, acc
):
    i = pl.program_id(0)
    steps = pl.num_programs(0)
    offset = bounds_ref[steps]

    @pl.when(i == 0)
    def _():
        dkv_ref[...] = jnp.zeros_like(dkv_ref)

    q = both_heads_low(q_ref[...].astype(f32) * SCALE_OF_SCORES).astype(bf16)
    grad = do_ref[...].astype(f32)
    product = grad * o_ref[...]
    low = lower_lanes(product.shape)
    delta = jnp.concatenate(
        [
            jnp.sum(jnp.where(low, product, 0.0), axis=1, keepdims=True),
            jnp.sum(jnp.where(low, 0.0, product), axis=1, keepdims=True),
        ],
        axis=0,
    )
    grad = both_heads_high(grad).astype(bf16)
    sources = jnp.concatenate([q, grad], axis=0)
    doc = doc_ref[...]
    lse = lse_ref[0]
    acc[...] = jnp.zeros_like(acc)

    def step(j, carried):
        start = pl.multiple_of(j * BLOCK, BLOCK)
        kv = kv_ref[pl.ds(start, BLOCK), :]
        scores = contract_cols(q, kv)
        allowed = allowed_pairs(scores.shape, (i + offset) * BLOCK, j * BLOCK, doc)
        probs = jnp.exp(jnp.where(allowed, scores - lse, NEGATIVE_HUGE))
        grad_probs = contract_cols(grad, kv)
        grad_scores = (probs * (grad_probs - delta)).astype(bf16)
        acc[...] += jnp.dot(grad_scores, kv, preferred_element_type=f32)
        both = jnp.concatenate([grad_scores, probs.astype(bf16)], axis=0)
        dkv_ref[pl.ds(start, BLOCK), :] += contract_rows(both, sources)
        return carried

    lax.fori_loop(bounds_ref[i], i + offset + 1, step, 0)
    first, second = acc[:BLOCK], acc[BLOCK:]
    dq_ref[...] = jnp.where(lower_lanes(first.shape), first, pltpu.roll(second, HEAD_SIZE, 1))


def attend_back(bounds, qkv, kv, kv_at, doc, grad, out, lse):
    queries, keys = qkv.shape[0], kv.shape[0]
    steps = queries // BLOCK
    pair = pl.BlockSpec((BLOCK, PAIR), lambda i, s: (i, 0))
    return pl.pallas_call(
        attend_back_kernel,
        grid_spec=pltpu.PrefetchScalarGridSpec(
            num_scalar_prefetch=1,
            grid=(steps,),
            in_specs=[
                pair,
                pl.BlockSpec((keys, PAIR), lambda i, s: (0, kv_at)),
                pl.BlockSpec((BLOCK, 1), lambda i, s: (i, 0)),
                pair,
                pair,
                pl.BlockSpec((1, 2 * BLOCK, 1), lambda i, s: (i, 0, 0)),
            ],
            out_specs=[pair, pl.BlockSpec((keys, PAIR), lambda i, s: (0, 0))],
            scratch_shapes=[pltpu.VMEM((2 * BLOCK, PAIR), f32)],
        ),
        out_shape=[
            jax.ShapeDtypeStruct((queries, PAIR), f32),
            jax.ShapeDtypeStruct((keys, PAIR), f32),
        ],
        compiler_params=pltpu.CompilerParams(vmem_limit_bytes=VMEM_LIMIT),
        cost_estimate=pl.CostEstimate(
            flops=10 * queries * keys * PAIR,
            bytes_accessed=8 * 2**20,
            transcendentals=queries * keys,
        ),
        name="attend_back",
    )(bounds, qkv, kv, doc, grad, out, lse)


def unrotate_kernel(dq_ref, dkv_ref, cos_ref, sin_ref, out_ref):
    cos, sin = cos_ref[...], sin_ref[...]
    dq = rotate_lanes(dq_ref[...] * SCALE_OF_SCORES, cos[:, :PAIR], -sin[:, :PAIR])
    dkv = rotate_lanes(dkv_ref[...], cos[:, PAIR:], -sin[:, PAIR:])
    out_ref[...] = jnp.concatenate([dq, dkv], axis=1).astype(bf16)


def unrotate(dq, dkv, cos, sin):
    rows = dq.shape[0]
    pair = pl.BlockSpec((2 * BLOCK, PAIR), lambda i: (i, 0))
    pack = pl.BlockSpec((2 * BLOCK, HEAD_PACK), lambda i: (i, 0))
    return pl.pallas_call(
        unrotate_kernel,
        grid=(rows // (2 * BLOCK),),
        in_specs=[pair, pair, pack, pack],
        out_specs=pack,
        out_shape=jax.ShapeDtypeStruct((rows, HEAD_PACK), bf16),
        cost_estimate=pl.CostEstimate(
            flops=rows * HEAD_PACK * 8, bytes_accessed=rows * HEAD_PACK * 14, transcendentals=0
        ),
        name="unrotate",
    )(dq, dkv, cos, sin)


def exchange(x, axes):
    return lax.all_to_all(x, axes, 0, 0, tiled=True)


def body(
    tokens,
    cotangent,
    segment_ids,
    routes,
    norm_attn,
    w_query,
    key_weight_matrix,
    value_weight_matrix,
    w_output,
    norm_moe,
    w_router,
    expert_in,
    expert_out,
):
    x_local = tokens[0].astype(f32)
    token_count, width = x_local.shape
    seg_row = segment_ids[0]
    group = lax.axis_index("a")
    head_axes = SEQ if lax.axis_size(SEQ) == KEY_VALUE_HEADS else ("b",)
    whole_rows = head_axes == SEQ
    span = token_count * KEY_VALUE_HEADS
    span_start = 0 if whole_rows else group * span
    tok_start = lax.axis_index(SEQ) * token_count

    def start_of_doc(ids):
        return jnp.sum((seg_row[None, :] < ids[:, None]).astype(jnp.int32), axis=1)

    seg_local = lax.dynamic_slice_in_dim(seg_row, tok_start, token_count)
    rope_local = tok_start + jnp.arange(token_count, dtype=jnp.int32) - start_of_doc(seg_local)
    cos_local, sin_local = rotation_tables(rope_local, True)
    seg_span = lax.dynamic_slice_in_dim(seg_row, span_start, span)
    doc_span = start_of_doc(seg_span)
    cos_span, sin_span = rotation_tables(
        span_start + jnp.arange(span, dtype=jnp.int32) - doc_span, True
    )
    bounds = jnp.concatenate(
        [
            doc_span.reshape(-1, BLOCK)[:, 0] // BLOCK,
            jnp.full((1,), span_start // BLOCK, jnp.int32),
        ]
    )
    doc_column = doc_span[:, None]

    own_rows = w_query.shape[0]
    by_head = jnp.concatenate(
        [
            w_query.astype(bf16).reshape(own_rows, KEY_VALUE_HEADS, PAIR),
            key_weight_matrix.astype(bf16).reshape(own_rows, KEY_VALUE_HEADS, HEAD_SIZE),
            value_weight_matrix.astype(bf16).reshape(own_rows, KEY_VALUE_HEADS, HEAD_SIZE),
        ],
        axis=2,
    ).reshape(own_rows, KEY_VALUE_HEADS * HEAD_PACK)
    qkv_width = KEY_VALUE_HEADS * HEAD_PACK
    first_all = gather(
        jnp.concatenate([by_head, pad_lanes(norm_attn.astype(bf16)[:, None], LANES)], axis=1), ALL
    )
    second_all = gather(
        jnp.concatenate(
            [
                w_output.astype(bf16),
                pad_lanes(
                    jnp.concatenate([w_router.astype(bf16), norm_moe.astype(bf16)[:, None]], axis=1),
                    LANES,
                ),
            ],
            axis=1,
        ),
        ALL,
    )
    experts_low = jnp.concatenate([expert_in.astype(bf16), expert_out.astype(bf16)], axis=1)
    experts_all = gather(experts_low, PLANE).reshape(EXPERTS_HERE, width, 3 * F)
    in_w, out_w = experts_all[:, :, : 2 * F], experts_all[:, :, 2 * F :]
    output_w = second_all[:, :width]
    router_w = second_all[:, width : width + E]
    gain_two_f = second_all[:, width + E].astype(f32)
    gain_one_f = first_all[:, qkv_width].astype(f32)

    expert_ids = jnp.arange(E, dtype=jnp.int32)
    routed_own = jnp.any(routes[0][:, :, None] == expert_ids[None, None, :], axis=1)
    early_all = chain_gather(
        jnp.concatenate([cotangent[0], pad_lanes(routed_own.astype(bf16), LANES)], axis=1), "a"
    )
    grad_all = early_all[:, :width]
    routed = early_all[:, width : width + E] > 0.5

    by_heads, normed_one = project(tokens[0], first_all, cos_local, sin_local)
    qkv = exchange(by_heads, head_axes).reshape(span, HEAD_PACK)
    if whole_rows:
        kv, kv_at = qkv, 1
    else:
        kv, kv_at = gather(qkv[:, PAIR:], "a"), 0
    attention_result, attended, log_total = attend(bounds, qkv, kv, kv_at, doc_column)
    attended_low = (
        exchange(attended.reshape(KEY_VALUE_HEADS, token_count, PAIR), head_axes)
        .transpose(1, 0, 2)
        .reshape(token_count, QUERY_HEADS * HEAD_SIZE)
    )
    attn_out = jnp.dot(attended_low, output_w, preferred_element_type=f32)
    resid = x_local + RESIDUAL_SCALE * attn_out
    normed_two = rms_scale(resid, gain_two_f).astype(bf16)

    normed_all = gather(normed_two, "a")
    logits = jnp.dot(normed_all, router_w, preferred_element_type=f32)
    top_logit = jnp.max(jnp.where(routed, logits, NEGATIVE_HUGE), axis=-1, keepdims=True)
    weights = jnp.where(routed, jnp.exp(jnp.minimum(logits - top_logit, 0.0)), 0.0)
    gates_all = weights / jnp.sum(weights, axis=-1, keepdims=True)
    gates_group = lax.dynamic_slice_in_dim(gates_all, group * EXPERTS_HERE, EXPERTS_HERE, 1)
    gate_cols = gates_group.T[:, :, None]

    grad_hidden = jnp.einsum("td,edf->etf", grad_all, out_w, preferred_element_type=f32)
    pre_act = jnp.einsum("td,edf->etf", normed_all, in_w, preferred_element_type=f32)
    gate_pre = pre_act[..., :F]
    up_pre = pre_act[..., F:]
    gate_sig = jax.nn.sigmoid(gate_pre)
    gate_act = gate_pre * gate_sig
    hidden = gate_act * up_pre
    gated_hidden = (gate_cols * hidden).astype(bf16)
    grad_gates = RESIDUAL_SCALE * jnp.sum(hidden.astype(bf16).astype(f32) * grad_hidden, axis=-1)
    scaled_grad = (RESIDUAL_SCALE * gate_cols) * grad_hidden
    grad_gate = scaled_grad * up_pre * (gate_sig + gate_pre * gate_sig * (1.0 - gate_sig))
    grad_up = scaled_grad * gate_act
    grad_pre = jnp.concatenate([grad_gate, grad_up], axis=-1).astype(bf16)

    back_part = jnp.einsum("etf,edf->td", grad_pre, in_w, preferred_element_type=f32)
    gate_grads = jnp.zeros((gates_all.shape[0], E), f32)
    gate_grads = lax.dynamic_update_slice_in_dim(gate_grads, grad_gates.T, group * EXPERTS_HERE, 1)
    gate_high = gate_grads.astype(bf16)
    gate_low = (gate_grads - lax.reduce_precision(gate_grads, 8, 7)).astype(bf16)
    back_own = scatter_sum(
        jnp.concatenate(
            [back_part.astype(bf16), pad_lanes(jnp.concatenate([gate_high, gate_low], 1), LANES)],
            axis=1,
        ),
        "a",
    ).astype(f32)

    grad_in_part = jnp.einsum("td,etf->edf", normed_all, grad_pre, preferred_element_type=f32)
    grad_out_part = RESIDUAL_SCALE * jnp.einsum(
        "td,etf->edf", grad_all, gated_hidden, preferred_element_type=f32
    )
    grad_experts = scatter_sum(
        jnp.concatenate([grad_in_part.astype(bf16), grad_out_part.astype(bf16)], axis=2).reshape(
            EXPERTS_HERE * width, 3 * F
        ),
        PLANE,
    ).astype(f32)
    moe_part = jnp.einsum("etf,edf->td", gated_hidden, out_w, preferred_element_type=f32)
    moe_sum = scatter_sum(moe_part.astype(bf16), "a").astype(f32)
    layer_sum = resid + RESIDUAL_SCALE * moe_sum

    grad_out = cotangent[0].astype(f32)
    gates = lax.dynamic_slice_in_dim(gates_all, group * token_count, token_count)
    gate_grads_own = back_own[:, width : width + E] + back_own[:, width + E : width + 2 * E]
    grad_logits = gates * (gate_grads_own - jnp.sum(gates * gate_grads_own, axis=-1, keepdims=True))
    grad_normed_two = back_own[:, :width] + jnp.dot(
        grad_logits, router_w.astype(f32).T, precision=HIGHEST_DOT
    )
    grad_router = jnp.dot(normed_two.astype(f32).T, grad_logits, precision=HIGHEST_DOT)
    grad_resid_norm, grad_gain_two = rms_back(resid, gain_two_f, grad_normed_two)
    grad_resid = grad_out + grad_resid_norm
    grad_attn_low = (RESIDUAL_SCALE * grad_resid).astype(bf16)
    grad_heads = contract_cols(grad_attn_low, output_w).astype(bf16)
    grad_mixed = exchange(
        grad_heads.reshape(token_count, KEY_VALUE_HEADS, PAIR).transpose(1, 0, 2), head_axes
    ).reshape(span, PAIR)
    grad_q, grad_kv = attend_back(
        bounds, qkv, kv, kv_at, doc_column, grad_mixed, attention_result, log_total
    )
    if not whole_rows:
        grad_kv = scatter_sum(grad_kv.astype(bf16), "a").astype(f32)
    grad_qkv = (
        exchange(
            unrotate(grad_q, grad_kv, cos_span, sin_span).reshape(
                KEY_VALUE_HEADS, token_count, HEAD_PACK
            ),
            head_axes,
        )
        .transpose(1, 0, 2)
        .reshape(token_count, qkv_width)
    )
    grad_normed_one = contract_cols(grad_qkv, first_all[:, :qkv_width])
    grad_x_norm, grad_gain_one = rms_back(x_local, gain_one_f, grad_normed_one)
    grad_input = grad_resid + grad_x_norm

    orders = (("c", "y", "b", "a"), ("c", "b", "y", "a"))
    cut = 3 * qkv_width // 4
    small = jnp.concatenate([grad_router, grad_gain_one[:, None], grad_gain_two[:, None]], axis=1)

    def weight_rows(acts, grads, order):
        return contract_rows(acts, grads).astype(bf16)

    left = jnp.concatenate(
        [
            rows_for(contract_rows(normed_one, grad_qkv[:, :cut]).astype(bf16), orders[0]),
            rows_for(pad_lanes(small, LANES).astype(bf16), orders[0]),
        ],
        axis=1,
    )
    right = jnp.concatenate(
        [
            rows_for(contract_rows(normed_one, grad_qkv[:, cut:]).astype(bf16), orders[1]),
            rows_for(contract_rows(attended_low, grad_attn_low).astype(bf16), orders[1]),
        ],
        axis=1,
    )
    left, right = halve(left, "c"), halve(right, "c")
    left, right = halve(left, "y"), halve(right, "b")
    left, right = halve(left, "b"), halve(right, "y")
    total = line_sum(jnp.concatenate([left, right], axis=1), "a")
    small_sum = total[:, cut : cut + LANES]
    qkv_sum = jnp.concatenate(
        [total[:, :cut], total[:, cut + LANES : qkv_width + LANES]], axis=1
    ).reshape(own_rows, KEY_VALUE_HEADS, HEAD_PACK)
    return (
        layer_sum.astype(bf16)[None],
        grad_input[None],
        small_sum[:, E],
        qkv_sum[:, :, :PAIR].reshape(own_rows, -1),
        qkv_sum[:, :, PAIR : PAIR + HEAD_SIZE].reshape(own_rows, -1),
        qkv_sum[:, :, PAIR + HEAD_SIZE :].reshape(own_rows, -1),
        total[:, qkv_width + LANES :],
        small_sum[:, E + 1],
        small_sum[:, :E],
        grad_experts[:, : 2 * F],
        grad_experts[:, 2 * F :],
    )


def solution(mesh):
    seq, row = mesh.shape["seq"], mesh.shape["row"]
    cut = Mesh(mesh.devices.reshape(GROUPS, seq // GROUPS, row // 2, 2), ALL)
    token_spec = P(("y", "c"), SEQ, None)
    row_spec = P(ALL, None)
    flat_spec = P(ALL)
    in_specs = (
        token_spec,
        token_spec,
        P(("y", "c"), None),
        token_spec,
        flat_spec,
        row_spec,
        row_spec,
        row_spec,
        row_spec,
        flat_spec,
        row_spec,
        row_spec,
        row_spec,
    )
    out_specs = (
        token_spec,
        token_spec,
        flat_spec,
        row_spec,
        row_spec,
        row_spec,
        row_spec,
        flat_spec,
        row_spec,
        row_spec,
        row_spec,
    )
    return jax.shard_map(body, mesh=cut, in_specs=in_specs, out_specs=out_specs, check_vma=False)
```

time: 1040 us -> 663 us (0.64)
  waiting for transfers between devices: 739 us -> 286 us
  Pallas kernels: 0 us -> 81.3 us
  starting transfers between devices: 0.91 us -> 62.5 us
  blocking collectives: 42.8 us -> 0 us
  matrix products: 123 us -> 90.5 us
  other arithmetic: 44.9 us -> 57.6 us
    reduce_scatter x9 -> x3, waiting for transfers between devices: 410 us -> 31.8 us  [scatter_sum(): return lax.psum_scatter(x, axes, scatter_dimension=0, tiled=True)]
    all_gather x7 -> x4, waiting for transfers between devices: 328 us -> 109 us  [gather(): return lax.all_gather(x, axes, axis=0, tiled=True)]
    ppermute x0 -> x18, waiting for transfers between devices: none -> 84.1 us  [the longest x3 55.4 us: chain_gather(): down = lax.ppermute(down, axis, [(i + 1, i) for i in range(n - 1)])]
    pallas_call x0 -> x4, Pallas kernels: none -> 81.3 us  [the longest x1 42 us: attend(): pl.pallas_call(attend_kernel, grid_spec=pltpu.PrefetchScalarGridSpec(num_...]
    all_to_all x0 -> x4, waiting for transfers between devices: none -> 61.4 us  [exchange(): return lax.all_to_all(x, axes, 0, 0, tiled=True)]
    ppermute x0 -> x18, starting transfers between devices: none -> 44.2 us  [the longest x6 20.3 us: line_sum(): total = total + lax.ppermute(block, axis, pairs).astype(f32)]
    all_gather x1 -> x0, blocking collectives: 42.8 us -> none  [gather(): return lax.all_gather(x, axes, axis=0, tiled=True)]
    dot_general x17 -> x9, matrix products: 105 us -> 76.4 us  [the longest x1 16.4 us: body(): jnp.einsum('td,edf->etf', normed_all, in_w, preferred_element_type=f32)]
  transfers between devices with their start and end apart: 16 -> 29, of which waited for: 16 -> 16; matrix products, arithmetic and copies ran while one was open for 12% -> 21% of each run, Pallas kernels for 0% -> 12%
where the time goes in v2:
time: 663 us; the launch traced here: 653 us
  waiting for transfers between devices  286 us (43%)
  matrix products  90.5 us (14%)
  Pallas kernels  81.3 us (12%)
  starting transfers between devices  62.5 us (9%)
  local copies, waits for them, and re-layouts  60 us (9%)
  other arithmetic  57.6 us (9%)
  between operations  15.5 us (2%)
    all_gather x4, waiting for transfers between devices, gather(): return lax.all_gather(x, axes, axis=0, tiled=True)  109 us
    all_to_all x4, waiting for transfers between devices, exchange(): return lax.all_to_all(x, axes, 0, 0, tiled=True)  61.4 us
    ppermute x3, waiting for transfers between devices, chain_gather(): down = lax.ppermute(down, axis, [(i + 1, i) for i in range(n - 1)])  55.4 us
    pallas_call x1, Pallas kernels, attend(): pl.pallas_call(attend_kernel, grid_spec=pltpu.PrefetchScalarGridSpec(num_...  42 us
    reduce_scatter x3, waiting for transfers between devices, scatter_sum(): return lax.psum_scatter(x, axes, scatter_dimension=0, tiled=True)  31.8 us
    pallas_call x1, Pallas kernels, attend_back(): pl.pallas_call(attend_back_kernel, grid_spec=pltpu.PrefetchScalarGridSpec...  26 us
    ppermute x6, waiting for transfers between devices, halve(): lax.ppermute(lax.dynamic_index_in_dim(v, 1 - me, 0, False), axis, [(0, 1)...  25.8 us
    ppermute x6, starting transfers between devices, line_sum(): total = total + lax.ppermute(block, axis, pairs).astype(f32)  20.3 us
  transfers between devices with their start and end apart: 29, of which 16 were waited for; matrix products, arithmetic and copies ran while one was open for 21% of the time, Pallas kernels for 12%

profile of v2, /device:TPU:0, one launch (start us, length us, event | category | flops | bytes accessed | tf_op | source)
XLA Modules:
  0.0 653.4 jit_solution(7862058317100874607)
XLA Ops:
  19.0 58.5 %all-gather.5.cloned.1.call-done.gain_ref.w_ref = bf16[1024,2176]{1,0:T(8,128)(2,1)} async-done(((bf16[32,2176]{1,0:T(8,128)(2,1)}), bf16[1024,2176]{1,0:T(8,128)(2,1)}) %all-gather.5.cloned.1.call-update) | async-done | bytes 4456464 | tf_op jit(solution)/shard_map/all_gather | solution.py:79
  77.5 8.2 %project.1 = (bf16[8,256,256]{2,1,0:T(8,128)(2,1)}, bf16[256,1024]{1,0:T(8,128)(2,1)}) custom-call(bf16[256,1024]{1,0:T(8,128)(2,1)} %bitcast.192, bf16[1024,2176]{1,0:T(8,128)(2,1)} %all-gather.5.cloned.1.call-done.gain_ref.w_ref, bf16[1024,2176]{1,0:T(8,128)(2,1)} %all-gather.5.cloned.1.call-done.gain_ref.w_ref, f32[256,256]{1,0:T(8,128)} %concatenate.83.cos_ref, ...), custom_call_target="tpu_custom_call" | custom-call | flops 1073741824 | bytes 6291456 | tf_op jit(solution)/shard_map/project/pallas_call | solution.py:163
  85.7 3.8 all-to-all-start
  93.4 25.3 %all-to-all-done = bf16[8,256,256]{2,1,0:T(8,128)(2,1)S(1)} async-done(((bf16[8,256,256]{2,1,0:T(8,128)(2,1)}), bf16[8,256,256]{2,1,0:T(8,128)(2,1)S(1)}, u32[]{:S(2)}, u32[]{:S(2)}) %all-to-all-start) | async-done | bytes 1048608 | tf_op jit(solution)/shard_map/all_to_all | solution.py:386
  119.6 42.0 %attend.1 = (f32[2048,128]{1,0:T(8,128)}, bf16[2048,128]{1,0:T(8,128)(2,1)}, f32[8,512,1]{2,1,0:T(8,128)}) custom-call(s32[9]{0:T(128)} %pad_add_fusion.bounds_ref, bf16[2048,256]{1,0:T(8,128)(2,1)} %bitcast.212, bf16[2048,256]{1,0:T(8,128)(2,1)} %bitcast.213, s32[2048,1]{1,0:T(8,128)} %copy.150.doc_ref), custom_call_target="tpu_custom_call" | custom-call | flops 2147483648 | bytes 6291456 | tf_op jit(solution)/shard_map/attend/pallas_call | solution.py:251
  161.6 2.0 copy.151
  163.6 3.6 all-to-all-start.1
  168.5 13.3 %all-to-all-done.1 = bf16[8,256,128]{1,2,0:T(8,128)(2,1)S(1)} async-done(((bf16[8,256,128]{1,2,0:T(8,128)(2,1)}), bf16[8,256,128]{1,2,0:T(8,128)(2,1)S(1)}, u32[]{:S(2)}, u32[]{:S(2)}) %all-to-all-start.1) | async-done | bytes 524320 | tf_op jit(solution)/shard_map/all_to_all | solution.py:386
  181.8 2.7 multiply_reduce_fusion.2
  190.3 4.6 collective-permute-start
  194.9 38.2 %collective-permute-done.1 = bf16[256,1152]{1,0:T(8,128)(2,1)S(1)} collective-permute-done((bf16[256,1152]{1,0:T(8,128)(2,1)S(1)}, bf16[256,1152]{1,0:T(8,128)(2,1)S(1)}, u32[]{:S(2)}, u32[]{:S(2)}) %collective-permute-start.1) | collective-permute-done | bytes 589856 | tf_op jit(solution)/shard_map/ppermute | solution.py:96
  234.4 5.4 collective-permute-start.4
  239.8 11.2 %collective-permute-done.2 = bf16[256,1152]{1,0:T(8,128)(2,1)S(1)} collective-permute-done((bf16[256,1152]{1,0:T(8,128)(2,1)S(1)}, bf16[256,1152]{1,0:T(8,128)(2,1)S(1)}, u32[]{:S(2)}, u32[]{:S(2)}) %collective-permute-start.2) | collective-permute-done | bytes 589856 | tf_op jit(solution)/shard_map/ppermute | solution.py:96
  254.8 4.6 collective-permute-start.5
  259.4 6.0 collective-permute-done.3
  265.4 2.0 bitcast_dynamic-update-slice_fusion.2
  270.2 2.5 select_reduce_fusion
  275.9 50.2 %all-gather.11.cloned.1.call-done = bf16[4096,1536]{1,0:T(8,128)(2,1)} async-done(((bf16[512,1536]{1,0:T(8,128)(2,1)}), bf16[4096,1536]{1,0:T(8,128)(2,1)}) %all-gather.11.cloned.1.call-update) | async-done | bytes 12582928 | tf_op jit(solution)/shard_map/all_gather | solution.py:79
  326.2 16.4 %convolution_bitcast_fusion = f32[4,1024,1024]{1,2,0:T(8,128)} fusion(bf16[4,1024,1536]{2,1,0:T(8,128)(2,1)} %bitcast.228, bf16[1024,1024]{1,0:T(8,128)(2,1)} %all-gather.9.cloned.1.call-done), kind=kOutput, calls=%fused_computation.2 | convolution fusion | flops 8589934592 | bytes 27262976 | tf_op jit(solution)/shard_map/td,edf->etf/dot_general | solution.py:500
  342.6 16.1 %multiply_convert_fusion.2 = (bf16[4,1024,512]{1,2,0:T(8,128)(2,1)}, bf16[4,1024,512]{1,2,0:T(8,128)(2,1)}, f32[4,1024]{1,0:T(4,128)S(1)}, bf16[4,1024,512]{1,2,0:T(8,128)(2,1)}) fusion(f32[4,1024,1024]{1,2,0:T(8,128)} %convolution_bitcast_fusion, f32[4,1024]{1,0:T(4,128)S(1)} %copy.160, f32[4,1024]{1,0:T(4,128)S(1)} %copy.156, ...), kind=kOutput, calls=%fused_computation.10 | convolution fusion | flops 4336906240 | bytes 35700736 | tf_op jit(solution)/shard_map/td,edf->etf/dot_general | solution.py:499
  359.0 2.3 dynamic_update_slice.20
  361.6 14.2 %bitcast_convert_fusion = bf16[1024,1024]{1,0:T(8,128)(2,1)S(1)} fusion(bf16[4,1024,1536]{2,1,0:T(8,128)(2,1)} %bitcast.230, bf16[4,1024,512]{1,2,0:T(8,128)(2,1)} %get-tuple-element.100, bf16[4,1024,512]{1,2,0:T(8,128)(2,1)} %get-tuple-element.99), kind=kOutput, calls=%fused_computation.23 | convolution fusion | flops 8607760384 | bytes 18874368 | tf_op jit(solution)/shard_map/etf,edf->td/dot_general | solution.py:513
  377.5 9.3 %bitcast_convert_fusion.1 = bf16[1024,1024]{1,0:T(8,128)(2,1)} fusion(bf16[4,1024,512]{1,2,0:T(8,128)(2,1)} %get-tuple-element.102, bf16[4,1024,1536]{2,1,0:T(8,128)(2,1)} %bitcast.231), kind=kOutput, calls=%fused_computation.24 | convolution fusion | flops 4296015872 | bytes 10485760 | tf_op jit(solution)/shard_map/etf,edf->td/dot_general | solution.py:536
  387.1 7.4 %fusion.4 = bf16[4,1024,512]{1,2,0:T(8,128)(2,1)S(1)} fusion(bf16[4,1024,512]{1,2,0:T(8,128)(2,1)} %get-tuple-element.102, bf16[1024,1152]{1,0:T(8,128)(2,1)} %bitcast.16), kind=kOutput, calls=%fused_computation.20 | convolution fusion | flops 4299161600 | bytes 10485760 | tf_op jit(solution)/shard_map/td,etf->edf/dot_general | solution.py:527
  394.5 12.9 %convert_bitcast_fusion = bf16[4,1024,1024]{1,2,0:T(8,128)(2,1)S(1)} fusion(bf16[4,1024,512]{1,2,0:T(8,128)(2,1)} %get-tuple-element.100, bf16[4,1024,512]{1,2,0:T(8,128)(2,1)} %get-tuple-element.99, bf16[1024,1024]{1,0:T(8,128)(2,1)} %all-gather.9.cloned.1.call-done), kind=kOutput, calls=%fused_computation.8 | convolution fusion | flops 8610906112 | bytes 18874368 | tf_op jit(solution)/shard_map/td,etf->edf/dot_general | solution.py:526
  407.4 12.7 %pad_maximum_fusion = bf16[4,1024,1536]{1,2,0:T(8,128)(2,1)} fusion(bf16[4,1024,512]{1,2,0:T(8,128)(2,1)S(1)} %fusion.4, bf16[4,1024,1024]{1,2,0:T(8,128)(2,1)S(1)} %convert_bitcast_fusion), kind=kLoop, calls=%fused_computation.1 | loop fusion | flops 25165824 | bytes 25165824 | tf_op jit(solution)/shard_map/concatenate | solution.py:531
  420.1 16.7 %copy.175 = bf16[4,1024,1536]{2,1,0:T(8,128)(2,1)} copy(bf16[4,1024,1536]{1,2,0:T(8,128)(2,1)} %pad_maximum_fusion) | data formatting | bytes 25165824 | tf_op jit(solution)/shard_map/concatenate | solution.py:531
  440.2 31.8 %reduce-scatter.4.cloned.1.call-done = bf16[256,1024]{1,0:T(8,128)(2,1)} async-done(((bf16[1024,1024]{1,0:T(8,128)(2,1)}), bf16[256,1024]{1,0:T(8,128)(2,1)}) %reduce-scatter.4.cloned.1.call-update) | async-done | bytes 524304 | tf_op jit(solution)/shard_map/reduce_scatter | solution.py:83
  472.0 2.4 subtract_add_fusion
  477.0 4.4 all-to-all-start.2
  481.4 3.7 multiply_sine_fusion
  486.2 6.9 %concatenate.92.cos_ref = f32[2048,256]{1,0:T(8,128)} concatenate(f32[2048,32]{1,0:T(8,128)S(1)} %get-tuple-element.117, f32[2048,32]{1,0:T(8,128)S(1)} %get-tuple-element.117, f32[2048,32]{1,0:T(8,128)S(1)} %get-tuple-element.117, f32[2048,32]{1,0:T(8,128)S(1)} %get-tuple-element.117, f32[2048,32]{1,0:T(8,128)S(1)} %get-tuple-element.117, f32[2048,32]{1,0:T(8,128)S(1)} %get-tuple-element.117, ...), dimensions={1} | concatenate | bytes 4194304 | tf_op jit(solution)/shard_map/concatenate | solution.py:45
  493.1 5.5 concatenate.93.sin_ref
  498.6 26.0 %attend_back.1 = (f32[2048,128]{1,0:T(8,128)}, f32[2048,128]{1,0:T(8,128)}) custom-call(s32[9]{0:T(128)} %pad_add_fusion.bounds_ref, bf16[2048,256]{1,0:T(8,128)(2,1)} %bitcast.214, bf16[2048,256]{1,0:T(8,128)(2,1)} %bitcast.215, s32[2048,1]{1,0:T(8,128)} %copy.150.doc_ref, bf16[2048,128]{1,0:T(8,128)(2,1)} %bitcast.28.do_ref, ...), custom_call_target="tpu_custom_call" | custom-call | flops 5368709120 | bytes 8388608 | tf_op jit(solution)/shard_map/attend_back/pallas_call | solution.py:331
  524.6 5.2 unrotate.1
  529.7 2.4 copy.169
  532.1 6.1 all-to-all-start.3
  541.0 22.8 %all-to-all-done.3 = bf16[8,256,256]{1,2,0:T(8,128)(2,1)S(1)} async-done(((bf16[8,256,256]{1,2,0:T(8,128)(2,1)}), bf16[8,256,256]{1,2,0:T(8,128)(2,1)S(1)}, u32[]{:S(2)}, u32[]{:S(2)}) %all-to-all-start.3) | async-done | bytes 1048608 | tf_op jit(solution)/shard_map/all_to_all | solution.py:386
  569.9 2.4 fusion.51
  574.2 2.2 fusion.12
  583.5 14.0 %collective-permute-done.10 = bf16[256,1536]{1,0:T(8,128)(2,1)} collective-permute-done((bf16[256,1536]{1,0:T(8,128)(2,1)}, bf16[256,1536]{1,0:T(8,128)(2,1)}, u32[]{:S(2)}, u32[]{:S(2)}) %collective-permute-start.10) | collective-permute-done | bytes 786464 | tf_op jit(solution)/shard_map/ppermute | solution.py:112
  600.6 3.2 collective-permute-done.7
  604.9 6.2 collective-permute-done.11
  611.2 2.5 collective-permute-done.8
  615.2 4.6 collective-permute-start.16
  621.1 5.5 collective-permute-start.14
  627.9 6.4 collective-permute-start.12
  642.1 2.9 slice.142
  (212 shorter events, 79.1 us)
Async XLA Ops:
  7.2 70.3 %all-gather.5.cloned.1.call-start = ((), (), s32[]{:S(2)}) async-start(), calls=%async_computation.7 | async-start | bytes 4595712 | tf_op jit(solution)/shard_map/all_gather | solution.py:79
  11.7 155.6 %all-gather.7.cloned.1.call-start = ((), (), s32[]{:S(2)}) async-start(), calls=%async_computation.8 | async-start | bytes 2433024 | tf_op jit(solution)/shard_map/all_gather | solution.py:79
  77.5 12.0 %copy-start.24 = (s32[1,2048]{1,0:T(1,128)S(1)}, s32[1,2048]{1,0:T(1,128)}, u32[]{:S(2)}) copy-start(s32[1,2048]{1,0:T(1,128)} %param.15) | copy-start | bytes 24580
  85.7 32.9 %all-to-all-start = ((bf16[8,256,256]{2,1,0:T(8,128)(2,1)}), bf16[8,256,256]{2,1,0:T(8,128)(2,1)S(1)}, u32[]{:S(2)}, u32[]{:S(2)}) async-start(bf16[8,256,256]{2,1,0:T(8,128)(2,1)} %get-tuple-element.18), calls=%async_computation | async-start | bytes 2097152 | tf_op jit(solution)/shard_map/all_to_all | solution.py:386
  119.6 62.2 %copy-start.9 = (bf16[1,256,1024]{2,1,0:T(8,128)(2,1)S(1)}, bf16[1,256,1024]{2,1,0:T(8,128)(2,1)}, u32[]{:S(2)}) copy-start(bf16[1,256,1024]{2,1,0:T(8,128)(2,1)} %param.13) | copy-start | bytes 1572868
  163.6 18.2 %all-to-all-start.1 = ((bf16[8,256,128]{1,2,0:T(8,128)(2,1)}), bf16[8,256,128]{1,2,0:T(8,128)(2,1)S(1)}, u32[]{:S(2)}, u32[]{:S(2)}) async-start(bf16[8,256,128]{1,2,0:T(8,128)(2,1)} %copy.151), calls=%async_computation.1 | async-start | bytes 1048576 | tf_op jit(solution)/shard_map/all_to_all | solution.py:386
  167.2 103.0 %all-gather.9.cloned.1.call-start = ((), (), s32[]{:S(2)}) async-start(), calls=%async_computation.9 | async-start | bytes 2621440 | tf_op jit(solution)/shard_map/all_gather | solution.py:79
  181.8 3.7 copy-start.18
  181.8 3.7 copy-start.21
  185.5 140.7 %all-gather.11.cloned.1.call-start = ((), (), s32[]{:S(2)}) async-start(), calls=%async_computation.10 | async-start | bytes 14155776 | tf_op jit(solution)/shard_map/all_gather | solution.py:79
  188.7 248.2 %reduce-scatter.6.cloned.1.call-start = ((), (), s32[]{:S(2)}) async-start(), calls=%async_computation.12 | async-start | bytes 2949120 | tf_op jit(solution)/shard_map/reduce_scatter | solution.py:83
  189.0 44.1 %collective-permute-start.1 = (bf16[256,1152]{1,0:T(8,128)(2,1)S(1)}, bf16[256,1152]{1,0:T(8,128)(2,1)S(1)}, u32[]{:S(2)}, u32[]{:S(2)}) collective-permute-start(bf16[256,1152]{1,0:T(8,128)(2,1)S(1)} %pad_maximum_fusion.9), channel_id=1, source_target_pairs={{8,0},{16,8},{24,16},{9,1},{17,9},{25,17},{10,2},{18,10},{26,18},{... | collective-permute-start | bytes 1769480 | tf_op jit(solution)/shard_map/ppermute | solution.py:96
  190.3 44.1 %collective-permute-start = (bf16[256,1152]{1,0:T(8,128)(2,1)S(1)}, bf16[256,1152]{1,0:T(8,128)(2,1)S(1)}, u32[]{:S(2)}, u32[]{:S(2)}) collective-permute-start(bf16[256,1152]{1,0:T(8,128)(2,1)S(1)} %pad_maximum_fusion.9), channel_id=1, source_target_pairs={{0,8},{8,16},{16,24},{1,9},{9,17},{17,25},{2,10},{10,18},{18,26},{... | collective-permute-start | bytes 1769480 | tf_op jit(solution)/shard_map/ppermute | solution.py:95
  233.1 17.9 %collective-permute-start.2 = (bf16[256,1152]{1,0:T(8,128)(2,1)S(1)}, bf16[256,1152]{1,0:T(8,128)(2,1)S(1)}, u32[]{:S(2)}, u32[]{:S(2)}) collective-permute-start(bf16[256,1152]{1,0:T(8,128)(2,1)S(1)} %collective-permute-done.1), channel_id=1, source_target_pairs={{8,0},{16,8},{24,16},{9,1},{17,9},{25,17},{10,2},{18,10},{26,18},{... | collective-permute-start | bytes 1769480 | tf_op jit(solution)/shard_map/ppermute | solution.py:96
  234.4 20.4 %collective-permute-start.4 = (bf16[256,1152]{1,0:T(8,128)(2,1)S(1)}, bf16[256,1152]{1,0:T(8,128)(2,1)}, u32[]{:S(2)}, u32[]{:S(2)}) collective-permute-start(bf16[256,1152]{1,0:T(8,128)(2,1)S(1)} %collective-permute-done), channel_id=1, source_target_pairs={{0,8},{8,16},{16,24},{1,9},{9,17},{17,25},{2,10},{10,18},{18,26},{... | collective-permute-start | bytes 1769480 | tf_op jit(solution)/shard_map/ppermute | solution.py:95
  251.0 14.4 %collective-permute-start.3 = (bf16[256,1152]{1,0:T(8,128)(2,1)S(1)}, bf16[256,1152]{1,0:T(8,128)(2,1)}, u32[]{:S(2)}, u32[]{:S(2)}) collective-permute-start(bf16[256,1152]{1,0:T(8,128)(2,1)S(1)} %collective-permute-done.2), channel_id=1, source_target_pairs={{8,0},{16,8},{24,16},{9,1},{17,9},{25,17},{10,2},{18,10},{26,18},{... | collective-permute-start | bytes 1769480 | tf_op jit(solution)/shard_map/ppermute | solution.py:96
  254.8 14.5 %collective-permute-start.5 = (bf16[256,1152]{1,0:T(8,128)(2,1)}, bf16[256,1152]{1,0:T(8,128)(2,1)S(1)}, u32[]{:S(2)}, u32[]{:S(2)}) collective-permute-start(bf16[256,1152]{1,0:T(8,128)(2,1)} %collective-permute-done.4), channel_id=1, source_target_pairs={{0,8},{8,16},{16,24},{1,9},{9,17},{17,25},{2,10},{10,18},{18,26},{... | collective-permute-start | bytes 1769480 | tf_op jit(solution)/shard_map/ppermute | solution.py:95
  377.5 94.5 %reduce-scatter.4.cloned.1.call-start = ((), (), s32[]{:S(2)}) async-start(), calls=%async_computation.11 | async-start | bytes 2621440 | tf_op jit(solution)/shard_map/reduce_scatter | solution.py:83
  386.9 255.3 %reduce-scatter.8.cloned.1.call-start = ((), (), s32[]{:S(2)}) async-start(), calls=%async_computation.13 | async-start | bytes 14155776 | tf_op jit(solution)/shard_map/reduce_scatter | solution.py:83
  472.0 3.4 copy-start.23
  477.0 21.6 %all-to-all-start.2 = ((bf16[8,256,128]{2,1,0:T(8,128)(2,1)}), bf16[8,256,128]{2,1,0:T(8,128)(2,1)}, u32[]{:S(2)}, u32[]{:S(2)}) async-start(bf16[8,256,128]{2,1,0:T(8,128)(2,1)} %bitcast.173), calls=%async_computation.4 | async-start | bytes 1048576 | tf_op jit(solution)/shard_map/all_to_all | solution.py:386
  529.7 8.5 %copy-start.10 = (bf16[1,256,1024]{2,1,0:T(8,128)(2,1)S(1)}, bf16[1,256,1024]{2,1,0:T(8,128)(2,1)}, u32[]{:S(2)}) copy-start(bf16[1,256,1024]{2,1,0:T(8,128)(2,1)} %param.13) | copy-start | bytes 1572868
  529.7 9.8 %copy-start.3 = (f32[256,1024]{1,0:T(8,128)S(1)}, f32[256,1024]{1,0:T(8,128)}, u32[]{:S(2)}) copy-start(f32[256,1024]{1,0:T(8,128)} %copy-done.2) | copy-start | bytes 3145732
  529.7 9.8 %copy-start.19 = (bf16[8,256,128]{1,2,0:T(8,128)(2,1)S(1)}, bf16[8,256,128]{1,2,0:T(8,128)(2,1)}, u32[]{:S(2)}) copy-start(bf16[8,256,128]{1,2,0:T(8,128)(2,1)} %copy-done.18) | copy-start | bytes 1572868
  532.1 31.6 %all-to-all-start.3 = ((bf16[8,256,256]{1,2,0:T(8,128)(2,1)}), bf16[8,256,256]{1,2,0:T(8,128)(2,1)S(1)}, u32[]{:S(2)}, u32[]{:S(2)}) async-start(bf16[8,256,256]{1,2,0:T(8,128)(2,1)} %copy.169), calls=%async_computation.5 | async-start | bytes 2097152 | tf_op jit(solution)/shard_map/all_to_all | solution.py:386
  540.5 26.6 %copy-start = (bf16[4,2,2,2,32,1024]{5,4,0,2,1,3:T(8,128)(2,1)}, bf16[4,2,2,2,32,1024]{5,4,0,2,1,3:T(8,128)(2,1)S(1)}, u32[]{:S(2)}) copy-start(bf16[4,2,2,2,32,1024]{5,4,0,2,1,3:T(8,128)(2,1)S(1)} %copy.174) | copy-start | bytes 6291460
  563.8 3.5 copy-start.15
  565.6 1.6 copy-start.17
  565.7 3.4 slice-start
  567.3 1.9 slice-start.1
  567.3 6.9 %collective-permute-start.9 = (bf16[512,1536]{1,0:T(8,128)(2,1)}, bf16[512,1536]{1,0:T(8,128)(2,1)}, u32[]{:S(2)}, u32[]{:S(2)}) collective-permute-start(bf16[512,1536]{1,0:T(8,128)(2,1)} %fusion.29), channel_id=1, source_target_pairs={{0,1},{1,0},{2,3},{3,2},{4,5},{5,4},{6,7},{7,6},{8,9},{9,8},{10,11... | collective-permute-start | bytes 4718600 | tf_op jit(solution)/shard_map/ppermute | solution.py:112
  573.9 4.9 collective-permute-start.6
  576.4 2.3 copy-start.7
  577.5 19.9 %collective-permute-start.10 = (bf16[256,1536]{1,0:T(8,128)(2,1)}, bf16[256,1536]{1,0:T(8,128)(2,1)}, u32[]{:S(2)}, u32[]{:S(2)}) collective-permute-start(bf16[256,1536]{1,0:T(8,128)(2,1)} %dynamic-slice_bitcast_fusion.1), channel_id=1, source_target_pairs={{0,4},{4,0},{1,5},{5,1},{2,6},{6,2},{3,7},{7,3},{8,12},{12,8},{9,1... | collective-permute-start | bytes 2359304 | tf_op jit(solution)/shard_map/ppermute | solution.py:112
  581.9 21.9 %copy-start.6 = (bf16[512,1664]{1,0:T(8,128)(2,1)S(1)}, bf16[512,1664]{1,0:T(8,128)(2,1)}, u32[]{:S(2)}) copy-start(bf16[512,1664]{1,0:T(8,128)(2,1)} %copy-done.5) | copy-start | bytes 5111812
  581.9 21.9 %collective-permute-start.7 = (bf16[256,1664]{1,0:T(8,128)(2,1)S(1)}, bf16[256,1664]{1,0:T(8,128)(2,1)S(1)}, u32[]{:S(2)}, u32[]{:S(2)}) collective-permute-start(bf16[256,1664]{1,0:T(8,128)(2,1)S(1)} %dynamic-slice_bitcast_fusion), channel_id=1, source_target_pairs={{0,2},{2,0},{1,3},{3,1},{4,6},{6,4},{5,7},{7,5},{8,10},{10,8},{9,1... | collective-permute-start | bytes 2555912 | tf_op jit(solution)/shard_map/ppermute | solution.py:112
  599.0 12.0 %collective-permute-start.11 = (bf16[128,1536]{1,0:T(8,128)(2,1)S(1)}, bf16[128,1536]{1,0:T(8,128)(2,1)S(1)}, u32[]{:S(2)}, u32[]{:S(2)}) collective-permute-start(bf16[128,1536]{1,0:T(8,128)(2,1)S(1)} %dynamic-slice_bitcast_fusion.4), channel_id=1, source_target_pairs={{0,2},{2,0},{1,3},{3,1},{4,6},{6,4},{5,7},{7,5},{8,10},{10,8},{9,1... | collective-permute-start | bytes 1179656 | tf_op jit(solution)/shard_map/ppermute | solution.py:112
  604.1 30.2 %copy-start.4 = (f32[256,1024]{1,0:T(8,128)S(1)}, f32[256,1024]{1,0:T(8,128)}, u32[]{:S(2)}) copy-start(f32[256,1024]{1,0:T(8,128)} %copy-done.2) | copy-start | bytes 3145732
  604.1 30.2 %copy-start.12 = (bf16[1,256,1024]{2,1,0:T(8,128)(2,1)S(1)}, bf16[1,256,1024]{2,1,0:T(8,128)(2,1)}, u32[]{:S(2)}) copy-start(bf16[1,256,1024]{2,1,0:T(8,128)(2,1)} %param.13) | copy-start | bytes 1572868
  604.1 30.2 %copy-start.20 = (f32[256,1024]{1,0:T(8,128)S(1)}, f32[256,1024]{1,0:T(8,128)}, u32[]{:S(2)}) copy-start(f32[256,1024]{1,0:T(8,128)} %get-tuple-element.130) | copy-start | bytes 3145732
  604.1 9.5 %collective-permute-start.8 = (bf16[128,1664]{1,0:T(8,128)(2,1)S(1)}, bf16[128,1664]{1,0:T(8,128)(2,1)S(1)}, u32[]{:S(2)}, u32[]{:S(2)}) collective-permute-start(bf16[128,1664]{1,0:T(8,128)(2,1)S(1)} %dynamic-slice_bitcast_fusion.3), channel_id=1, source_target_pairs={{0,4},{4,0},{1,5},{5,1},{2,6},{6,2},{3,7},{7,3},{8,12},{12,8},{9,1... | collective-permute-start | bytes 1277960 | tf_op jit(solution)/shard_map/ppermute | solution.py:112
  613.9 14.0 %collective-permute-start.17 = (bf16[32,3200]{1,0:T(8,128)(2,1)S(1)}, bf16[32,3200]{1,0:T(8,128)(2,1)S(1)}, u32[]{:S(2)}, u32[]{:S(2)}) collective-permute-start(bf16[32,3200]{1,0:T(8,128)(2,1)S(1)} %get-tuple-element.106), channel_id=1, source_target_pairs={{8,0},{16,8},{24,16},{9,1},{17,9},{25,17},{10,2},{18,10},{26,18},{... | collective-permute-start | bytes 614408 | tf_op jit(solution)/shard_map/ppermute | solution.py:125
  615.2 20.3 %collective-permute-start.16 = (bf16[32,3200]{1,0:T(8,128)(2,1)S(1)}, bf16[32,3200]{1,0:T(8,128)(2,1)S(1)}, u32[]{:S(2)}, u32[]{:S(2)}) collective-permute-start(bf16[32,3200]{1,0:T(8,128)(2,1)S(1)} %get-tuple-element.107), channel_id=1, source_target_pairs={{0,8},{8,16},{16,24},{1,9},{9,17},{17,25},{2,10},{10,18},{18,26},{... | collective-permute-start | bytes 614408 | tf_op jit(solution)/shard_map/ppermute | solution.py:125
  619.8 15.8 %collective-permute-start.15 = (bf16[32,3200]{1,0:T(8,128)(2,1)S(1)}, bf16[32,3200]{1,0:T(8,128)(2,1)S(1)}, u32[]{:S(2)}, u32[]{:S(2)}) collective-permute-start(bf16[32,3200]{1,0:T(8,128)(2,1)S(1)} %get-tuple-element.108), channel_id=1, source_target_pairs={{16,0},{24,8},{17,1},{25,9},{18,2},{26,10},{19,3},{27,11},{20,4},{... | collective-permute-start | bytes 614408 | tf_op jit(solution)/shard_map/ppermute | solution.py:125
  621.1 14.5 %collective-permute-start.14 = (bf16[32,3200]{1,0:T(8,128)(2,1)S(1)}, bf16[32,3200]{1,0:T(8,128)(2,1)S(1)}, u32[]{:S(2)}, u32[]{:S(2)}) collective-permute-start(bf16[32,3200]{1,0:T(8,128)(2,1)S(1)} %get-tuple-element.109), channel_id=1, source_target_pairs={{0,16},{8,24},{1,17},{9,25},{2,18},{10,26},{3,19},{11,27},{4,20},{... | collective-permute-start | bytes 614408 | tf_op jit(solution)/shard_map/ppermute | solution.py:125
  626.6 9.4 %collective-permute-start.13 = (bf16[32,3200]{1,0:T(8,128)(2,1)S(1)}, bf16[32,3200]{1,0:T(8,128)(2,1)S(1)}, u32[]{:S(2)}, u32[]{:S(2)}) collective-permute-start(bf16[32,3200]{1,0:T(8,128)(2,1)S(1)} %get-tuple-element.110), channel_id=1, source_target_pairs={{24,0},{25,1},{26,2},{27,3},{28,4},{29,5},{30,6},{31,7}} | collective-permute-start | bytes 614408 | tf_op jit(solution)/shard_map/ppermute | solution.py:125
  627.9 9.6 %collective-permute-start.12 = (bf16[32,3200]{1,0:T(8,128)(2,1)S(1)}, bf16[32,3200]{1,0:T(8,128)(2,1)S(1)}, u32[]{:S(2)}, u32[]{:S(2)}) collective-permute-start(bf16[32,3200]{1,0:T(8,128)(2,1)S(1)} %get-tuple-element.105), channel_id=1, source_target_pairs={{0,24},{1,25},{2,26},{3,27},{4,28},{5,29},{6,30},{7,31}} | collective-permute-start | bytes 614408 | tf_op jit(solution)/shard_map/ppermute | solution.py:125
  642.1 2.9 copy-start.8
  (9 other events, 11.4 us)
Sparse Core Ops, SparseCore 0:
  11.8 65.6 all-gather.4
  81.0 62.3 all-gather.6
  185.6 61.9 all-gather.8
  249.3 76.7 all-gather.10
  377.6 48.8 reduce-scatter.5
  428.6 43.3 reduce-scatter.3
  475.9 96.0 reduce-scatter.7

commit v3 on v2

--- a/solution.py
+++ b/solution.py
@@ -1,5 +1,3 @@
-import functools
-
 import jax
 import jax.numpy as jnp
 from jax import lax
@@ -114,18 +112,6 @@
     return (own.astype(f32) + other.astype(f32)).astype(v.dtype)
 
 
-def line_sum(v, axis):
-    n, me = lax.axis_size(axis), lax.axis_index(axis)
-    v = v.reshape((n, v.shape[0] // n) + v.shape[1:])
-    total = lax.dynamic_index_in_dim(v, me, 0, False).astype(f32)
-    for k in range(n - 1, 0, -1):
-        for step in (k, -k):
-            pairs = [(i, i + step) for i in range(n) if 0 <= i + step < n]
-            block = lax.dynamic_index_in_dim(v, jnp.clip(me + step, 0, n - 1), 0, False)
-            total = total + lax.ppermute(block, axis, pairs).astype(f32)
-    return total
-
-
 def rows_for(x, order):
     sizes = tuple(lax.axis_size(axis) for axis in ALL)
     shape = sizes + (x.shape[0] // lax.axis_size(ALL),) + x.shape[1:]
@@ -148,7 +134,7 @@
     @pl.when(pl.program_id(0) == 0)
     def _():
         x = x_ref[...].astype(f32)
-        gain = jnp.transpose(gain_ref[...].astype(f32))[0:1, :]
+        gain = jnp.transpose(gain_ref[...].astype(f32))[E : E + 1, :]
         normed_ref[...] = rms_scale(x, gain).astype(bf16)
 
     pre = jnp.dot(normed_ref[...], w_ref[...], preferred_element_type=f32)
@@ -159,7 +145,7 @@
     tokens, width = x.shape
     whole = pl.BlockSpec((tokens, width), lambda h: (0, 0))
     table = pl.BlockSpec((tokens, HEAD_PACK), lambda h: (0, 0))
-    gain_at = KEY_VALUE_HEADS * HEAD_PACK // LANES
+    gain_at = packed.shape[1] // LANES - 1
     return pl.pallas_call(
         project_kernel,
         grid=(KEY_VALUE_HEADS,),
@@ -210,38 +196,48 @@
     return (keys >= jnp.concatenate([doc, doc], axis=0)) & (keys <= rows)
 
 
-def attend_kernel(bounds_ref, q_ref, kv_ref, doc_ref, o_ref, low_ref, lse_ref, top, total, acc):
+def attend_kernel(bounds_ref, q_ref, kv_ref, doc_ref, o_ref, low_ref, lse_ref, kept, top, total, acc):
     i = pl.program_id(0)
     steps = pl.num_programs(0)
     offset = bounds_ref[steps]
+    first, last = bounds_ref[i], i + offset + 1
     q = both_heads_low(q_ref[...].astype(f32) * SCALE_OF_SCORES).astype(bf16)
     doc = doc_ref[...]
     top[...] = jnp.full_like(top, NEGATIVE_HUGE)
     total[...] = jnp.zeros_like(total)
     acc[...] = jnp.zeros_like(acc)
 
-    def step(j, carried):
+    def score(j, carried):
         start = pl.multiple_of(j * BLOCK, BLOCK)
-        kv = kv_ref[pl.ds(start, BLOCK), :]
-        scores = contract_cols(q, kv)
+        scores = contract_cols(q, kv_ref[pl.ds(start, BLOCK), :])
         allowed = allowed_pairs(scores.shape, (i + offset) * BLOCK, j * BLOCK, doc)
         scores = jnp.where(allowed, scores, NEGATIVE_HUGE)
-        old = top[...]
-        new = jnp.maximum(old, jnp.max(scores, axis=1, keepdims=True))
-        probs = jnp.exp(scores - new)
-        keep = jnp.exp(old - new)
-        top[...] = new
-        total[...] = total[...] * keep + jnp.sum(probs, axis=1, keepdims=True)
-        acc[...] = acc[...] * keep + jnp.dot(probs.astype(bf16), kv, preferred_element_type=f32)
+        kept[:, pl.ds(start, BLOCK)] = scores
+        top[...] = jnp.maximum(top[...], jnp.maximum(scores[:, :LANES], scores[:, LANES:]))
         return carried
 
-    lax.fori_loop(bounds_ref[i], i + offset + 1, step, 0)
-    mixed = acc[...] / total[...]
-    first, second = mixed[:BLOCK], mixed[BLOCK:]
-    out = jnp.where(lower_lanes(first.shape), pltpu.roll(first, HEAD_SIZE, 1), second)
+    lax.fori_loop(first, last, score, 0)
+    highest = jnp.max(top[...], axis=1, keepdims=True)
+
+    def mix(j, carried):
+        start = pl.multiple_of(j * BLOCK, BLOCK)
+        probs = jnp.exp(kept[:, pl.ds(start, BLOCK)] - highest)
+        total[...] += probs[:, :LANES] + probs[:, LANES:]
+        acc[...] += jnp.dot(
+            probs.astype(bf16), kv_ref[pl.ds(start, BLOCK), :], preferred_element_type=f32
+        )
+        return carried
+
+    lax.fori_loop(first, last, mix, 0)
+    row_total = jnp.sum(total[...], axis=1, keepdims=True)
+    mixed = acc[...] / row_total
+    first_head, second_head = mixed[:BLOCK], mixed[BLOCK:]
+    out = jnp.where(
+        lower_lanes(first_head.shape), pltpu.roll(first_head, HEAD_SIZE, 1), second_head
+    )
     o_ref[...] = out
     low_ref[...] = out.astype(bf16)
-    lse_ref[0] = top[...] + jnp.log(total[...])
+    lse_ref[0] = highest + jnp.log(row_total)
 
 
 def attend(bounds, qkv, kv, kv_at, doc):
@@ -260,8 +256,9 @@
             ],
             out_specs=[pair, pair, pl.BlockSpec((1, 2 * BLOCK, 1), lambda i, s: (i, 0, 0))],
             scratch_shapes=[
-                pltpu.VMEM((2 * BLOCK, 1), f32),
-                pltpu.VMEM((2 * BLOCK, 1), f32),
+                pltpu.VMEM((2 * BLOCK, keys), f32),
+                pltpu.VMEM((2 * BLOCK, LANES), f32),
+                pltpu.VMEM((2 * BLOCK, LANES), f32),
                 pltpu.VMEM((2 * BLOCK, PAIR), f32),
             ],
         ),
@@ -380,6 +377,151 @@
         ),
         name="unrotate",
     )(dq, dkv, cos, sin)
+
+
+def lane_column(x, at):
+    lane = lax.broadcasted_iota(jnp.int32, x.shape, 1)
+    return jnp.sum(jnp.where(lane == at, x, 0.0), axis=1, keepdims=True)
+
+
+def experts_kernel(
+    group_ref, n_ref, routed_ref, router_ref, w_ref, z_ref,
+    back_ref, gates_ref, hidden_ref, pre_ref, acc, dots,
+):
+    e = pl.program_id(0)
+    own = group_ref[0] * EXPERTS_HERE + e
+    rows = n_ref.shape[0]
+
+    @pl.when(e == 0)
+    def _():
+        logits = jnp.dot(n_ref[...], router_ref[...], preferred_element_type=f32)
+        routed = routed_ref[...].astype(f32) > 0.5
+        highest = jnp.max(jnp.where(routed, logits, NEGATIVE_HUGE), axis=1, keepdims=True)
+        weights = jnp.where(routed, jnp.exp(jnp.where(routed, logits - highest, 0.0)), 0.0)
+        gates_ref[...] = weights / jnp.sum(weights, axis=1, keepdims=True)
+        acc[...] = jnp.zeros_like(acc)
+        dots[...] = jnp.zeros_like(dots)
+
+    w_in = w_ref[0, :, : 2 * F]
+    for t in range(rows // BLOCK):
+        part = pl.ds(t * BLOCK, BLOCK)
+        pre = jnp.dot(n_ref[part, :], w_in, preferred_element_type=f32)
+        gate, up = pre[:, :F], pre[:, F:]
+        z = z_ref[0, part, :]
+        weight = lane_column(gates_ref[part, :], own)
+        sig = 1.0 / (1.0 + jnp.exp(-gate))
+        act = gate * sig
+        hidden = act * up
+        hidden_ref[0, part, :] = (weight * hidden).astype(bf16)
+        dot = RESIDUAL_SCALE * jnp.sum(hidden.astype(bf16).astype(f32) * z, axis=1, keepdims=True)
+        lane = lax.broadcasted_iota(jnp.int32, (BLOCK, LANES), 1)
+        dots[part, :] += jnp.where(lane == own, dot, 0.0)
+        scaled = (RESIDUAL_SCALE * weight) * z
+        pre_ref[0, part, :F] = (scaled * up * (sig + act * (1.0 - sig))).astype(bf16)
+        pre_ref[0, part, F:] = (scaled * act).astype(bf16)
+        acc[part, :] += contract_cols(pre_ref[0, part, :], w_in)
+
+    @pl.when(e == EXPERTS_HERE - 1)
+    def _():
+        width = n_ref.shape[1]
+        back_ref[:, :width] = acc[...].astype(bf16)
+        high = dots[...].astype(bf16)
+        low = dots[...] - high.astype(f32)
+        back_ref[:, width:] = (high.astype(f32) + pltpu.roll(low, E, 1)).astype(bf16)
+
+
+def experts(group, normed, early, packed, w_all, z):
+    rows, width = normed.shape
+    count = w_all.shape[0]
+    whole = pl.BlockSpec((rows, width), lambda e, g: (0, 0))
+    column = width // LANES
+    router_at = packed.shape[1] // LANES - 1
+    return pl.pallas_call(
+        experts_kernel,
+        grid_spec=pltpu.PrefetchScalarGridSpec(
+            num_scalar_prefetch=1,
+            grid=(count,),
+            in_specs=[
+                whole,
+                pl.BlockSpec((rows, LANES), lambda e, g: (0, column)),
+                pl.BlockSpec((width, LANES), lambda e, g: (0, router_at)),
+                pl.BlockSpec((1, width, 3 * F), lambda e, g: (e, 0, 0)),
+                pl.BlockSpec((1, rows, F), lambda e, g: (e, 0, 0)),
+            ],
+            out_specs=[
+                pl.BlockSpec((rows, width + LANES), lambda e, g: (0, 0)),
+                pl.BlockSpec((rows, LANES), lambda e, g: (0, 0)),
+                pl.BlockSpec((1, rows, F), lambda e, g: (e, 0, 0)),
+                pl.BlockSpec((1, rows, 2 * F), lambda e, g: (e, 0, 0)),
+            ],
+            scratch_shapes=[pltpu.VMEM((rows, width), f32), pltpu.VMEM((rows, LANES), f32)],
+        ),
+        out_shape=[
+            jax.ShapeDtypeStruct((rows, width + LANES), bf16),
+            jax.ShapeDtypeStruct((rows, LANES), f32),
+            jax.ShapeDtypeStruct((count, rows, F), bf16),
+            jax.ShapeDtypeStruct((count, rows, 2 * F), bf16),
+        ],
+        compiler_params=pltpu.CompilerParams(vmem_limit_bytes=VMEM_LIMIT),
+        cost_estimate=pl.CostEstimate(
+            flops=2 * count * rows * width * 4 * F, bytes_accessed=40 * 2**20, transcendentals=0
+        ),
+        name="experts",
+    )(group, normed, early, packed, w_all, z)
+
+
+def expert_grads_kernel(n_ref, ct_ref, w_ref, hidden_ref, pre_ref, y_ref, grad_ref, n_t, ct_t, acc):
+    e = pl.program_id(0)
+
+    @pl.when(e == 0)
+    def _():
+        n_t[...] = jnp.transpose(n_ref[...])
+        ct_t[...] = jnp.transpose(ct_ref[...])
+        acc[...] = jnp.zeros_like(acc)
+
+    grad_ref[0, :, : 2 * F] = jnp.dot(
+        n_t[...], pre_ref[0], preferred_element_type=f32
+    ).astype(bf16)
+    grad_ref[0, :, 2 * F :] = (
+        RESIDUAL_SCALE * jnp.dot(ct_t[...], hidden_ref[0], preferred_element_type=f32)
+    ).astype(bf16)
+    acc[...] += contract_cols(hidden_ref[0], w_ref[0, :, 2 * F :])
+
+    @pl.when(e == EXPERTS_HERE - 1)
+    def _():
+        y_ref[...] = acc[...].astype(bf16)
+
+
+def expert_grads(normed, early, w_all, hidden, pre):
+    rows, width = normed.shape
+    count = w_all.shape[0]
+    whole = pl.BlockSpec((rows, width), lambda e: (0, 0))
+    return pl.pallas_call(
+        expert_grads_kernel,
+        grid=(count,),
+        in_specs=[
+            whole,
+            whole,
+            pl.BlockSpec((1, width, 3 * F), lambda e: (e, 0, 0)),
+            pl.BlockSpec((1, rows, F), lambda e: (e, 0, 0)),
+            pl.BlockSpec((1, rows, 2 * F), lambda e: (e, 0, 0)),
+        ],
+        out_specs=[whole, pl.BlockSpec((1, width, 3 * F), lambda e: (e, 0, 0))],
+        out_shape=[
+            jax.ShapeDtypeStruct((rows, width), bf16),
+            jax.ShapeDtypeStruct((count, width, 3 * F), bf16),
+        ],
+        scratch_shapes=[
+            pltpu.VMEM((width, rows), bf16),
+            pltpu.VMEM((width, rows), bf16),
+            pltpu.VMEM((rows, width), f32),
+        ],
+        compiler_params=pltpu.CompilerParams(vmem_limit_bytes=VMEM_LIMIT),
+        cost_estimate=pl.CostEstimate(
+            flops=2 * count * rows * width * 4 * F, bytes_accessed=40 * 2**20, transcendentals=0
+        ),
+        name="expert_grads",
+    )(normed, early, w_all, hidden, pre)
 
 
 def exchange(x, axes):
@@ -441,14 +583,19 @@
     ).reshape(own_rows, KEY_VALUE_HEADS * HEAD_PACK)
     qkv_width = KEY_VALUE_HEADS * HEAD_PACK
     first_all = gather(
-        jnp.concatenate([by_head, pad_lanes(norm_attn.astype(bf16)[:, None], LANES)], axis=1), ALL
-    )
-    second_all = gather(
         jnp.concatenate(
             [
+                by_head,
                 w_output.astype(bf16),
                 pad_lanes(
-                    jnp.concatenate([w_router.astype(bf16), norm_moe.astype(bf16)[:, None]], axis=1),
+                    jnp.concatenate(
+                        [
+                            w_router.astype(bf16),
+                            norm_attn.astype(bf16)[:, None],
+                            norm_moe.astype(bf16)[:, None],
+                        ],
+                        axis=1,
+                    ),
                     LANES,
                 ),
             ],
@@ -457,20 +604,29 @@
         ALL,
     )
     experts_low = jnp.concatenate([expert_in.astype(bf16), expert_out.astype(bf16)], axis=1)
+    first_all, experts_low, cos_local, sin_local, cos_span, sin_span, bounds, doc_column = (
+        lax.optimization_barrier(
+            (first_all, experts_low, cos_local, sin_local, cos_span, sin_span, bounds, doc_column)
+        )
+    )
     experts_all = gather(experts_low, PLANE).reshape(EXPERTS_HERE, width, 3 * F)
-    in_w, out_w = experts_all[:, :, : 2 * F], experts_all[:, :, 2 * F :]
-    output_w = second_all[:, :width]
-    router_w = second_all[:, width : width + E]
-    gain_two_f = second_all[:, width + E].astype(f32)
-    gain_one_f = first_all[:, qkv_width].astype(f32)
+    output_w = first_all[:, qkv_width : qkv_width + width]
+    small_at = qkv_width + width
+    router_w = first_all[:, small_at : small_at + E]
+    gain_one_f = first_all[:, small_at + E].astype(f32)
+    gain_two_f = first_all[:, small_at + E + 1].astype(f32)
 
     expert_ids = jnp.arange(E, dtype=jnp.int32)
     routed_own = jnp.any(routes[0][:, :, None] == expert_ids[None, None, :], axis=1)
     early_all = chain_gather(
-        jnp.concatenate([cotangent[0], pad_lanes(routed_own.astype(bf16), LANES)], axis=1), "a"
-    )
-    grad_all = early_all[:, :width]
-    routed = early_all[:, width : width + E] > 0.5
+        lax.optimization_barrier(
+            (
+                jnp.concatenate([cotangent[0], pad_lanes(routed_own.astype(bf16), LANES)], axis=1),
+                first_all,
+            )
+        )[0],
+        "a",
+    )
 
     by_heads, normed_one = project(tokens[0], first_all, cos_local, sin_local)
     qkv = exchange(by_heads, head_axes).reshape(span, HEAD_PACK)
@@ -488,57 +644,31 @@
     resid = x_local + RESIDUAL_SCALE * attn_out
     normed_two = rms_scale(resid, gain_two_f).astype(bf16)
 
+    normed_two, experts_all, early_all = lax.optimization_barrier(
+        (normed_two, experts_all, early_all)
+    )
     normed_all = gather(normed_two, "a")
-    logits = jnp.dot(normed_all, router_w, preferred_element_type=f32)
-    top_logit = jnp.max(jnp.where(routed, logits, NEGATIVE_HUGE), axis=-1, keepdims=True)
-    weights = jnp.where(routed, jnp.exp(jnp.minimum(logits - top_logit, 0.0)), 0.0)
-    gates_all = weights / jnp.sum(weights, axis=-1, keepdims=True)
-    gates_group = lax.dynamic_slice_in_dim(gates_all, group * EXPERTS_HERE, EXPERTS_HERE, 1)
-    gate_cols = gates_group.T[:, :, None]
-
-    grad_hidden = jnp.einsum("td,edf->etf", grad_all, out_w, preferred_element_type=f32)
-    pre_act = jnp.einsum("td,edf->etf", normed_all, in_w, preferred_element_type=f32)
-    gate_pre = pre_act[..., :F]
-    up_pre = pre_act[..., F:]
-    gate_sig = jax.nn.sigmoid(gate_pre)
-    gate_act = gate_pre * gate_sig
-    hidden = gate_act * up_pre
-    gated_hidden = (gate_cols * hidden).astype(bf16)
-    grad_gates = RESIDUAL_SCALE * jnp.sum(hidden.astype(bf16).astype(f32) * grad_hidden, axis=-1)
-    scaled_grad = (RESIDUAL_SCALE * gate_cols) * grad_hidden
-    grad_gate = scaled_grad * up_pre * (gate_sig + gate_pre * gate_sig * (1.0 - gate_sig))
-    grad_up = scaled_grad * gate_act
-    grad_pre = jnp.concatenate([grad_gate, grad_up], axis=-1).astype(bf16)
-
-    back_part = jnp.einsum("etf,edf->td", grad_pre, in_w, preferred_element_type=f32)
-    gate_grads = jnp.zeros((gates_all.shape[0], E), f32)
-    gate_grads = lax.dynamic_update_slice_in_dim(gate_grads, grad_gates.T, group * EXPERTS_HERE, 1)
-    gate_high = gate_grads.astype(bf16)
-    gate_low = (gate_grads - lax.reduce_precision(gate_grads, 8, 7)).astype(bf16)
-    back_own = scatter_sum(
-        jnp.concatenate(
-            [back_part.astype(bf16), pad_lanes(jnp.concatenate([gate_high, gate_low], 1), LANES)],
-            axis=1,
-        ),
-        "a",
-    ).astype(f32)
-
-    grad_in_part = jnp.einsum("td,etf->edf", normed_all, grad_pre, preferred_element_type=f32)
-    grad_out_part = RESIDUAL_SCALE * jnp.einsum(
-        "td,etf->edf", grad_all, gated_hidden, preferred_element_type=f32
-    )
-    grad_experts = scatter_sum(
-        jnp.concatenate([grad_in_part.astype(bf16), grad_out_part.astype(bf16)], axis=2).reshape(
-            EXPERTS_HERE * width, 3 * F
-        ),
-        PLANE,
-    ).astype(f32)
-    moe_part = jnp.einsum("etf,edf->td", gated_hidden, out_w, preferred_element_type=f32)
-    moe_sum = scatter_sum(moe_part.astype(bf16), "a").astype(f32)
-    layer_sum = resid + RESIDUAL_SCALE * moe_sum
+    grad_hidden = jnp.einsum(
+        "td,edf->etf",
+        early_all[:, :width],
+        experts_all[:, :, 2 * F :],
+        preferred_element_type=f32,
+    )
+    back_part, gates_all, gated_hidden, grad_pre = experts(
+        group.reshape(1), normed_all, early_all, first_all, experts_all, grad_hidden
+    )
+    back_own = scatter_sum(back_part, "a").astype(f32)
+    moe_part, grad_experts = expert_grads(
+        normed_all, early_all, experts_all, gated_hidden, grad_pre
+    )
+    back_own, moe_part, grad_experts = lax.optimization_barrier(
+        (back_own, moe_part, grad_experts)
+    )
+    grad_experts = scatter_sum(grad_experts.reshape(EXPERTS_HERE * width, 3 * F), PLANE)
+    moe_sum = scatter_sum(moe_part, "a")
 
     grad_out = cotangent[0].astype(f32)
-    gates = lax.dynamic_slice_in_dim(gates_all, group * token_count, token_count)
+    gates = lax.dynamic_slice_in_dim(gates_all, group * token_count, token_count)[:, :E]
     gate_grads_own = back_own[:, width : width + E] + back_own[:, width + E : width + 2 * E]
     grad_logits = gates * (gate_grads_own - jnp.sum(gates * gate_grads_own, axis=-1, keepdims=True))
     grad_normed_two = back_own[:, :width] + jnp.dot(
@@ -575,9 +705,6 @@
     cut = 3 * qkv_width // 4
     small = jnp.concatenate([grad_router, grad_gain_one[:, None], grad_gain_two[:, None]], axis=1)
 
-    def weight_rows(acts, grads, order):
-        return contract_rows(acts, grads).astype(bf16)
-
     left = jnp.concatenate(
         [
             rows_for(contract_rows(normed_one, grad_qkv[:, :cut]).astype(bf16), orders[0]),
@@ -595,7 +722,12 @@
     left, right = halve(left, "c"), halve(right, "c")
     left, right = halve(left, "y"), halve(right, "b")
     left, right = halve(left, "b"), halve(right, "y")
-    total = line_sum(jnp.concatenate([left, right], axis=1), "a")
+    last, grad_experts, moe_sum, resid = lax.optimization_barrier(
+        (jnp.concatenate([left, right], axis=1), grad_experts, moe_sum, resid)
+    )
+    total = scatter_sum(last, "a").astype(f32)
+    grad_experts = grad_experts.astype(f32)
+    layer_sum = resid + RESIDUAL_SCALE * moe_sum.astype(f32)
     small_sum = total[:, cut : cut + LANES]
     qkv_sum = jnp.concatenate(
         [total[:, :cut], total[:, cut + LANES : qkv_width + LANES]], axis=1

time: 663 us -> 550 us (0.83)
  matrix products: 90.5 us -> 27.5 us
  waiting for transfers between devices: 286 us -> 223 us
  Pallas kernels: 81.3 us -> 117 us
  blocking collectives: 0 us -> 33 us
  starting transfers between devices: 62.5 us -> 41.9 us
  other arithmetic: 57.6 us -> 38.7 us
  local copies, waits for them, and re-layouts: 60 us -> 42.5 us
    dot_general x7 -> x1, matrix products: 78.9 us -> 10.6 us  [body(): jnp.einsum('td,edf->etf', early_all[:, :width], experts_all[:, :, 2 * F:]...]
    pallas_call x0 -> x2, Pallas kernels: none -> 55.5 us  [the longest x1 28.9 us: experts(): pl.pallas_call(experts_kernel, grid_spec=pltpu.PrefetchScalarGridSpec(num...]
    ppermute x3, waiting for transfers between devices: 55.4 us -> 0.01 us  [chain_gather(): down = lax.ppermute(down, axis, [(i + 1, i) for i in range(n - 1)])]
    all_to_all x0 -> x1, blocking collectives: none -> 33 us  [exchange(): return lax.all_to_all(x, axes, 0, 0, tiled=True)]
    all_gather x4 -> x3, waiting for transfers between devices: 109 us -> 78.3 us  [gather(): return lax.all_gather(x, axes, axis=0, tiled=True)]
    ppermute x3, waiting for transfers between devices: 0.95 us -> 30.1 us  [chain_gather(): up = lax.ppermute(up, axis, [(i, i + 1) for i in range(n - 1)])]
    all_to_all x4 -> x3, waiting for transfers between devices: 61.4 us -> 32.9 us  [exchange(): return lax.all_to_all(x, axes, 0, 0, tiled=True)]
    pallas_call x1, Pallas kernels: 42 us -> 21.4 us  [attend(): pl.pallas_call(attend_kernel, grid_spec=pltpu.PrefetchScalarGridSpec(num_...]
  transfers between devices with their start and end apart: 29 -> 22, of which waited for: 16 -> 13; matrix products, arithmetic and copies ran while one was open for 21% -> 17% of each run, Pallas kernels for 12% -> 16%
where the time goes in v3:
time: 550 us; the launch traced here: 540 us
  waiting for transfers between devices  223 us (41%)
  Pallas kernels  117 us (21%)
  local copies, waits for them, and re-layouts  42.5 us (8%)
  starting transfers between devices  41.9 us (8%)
  other arithmetic  38.7 us (7%)
  blocking collectives  33 us (6%)
  matrix products  27.5 us (5%)
  between operations  15.3 us (3%)
    all_gather x3, waiting for transfers between devices, gather(): return lax.all_gather(x, axes, axis=0, tiled=True)  78.3 us
    ppermute x6, waiting for transfers between devices, halve(): lax.ppermute(lax.dynamic_index_in_dim(v, 1 - me, 0, False), axis, [(0, 1)...  41.5 us
    reduce_scatter x4, waiting for transfers between devices, scatter_sum(): return lax.psum_scatter(x, axes, scatter_dimension=0, tiled=True)  40 us
    all_to_all x1, blocking collectives, exchange(): return lax.all_to_all(x, axes, 0, 0, tiled=True)  33 us
    all_to_all x3, waiting for transfers between devices, exchange(): return lax.all_to_all(x, axes, 0, 0, tiled=True)  32.9 us
    ppermute x3, waiting for transfers between devices, chain_gather(): up = lax.ppermute(up, axis, [(i, i + 1) for i in range(n - 1)])  30.1 us
    pallas_call x1, Pallas kernels, experts(): pl.pallas_call(experts_kernel, grid_spec=pltpu.PrefetchScalarGridSpec(num...  28.9 us
    pallas_call x1, Pallas kernels, expert_grads(): pl.pallas_call(expert_grads_kernel, grid=(count,), in_specs=[whole, whole...  26.6 us
  transfers between devices with their start and end apart: 22, of which 13 were waited for; matrix products, arithmetic and copies ran while one was open for 17% of the time, Pallas kernels for 16%

profile of v3, /device:TPU:0, one launch (start us, length us, event | category | flops | bytes accessed | tf_op | source)
XLA Modules:
  0.0 539.8 jit_solution(3521074138915907654)
XLA Ops:
  16.5 1.8 convert_reduce_fusion
  20.2 3.7 multiply_sine_fusion
  25.0 6.6 %concatenate.70.cos_ref = f32[2048,256]{1,0:T(8,128)} concatenate(f32[2048,32]{1,0:T(8,128)S(1)} %get-tuple-element.142, f32[2048,32]{1,0:T(8,128)S(1)} %get-tuple-element.142, f32[2048,32]{1,0:T(8,128)S(1)} %get-tuple-element.142, f32[2048,32]{1,0:T(8,128)S(1)} %get-tuple-element.142, f32[2048,32]{1,0:T(8,128)S(1)} %get-tuple-element.142, f32[2048,32]{1,0:T(8,128)S(1)} %get-tuple-element.142, ...), dimensions={1} | concatenate | bytes 4194304 | tf_op jit(solution)/shard_map/concatenate | solution.py:43
  33.6 6.7 %concatenate.71.sin_ref = f32[2048,256]{1,0:T(8,128)} concatenate(f32[2048,32]{1,0:T(8,128)S(1)} %get-tuple-element.141, f32[2048,32]{1,0:T(8,128)S(1)} %get-tuple-element.140, f32[2048,32]{1,0:T(8,128)S(1)} %get-tuple-element.141, f32[2048,32]{1,0:T(8,128)S(1)} %get-tuple-element.140, f32[2048,32]{1,0:T(8,128)S(1)} %get-tuple-element.141, f32[2048,32]{1,0:T(8,128)S(1)} %get-tuple-element.140, ...), dimensions={1} | concatenate | bytes 4194304 | tf_op jit(solution)/shard_map/concatenate | solution.py:44
  40.9 2.4 pad_maximum_fusion
  43.3 44.5 %all-gather.4.cloned.1.call-done.gain_ref.w_ref.router_ref = bf16[1024,3200]{1,0:T(8,128)(2,1)} async-done(((bf16[32,3200]{1,0:T(8,128)(2,1)}), bf16[1024,3200]{1,0:T(8,128)(2,1)}) %all-gather.4.cloned.1.call-update) | async-done | bytes 6553616 | tf_op jit(solution)/shard_map/all_gather | solution.py:77
  89.4 8.4 %project.1 = (bf16[8,256,256]{2,1,0:T(8,128)(2,1)}, bf16[256,1024]{1,0:T(8,128)(2,1)}) custom-call(bf16[256,1024]{1,0:T(8,128)(2,1)} %bitcast.143, bf16[1024,3200]{1,0:T(8,128)(2,1)} %all-gather.4.cloned.1.call-done.gain_ref.w_ref.router_ref, bf16[1024,3200]{1,0:T(8,128)(2,1)} %all-gather.4.cloned.1.call-done.gain_ref.w_ref.router_ref, ...), custom_call_target="tpu_custom_call" | custom-call | flops 1073741824 | bytes 6291456 | tf_op jit(solution)/shard_map/project/pallas_call | solution.py:149
  97.8 5.9 %all-to-all-start = ((bf16[8,256,256]{2,1,0:T(8,128)(2,1)}), bf16[8,256,256]{2,1,0:T(8,128)(2,1)S(1)}, u32[]{:S(2)}, u32[]{:S(2)}) async-start(bf16[8,256,256]{2,1,0:T(8,128)(2,1)} %get-tuple-element.48), calls=%async_computation | async-start | bytes 2097152 | tf_op jit(solution)/shard_map/all_to_all | solution.py:528
  103.7 4.0 collective-permute-start
  109.0 1.3 copy.97.doc_ref
  110.3 23.4 %collective-permute-done = bf16[256,1152]{1,0:T(8,128)(2,1)S(1)} collective-permute-done((bf16[256,1152]{1,0:T(8,128)(2,1)S(1)}, bf16[256,1152]{1,0:T(8,128)(2,1)S(1)}, u32[]{:S(2)}, u32[]{:S(2)}) %collective-permute-start) | collective-permute-done | bytes 589856 | tf_op jit(solution)/shard_map/ppermute | solution.py:93
  133.7 9.8 %collective-permute-start.4 = (bf16[256,1152]{1,0:T(8,128)(2,1)S(1)}, bf16[256,1152]{1,0:T(8,128)(2,1)}, u32[]{:S(2)}, u32[]{:S(2)}) collective-permute-start(bf16[256,1152]{1,0:T(8,128)(2,1)S(1)} %collective-permute-done), channel_id=1, source_target_pairs={{0,8},{8,16},{16,24},{1,9},{9,17},{17,25},{2,10},{10,18},{18,26},{... | collective-permute-start | bytes 1769480 | tf_op jit(solution)/shard_map/ppermute | solution.py:93
  144.8 1.4 convert_reduce_fusion.2
  146.2 1.5 broadcast_in_dim.70
  148.6 6.8 %collective-permute-done.4 = bf16[256,1152]{1,0:T(8,128)(2,1)} collective-permute-done((bf16[256,1152]{1,0:T(8,128)(2,1)S(1)}, bf16[256,1152]{1,0:T(8,128)(2,1)}, u32[]{:S(2)}, u32[]{:S(2)}) %collective-permute-start.4) | collective-permute-done | bytes 589856 | tf_op jit(solution)/shard_map/ppermute | solution.py:93
  155.4 5.5 %collective-permute-start.5 = (bf16[256,1152]{1,0:T(8,128)(2,1)}, bf16[256,1152]{1,0:T(8,128)(2,1)}, u32[]{:S(2)}, u32[]{:S(2)}) collective-permute-start(bf16[256,1152]{1,0:T(8,128)(2,1)} %collective-permute-done.4), channel_id=1, source_target_pairs={{0,8},{8,16},{16,24},{1,9},{9,17},{17,25},{2,10},{10,18},{18,26},{... | collective-permute-start | bytes 1769480 | tf_op jit(solution)/shard_map/ppermute | solution.py:93
  162.8 21.4 %attend.1 = (f32[2048,128]{1,0:T(8,128)}, bf16[2048,128]{1,0:T(8,128)(2,1)}, f32[8,512,1]{2,1,0:T(8,128)}) custom-call(s32[9]{0:T(128)} %pad_add_fusion.bounds_ref, bf16[2048,256]{1,0:T(8,128)(2,1)} %bitcast.159, bf16[2048,256]{1,0:T(8,128)(2,1)} %bitcast.160, s32[2048,1]{1,0:T(8,128)} %copy.97.doc_ref), custom_call_target="tpu_custom_call" | custom-call | flops 2147483648 | bytes 6291456 | tf_op jit(solution)/shard_map/attend/pallas_call | solution.py:247
  184.3 2.1 copy.92
  186.4 4.3 all-to-all-start.1
  192.7 11.7 %all-to-all-done.1 = bf16[8,256,128]{1,2,0:T(8,128)(2,1)S(1)} async-done(((bf16[8,256,128]{1,2,0:T(8,128)(2,1)}), bf16[8,256,128]{1,2,0:T(8,128)(2,1)S(1)}, u32[]{:S(2)}, u32[]{:S(2)}) %all-to-all-start.1) | async-done | bytes 524320 | tf_op jit(solution)/shard_map/all_to_all | solution.py:528
  204.4 2.5 multiply_reduce_fusion.2
  208.1 10.6 %fusion.5.z_ref = f32[4,1024,512]{2,1,0:T(8,128)} fusion(bf16[4,1024,1536]{2,1,0:T(8,128)(2,1)} %bitcast.176, bf16[1024,1152]{1,0:T(8,128)(2,1)} %bitcast.18.routed_ref.ct_ref), kind=kOutput, calls=%fused_computation.14 | convolution fusion | flops 4294967296 | bytes 14680064 | tf_op jit(solution)/shard_map/td,edf->etf/dot_general | solution.py:651
  218.7 33.8 %all-gather.8.cloned.1.call-done.n_ref = bf16[1024,1024]{1,0:T(8,128)(2,1)} async-done(((bf16[256,1024]{1,0:T(8,128)(2,1)}), bf16[1024,1024]{1,0:T(8,128)(2,1)}) %all-gather.8.cloned.1.call-update) | async-done | bytes 2097168 | tf_op jit(solution)/shard_map/all_gather | solution.py:77
  252.5 28.9 %experts.1 = (bf16[1024,1152]{1,0:T(8,128)(2,1)}, f32[1024,128]{1,0:T(8,128)}, bf16[4,1024,512]{2,1,0:T(8,128)(2,1)}, bf16[4,1024,1024]{2,1,0:T(8,128)(2,1)}) custom-call(s32[1]{0:T(128)} %bitcast.11.group_ref, bf16[1024,1024]{1,0:T(8,128)(2,1)} %all-gather.8.cloned.1.call-done.n_ref, bf16[1024,1152]{1,0:T(8,128)(2,1)} %bitcast.18.routed_ref.ct_ref, ...), custom_call_target="tpu_custom_call" | custom-call | flops 17179869184 | bytes 41943040 | tf_op jit(solution)/shard_map/experts/pallas_call | solution.py:439
  281.8 26.6 %expert_grads.1 = (bf16[1024,1024]{1,0:T(8,128)(2,1)}, bf16[4,1024,1536]{2,1,0:T(8,128)(2,1)}) custom-call(bf16[1024,1024]{1,0:T(8,128)(2,1)} %all-gather.8.cloned.1.call-done.n_ref, bf16[1024,1152]{1,0:T(8,128)(2,1)} %bitcast.18.routed_ref.ct_ref, bf16[4,1024,1536]{2,1,0:T(8,128)(2,1)} %bitcast.178, bf16[4,1024,512]{2,1,0:T(8,128)(2,1)} %get-tuple-element.57.hidden_ref, ...), custom_call_target="tpu_custom_call" | custom-call | flops 17179869184 | bytes 41943040 | tf_op jit(solution)/shard_map/expert_grads/pallas_call | solution.py:499
  308.3 20.1 %reduce-scatter.5.cloned.1.call-done = bf16[256,1152]{1,0:T(8,128)(2,1)} async-done(((bf16[1024,1152]{1,0:T(8,128)(2,1)}), bf16[256,1152]{1,0:T(8,128)(2,1)}) %reduce-scatter.5.cloned.1.call-update) | async-done | bytes 589840 | tf_op jit(solution)/shard_map/reduce_scatter | solution.py:81
  332.4 1.8 multiply_reduce_fusion
  334.6 3.0 fusion.33
  337.7 33.0 %all_to_all.20 = bf16[8,256,128]{2,1,0:T(8,128)(2,1)} all-to-all(bf16[8,256,128]{2,1,0:T(8,128)(2,1)S(1)} %bitcast.154), channel_id=1, replica_groups=mesh['a'=4,'b'=2,'y'=2,'c'=2] {'a','b'}, dimensions={0} | all-to-all | bytes 1048576 | tf_op jit(solution)/shard_map/all_to_all | solution.py:528
  370.7 26.0 %attend_back.1 = (f32[2048,128]{1,0:T(8,128)}, f32[2048,128]{1,0:T(8,128)}) custom-call(s32[9]{0:T(128)} %pad_add_fusion.bounds_ref, bf16[2048,256]{1,0:T(8,128)(2,1)} %bitcast.161, bf16[2048,256]{1,0:T(8,128)(2,1)} %bitcast.162, s32[2048,1]{1,0:T(8,128)} %copy.97.doc_ref, bf16[2048,128]{1,0:T(8,128)(2,1)} %bitcast.165, ...), custom_call_target="tpu_custom_call" | custom-call | flops 5368709120 | bytes 8388608 | tf_op jit(solution)/shard_map/attend_back/pallas_call | solution.py:328
  396.7 6.1 %unrotate.1 = bf16[2048,256]{1,0:T(8,128)(2,1)} custom-call(f32[2048,128]{1,0:T(8,128)} %get-tuple-element.65.dq_ref, f32[2048,128]{1,0:T(8,128)} %get-tuple-element.66.dkv_ref, f32[2048,256]{1,0:T(8,128)} %concatenate.70.cos_ref, f32[2048,256]{1,0:T(8,128)} %concatenate.71.sin_ref), custom_call_target="tpu_custom_call" | custom-call | flops 4194304 | bytes 7340032 | tf_op jit(solution)/shard_map/unrotate/pallas_call | solution.py:369
  402.8 2.4 copy.98
  405.2 4.3 all-to-all-start.3
  412.1 21.2 %all-to-all-done.3 = bf16[8,256,256]{1,2,0:T(8,128)(2,1)} async-done(((bf16[8,256,256]{1,2,0:T(8,128)(2,1)}), bf16[8,256,256]{1,2,0:T(8,128)(2,1)}, u32[]{:S(2)}, u32[]{:S(2)}) %all-to-all-start.3) | async-done | bytes 1048608 | tf_op jit(solution)/shard_map/all_to_all | solution.py:528
  433.2 1.4 convolution_convert_fusion.2
  436.3 3.3 convolution_convert_fusion
  440.7 3.8 fusion.43
  444.8 1.3 fusion.16
  446.1 2.2 fusion.8
  450.0 1.9 fusion.4
  453.1 1.4 collective-permute-start.7
  454.6 22.2 %collective-permute-done.10 = bf16[256,1536]{1,0:T(8,128)(2,1)} collective-permute-done((bf16[256,1536]{1,0:T(8,128)(2,1)}, bf16[256,1536]{1,0:T(8,128)(2,1)}, u32[]{:S(2)}, u32[]{:S(2)}) %collective-permute-start.10) | collective-permute-done | bytes 786464 | tf_op jit(solution)/shard_map/ppermute | solution.py:110
  476.8 1.6 fusion.24
  478.4 1.4 collective-permute-start.11
  480.3 18.1 %collective-permute-done.11 = bf16[128,1536]{1,0:T(8,128)(2,1)S(1)} collective-permute-done((bf16[128,1536]{1,0:T(8,128)(2,1)S(1)}, bf16[128,1536]{1,0:T(8,128)(2,1)S(1)}, u32[]{:S(2)}, u32[]{:S(2)}) %collective-permute-start.11) | collective-permute-done | bytes 393248 | tf_op jit(solution)/shard_map/ppermute | solution.py:110
  501.5 2.9 slice.116
  505.5 1.6 fusion.42
  507.1 19.2 %reduce-scatter.11.cloned.1.call-done = bf16[32,3200]{1,0:T(8,128)(2,1)} async-done(((bf16[128,3200]{1,0:T(8,128)(2,1)}), bf16[32,3200]{1,0:T(8,128)(2,1)}) %reduce-scatter.11.cloned.1.call-update) | async-done | bytes 204816 | tf_op jit(solution)/shard_map/reduce_scatter | solution.py:81
  (183 shorter events, 48.8 us)
Async XLA Ops:
  7.2 7.3 %copy-start.21 = (f32[512,512]{1,0:T(8,128)S(1)}, f32[512,512]{1,0:T(8,128)}, u32[]{:S(2)}) copy-start(f32[512,512]{1,0:T(8,128)} %param.25) | copy-start | bytes 3145732
  7.2 8.2 %copy-start.16 = (f32[512,1024]{1,0:T(8,128)S(1)}, f32[512,1024]{1,0:T(8,128)}, u32[]{:S(2)}) copy-start(f32[512,1024]{1,0:T(8,128)} %param.24) | copy-start | bytes 6291460
  7.2 80.6 %all-gather.4.cloned.1.call-start = ((), (), s32[]{:S(2)}) async-start(), calls=%async_computation.8 | async-start | bytes 6758400 | tf_op jit(solution)/shard_map/all_gather | solution.py:77
  14.4 193.6 %all-gather.6.cloned.1.call-start = ((), (), s32[]{:S(2)}) async-start(), calls=%async_computation.9 | async-start | bytes 14155776 | tf_op jit(solution)/shard_map/all_gather | solution.py:77
  14.5 2.0 copy-start.26
  33.6 7.4 %copy-start.14 = (bf16[512,1024]{1,0:T(8,128)(2,1)S(1)}, bf16[512,1024]{1,0:T(8,128)(2,1)}, u32[]{:S(2)}) copy-start(bf16[512,1024]{1,0:T(8,128)(2,1)} %convert_element_type.195) | copy-start | bytes 3145732
  40.9 46.9 %copy-start.27 = (s32[1,256,8]{1,2,0:T(8,128)S(1)}, s32[1,256,8]{1,2,0:T(8,128)}, u32[]{:S(2)}) copy-start(s32[1,256,8]{1,2,0:T(8,128)} %param.16) | copy-start | bytes 24580
  40.9 47.1 %copy-start.17 = (bf16[1,256,1024]{2,1,0:T(8,128)(2,1)S(1)}, bf16[1,256,1024]{2,1,0:T(8,128)(2,1)}, u32[]{:S(2)}) copy-start(bf16[1,256,1024]{2,1,0:T(8,128)(2,1)} %param.14) | copy-start | bytes 1572868
  88.1 19.5 %collective-permute-start.1 = (bf16[256,1152]{1,0:T(8,128)(2,1)S(1)}, bf16[256,1152]{1,0:T(8,128)(2,1)S(1)}, u32[]{:S(2)}, u32[]{:S(2)}) collective-permute-start(bf16[256,1152]{1,0:T(8,128)(2,1)S(1)} %pad_maximum_fusion.2), channel_id=1, source_target_pairs={{8,0},{16,8},{24,16},{9,1},{17,9},{25,17},{10,2},{18,10},{26,18},{... | collective-permute-start | bytes 1769480 | tf_op jit(solution)/shard_map/ppermute | solution.py:94
  97.8 64.1 %all-to-all-start = ((bf16[8,256,256]{2,1,0:T(8,128)(2,1)}), bf16[8,256,256]{2,1,0:T(8,128)(2,1)S(1)}, u32[]{:S(2)}, u32[]{:S(2)}) async-start(bf16[8,256,256]{2,1,0:T(8,128)(2,1)} %get-tuple-element.48), calls=%async_computation | async-start | bytes 2097152 | tf_op jit(solution)/shard_map/all_to_all | solution.py:528
  103.7 30.1 %collective-permute-start = (bf16[256,1152]{1,0:T(8,128)(2,1)S(1)}, bf16[256,1152]{1,0:T(8,128)(2,1)S(1)}, u32[]{:S(2)}, u32[]{:S(2)}) collective-permute-start(bf16[256,1152]{1,0:T(8,128)(2,1)S(1)} %pad_maximum_fusion.2), channel_id=1, source_target_pairs={{0,8},{8,16},{16,24},{1,9},{9,17},{17,25},{2,10},{10,18},{18,26},{... | collective-permute-start | bytes 1769480 | tf_op jit(solution)/shard_map/ppermute | solution.py:93
  107.6 35.8 %collective-permute-start.2 = (bf16[256,1152]{1,0:T(8,128)(2,1)S(1)}, bf16[256,1152]{1,0:T(8,128)(2,1)S(1)}, u32[]{:S(2)}, u32[]{:S(2)}) collective-permute-start(bf16[256,1152]{1,0:T(8,128)(2,1)S(1)} %collective-permute-done.1), channel_id=1, source_target_pairs={{8,0},{16,8},{24,16},{9,1},{17,9},{25,17},{10,2},{18,10},{26,18},{... | collective-permute-start | bytes 1769480 | tf_op jit(solution)/shard_map/ppermute | solution.py:94
  133.7 21.7 %collective-permute-start.4 = (bf16[256,1152]{1,0:T(8,128)(2,1)S(1)}, bf16[256,1152]{1,0:T(8,128)(2,1)}, u32[]{:S(2)}, u32[]{:S(2)}) collective-permute-start(bf16[256,1152]{1,0:T(8,128)(2,1)S(1)} %collective-permute-done), channel_id=1, source_target_pairs={{0,8},{8,16},{16,24},{1,9},{9,17},{17,25},{2,10},{10,18},{18,26},{... | collective-permute-start | bytes 1769480 | tf_op jit(solution)/shard_map/ppermute | solution.py:93
  143.5 18.4 %copy-start.23 = (bf16[256,1152]{1,0:T(8,128)(2,1)}, bf16[256,1152]{1,0:T(8,128)(2,1)S(1)}, u32[]{:S(2)}) copy-start(bf16[256,1152]{1,0:T(8,128)(2,1)S(1)} %collective-permute-done.2) | copy-start | bytes 1769476
  143.5 17.4 %collective-permute-start.3 = (bf16[256,1152]{1,0:T(8,128)(2,1)S(1)}, bf16[256,1152]{1,0:T(8,128)(2,1)S(1)}, u32[]{:S(2)}, u32[]{:S(2)}) collective-permute-start(bf16[256,1152]{1,0:T(8,128)(2,1)S(1)} %collective-permute-done.2), channel_id=1, source_target_pairs={{8,0},{16,8},{24,16},{9,1},{17,9},{25,17},{10,2},{18,10},{26,18},{... | collective-permute-start | bytes 1769480 | tf_op jit(solution)/shard_map/ppermute | solution.py:94
  155.4 36.3 %collective-permute-start.5 = (bf16[256,1152]{1,0:T(8,128)(2,1)}, bf16[256,1152]{1,0:T(8,128)(2,1)}, u32[]{:S(2)}, u32[]{:S(2)}) collective-permute-start(bf16[256,1152]{1,0:T(8,128)(2,1)} %collective-permute-done.4), channel_id=1, source_target_pairs={{0,8},{8,16},{16,24},{1,9},{9,17},{17,25},{2,10},{10,18},{18,26},{... | collective-permute-start | bytes 1769480 | tf_op jit(solution)/shard_map/ppermute | solution.py:93
  184.3 6.5 %copy-start.24 = (bf16[256,1152]{1,0:T(8,128)(2,1)S(1)}, bf16[256,1152]{1,0:T(8,128)(2,1)}, u32[]{:S(2)}) copy-start(bf16[256,1152]{1,0:T(8,128)(2,1)} %copy-done.23) | copy-start | bytes 1769476
  186.4 18.1 %copy-start.10 = (bf16[1,256,1024]{2,1,0:T(8,128)(2,1)S(1)}, bf16[1,256,1024]{2,1,0:T(8,128)(2,1)}, u32[]{:S(2)}) copy-start(bf16[1,256,1024]{2,1,0:T(8,128)(2,1)} %param.13) | copy-start | bytes 1572868
  186.4 18.1 %all-to-all-start.1 = ((bf16[8,256,128]{1,2,0:T(8,128)(2,1)}), bf16[8,256,128]{1,2,0:T(8,128)(2,1)S(1)}, u32[]{:S(2)}, u32[]{:S(2)}) async-start(bf16[8,256,128]{1,2,0:T(8,128)(2,1)} %copy.92), calls=%async_computation.1 | async-start | bytes 1048576 | tf_op jit(solution)/shard_map/all_to_all | solution.py:528
  190.7 61.9 %all-gather.8.cloned.1.call-start = ((), (), s32[]{:S(2)}) async-start(), calls=%async_computation.10 | async-start | bytes 2621440 | tf_op jit(solution)/shard_map/all_gather | solution.py:77
  206.9 127.4 %copy-start.1 = (f32[256,1024]{1,0:T(8,128)}, f32[256,1024]{1,0:T(8,128)S(1)}, u32[]{:S(2)}) copy-start(f32[256,1024]{1,0:T(8,128)S(1)} %get-tuple-element.71) | copy-start | bytes 3145732
  208.1 120.4 %reduce-scatter.5.cloned.1.call-start = ((), (), s32[]{:S(2)}) async-start(), calls=%async_computation.11 | async-start | bytes 2949120 | tf_op jit(solution)/shard_map/reduce_scatter | solution.py:81
  281.5 219.2 %reduce-scatter.9.cloned.1.call-start = ((), (), s32[]{:S(2)}) async-start(), calls=%async_computation.13 | async-start | bytes 2621440 | tf_op jit(solution)/shard_map/reduce_scatter | solution.py:81
  329.6 171.8 %reduce-scatter.7.cloned.1.call-start = ((), (), s32[]{:S(2)}) async-start(), calls=%async_computation.12 | async-start | bytes 14155776 | tf_op jit(solution)/shard_map/reduce_scatter | solution.py:81
  330.2 4.1 copy-start.18
  334.6 75.4 %copy-start.3 = (f32[256,1024]{1,0:T(8,128)}, f32[256,1024]{1,0:T(8,128)S(1)}, u32[]{:S(2)}) copy-start(f32[256,1024]{1,0:T(8,128)S(1)} %subtract_add_fusion) | copy-start | bytes 3145732
  405.2 28.1 %all-to-all-start.3 = ((bf16[8,256,256]{1,2,0:T(8,128)(2,1)}), bf16[8,256,256]{1,2,0:T(8,128)(2,1)}, u32[]{:S(2)}, u32[]{:S(2)}) async-start(bf16[8,256,256]{1,2,0:T(8,128)(2,1)} %copy.98), calls=%async_computation.4 | async-start | bytes 2097152 | tf_op jit(solution)/shard_map/all_to_all | solution.py:528
  409.4 116.9 %reduce-scatter.11.cloned.1.call-start = ((), (), s32[]{:S(2)}) async-start(), calls=%async_computation.14 | async-start | bytes 1024000 | tf_op jit(solution)/shard_map/reduce_scatter | solution.py:81
  410.7 22.6 %copy-start.15 = (bf16[256,1024]{1,0:T(8,128)(2,1)S(1)}, bf16[256,1024]{1,0:T(8,128)(2,1)}, u32[]{:S(2)}) copy-start(bf16[256,1024]{1,0:T(8,128)(2,1)} %get-tuple-element.46) | copy-start | bytes 1572868
  410.9 25.2 %copy-start = (bf16[4,2,2,2,32,1024]{5,4,0,2,1,3:T(8,128)(2,1)}, bf16[4,2,2,2,32,1024]{5,4,0,2,1,3:T(8,128)(2,1)S(1)}, u32[]{:S(2)}) copy-start(bf16[4,2,2,2,32,1024]{5,4,0,2,1,3:T(8,128)(2,1)S(1)} %copy.103) | copy-start | bytes 6291460
  434.8 1.5 copy-start.5
  434.8 5.0 slice-start
  436.3 3.6 slice-start.1
  436.3 9.8 %collective-permute-start.9 = (bf16[512,1536]{1,0:T(8,128)(2,1)}, bf16[512,1536]{1,0:T(8,128)(2,1)}, u32[]{:S(2)}, u32[]{:S(2)}) collective-permute-start(bf16[512,1536]{1,0:T(8,128)(2,1)} %fusion.21), channel_id=1, source_target_pairs={{0,1},{1,0},{2,3},{3,2},{4,5},{5,4},{6,7},{7,6},{8,9},{9,8},{10,11... | collective-permute-start | bytes 4718600 | tf_op jit(solution)/shard_map/ppermute | solution.py:110
  446.1 3.9 collective-permute-start.6
  448.3 1.6 copy-start.8
  449.3 27.5 %collective-permute-start.10 = (bf16[256,1536]{1,0:T(8,128)(2,1)}, bf16[256,1536]{1,0:T(8,128)(2,1)}, u32[]{:S(2)}, u32[]{:S(2)}) collective-permute-start(bf16[256,1536]{1,0:T(8,128)(2,1)} %dynamic-slice_bitcast_fusion.1), channel_id=1, source_target_pairs={{0,4},{4,0},{1,5},{5,1},{2,6},{6,2},{3,7},{7,3},{8,12},{12,8},{9,1... | collective-permute-start | bytes 2359304 | tf_op jit(solution)/shard_map/ppermute | solution.py:110
  453.1 26.7 %copy-start.7 = (bf16[512,1664]{1,0:T(8,128)(2,1)S(1)}, bf16[512,1664]{1,0:T(8,128)(2,1)}, u32[]{:S(2)}) copy-start(bf16[512,1664]{1,0:T(8,128)(2,1)} %copy-done.6) | copy-start | bytes 5111812
  453.1 26.7 %collective-permute-start.7 = (bf16[256,1664]{1,0:T(8,128)(2,1)S(1)}, bf16[256,1664]{1,0:T(8,128)(2,1)S(1)}, u32[]{:S(2)}, u32[]{:S(2)}) collective-permute-start(bf16[256,1664]{1,0:T(8,128)(2,1)S(1)} %dynamic-slice_bitcast_fusion), channel_id=1, source_target_pairs={{0,2},{2,0},{1,3},{3,1},{4,6},{6,4},{5,7},{7,5},{8,10},{10,8},{9,1... | collective-permute-start | bytes 2555912 | tf_op jit(solution)/shard_map/ppermute | solution.py:110
  478.4 20.0 %collective-permute-start.11 = (bf16[128,1536]{1,0:T(8,128)(2,1)S(1)}, bf16[128,1536]{1,0:T(8,128)(2,1)S(1)}, u32[]{:S(2)}, u32[]{:S(2)}) collective-permute-start(bf16[128,1536]{1,0:T(8,128)(2,1)S(1)} %dynamic-slice_bitcast_fusion.3), channel_id=1, source_target_pairs={{0,2},{2,0},{1,3},{3,1},{4,6},{6,4},{5,7},{7,5},{8,10},{10,8},{9,1... | collective-permute-start | bytes 1179656 | tf_op jit(solution)/shard_map/ppermute | solution.py:110
  480.1 19.5 %collective-permute-start.8 = (bf16[128,1664]{1,0:T(8,128)(2,1)S(1)}, bf16[128,1664]{1,0:T(8,128)(2,1)S(1)}, u32[]{:S(2)}, u32[]{:S(2)}) collective-permute-start(bf16[128,1664]{1,0:T(8,128)(2,1)S(1)} %dynamic-slice_bitcast_fusion.2), channel_id=1, source_target_pairs={{0,4},{4,0},{1,5},{5,1},{2,6},{6,2},{3,7},{7,3},{8,12},{12,8},{9,1... | collective-permute-start | bytes 1277960 | tf_op jit(solution)/shard_map/ppermute | solution.py:110
  501.4 3.0 copy-start.9
  501.4 4.1 copy-start.2
  501.4 4.1 copy-start.4
  501.4 4.1 copy-start.12
  501.4 4.1 copy-start.20
  501.4 4.1 copy-start.25
  526.3 2.0 copy-start.19
  (4 other events, 4.2 us)
Sparse Core Ops, SparseCore 0:
  14.5 73.2 all-gather.3
  89.7 81.4 all-gather.5
  208.2 44.3 all-gather.7
  281.6 46.7 reduce-scatter.4
  330.6 51.5 reduce-scatter.8
  386.0 115.3 reduce-scatter.6
  503.8 22.5 reduce-scatter.10
